TPU v7x, 32 devices: a whole 2x2x4 slice. The times are simulated.
32 devices in a mesh: dom: 16 (over z, y, core), dest: 2 (over x).
Axes of the slice: x: 2, y: 2, z: 4, core: 2. Of those that a mesh axis runs over, the one named last changes fastest.
Arguments:
- features: bfloat16 [65536, 128], P('dom')
- w_input: bfloat16 [128, 512], replicated, may hold values from -0.5 to 0.5
- b_input: float32 [512], replicated, may hold values from -3 to 3
- w_output: float32 [512], replicated, may hold values from -0.25 to 0.25
- terminal: float32 [32, 65536], P('dest', 'dom'), may hold values from -4 to 4
- start_counts: int32 [32, 65536], P('dest', 'dom'), may hold values from 0 to 3
- visit_counts: int32 [32, 65536], P('dest', 'dom'), may hold values from 0 to 3
- dest_nodes: int32 [32], P('dest'), may hold values from 0 to 65535
- tile_rows: int32 [1280], P('dom'), may hold values from 0 to 31, as said below
- tile_cols: int32 [1280], P('dom'), may hold values from 0 to 47, as said below
- send_blocks: int32 [128, 2], P('dom'), may hold values from 0 to 31
- tile_weight: bfloat16 [1280, 128, 128], P('dom'), as said below
Outputs:
- values: float32 [32, 65536], P('dest', 'dom')
- grad_w_input: float32 [128, 512], replicated
- grad_b_input: float32 [512], replicated
- grad_w_output: float32 [512], replicated
Inputs may be any that keep to these rules, and one draw needn't show every extreme that they name: `tile_rows`: the first 32 tiles of every partition are its diagonal tiles, in order. `tile_cols`: the first 32 tiles of a partition have columns 0 .. 31 in order. A column of 32 or more names a slot of a neighbour q = p - f that exists; every slot of every existing neighbour is named by exactly one tile. `tile_weight`: every entry is zero or positive; every row of a diagonal tile has a positive entry.
All inputs are finite; a program needn't handle non-finite values.
Results may differ from a plain program's by a relative error of at most 0.0003.
Values sent between devices are 32-bit elements; how exact they have to be, the bound alone decides.
No kernel may reach another device: no remote copies, remote signals or barrier semaphores. Data moves between devices by JAX's collectives and lax.ppermute only.
A program may use at most 64 MiB of HBM per device.

v0:
```python
import functools
import math

import jax
import jax.numpy as jnp
from jax import lax
from jax.experimental import pallas as pl
from jax.experimental.pallas import tpu as pltpu
from jax.sharding import PartitionSpec as P

STEPS = 3
GOAL_GAIN = 32.0
VMEM_GRANT = 24 << 20

NT = (((1,), (1,)), ((), ()))
NN = (((1,), (0,)), ((), ()))


def offset_of(o, reach):
    return o - reach if o < reach else o - reach + 1


def neighbour(me, count, shift):
    there = me + shift
    present = jnp.logical_and(there >= 0, there < count)
    return present, jnp.where(present, there, me)


def call(kernel, out_shape, scratch, ins, smem, flops, moved):
    return pl.pallas_call(
        kernel,
        out_shape=out_shape,
        in_specs=[pl.BlockSpec(memory_space=pltpu.SMEM)] * smem
        + [pl.BlockSpec(memory_space=pltpu.VMEM)] * (len(ins) - smem),
        out_specs=jax.tree.map(lambda _: pl.BlockSpec(memory_space=pltpu.VMEM), out_shape),
        scratch_shapes=scratch,
        compiler_params=pltpu.CompilerParams(vmem_limit_bytes=VMEM_GRANT),
        cost_estimate=pl.CostEstimate(flops=flops, bytes_accessed=moved, transcendentals=0),
    )(*ins)


def store_split(ref, k, x):
    rows = x.shape[0]
    high = x.astype(jnp.bfloat16)
    low = (x - high.astype(jnp.float32)).astype(jnp.bfloat16)
    ref[k, :rows] = high
    ref[k, rows:] = low


def product(lhs, rhs, dims):
    both = lax.dot_general(lhs, rhs, dims, preferred_element_type=jnp.float32)
    rows = both.shape[0] // 2
    return both[:rows] + both[rows:]


def pack(out_ref, me, count, reach, width, sign, block):
    rows = None
    for o in range(2 * reach):
        _, there = neighbour(me, count, sign * offset_of(o, reach))
        for m in range(width):
            piece = block(o, m)
            rows = piece.shape[0]
            out_ref[there, m * rows : (m + 1) * rows] = piece


def network_kernel(w_ref, b_ref, v_ref, f_ref, act_ref, growth_ref):
    chunk = 512
    w = w_ref[...]
    b = b_ref[...]
    v = v_ref[...]
    for c in range(f_ref.shape[0] // chunk):
        pre = lax.dot_general(
            w, f_ref[c * chunk : (c + 1) * chunk], NT, preferred_element_type=jnp.float32
        )
        act = jnp.tanh(pre + b)
        act_ref[:, c * chunk : (c + 1) * chunk] = act
        grown = jnp.exp(jnp.sum(act * v, axis=0, keepdims=True))
        for k in range(chunk // 128):
            growth_ref[c * (chunk // 128) + k] = grown[:, k * 128 : (k + 1) * 128]


def first_kernel(count, reach, width, send_ref, term_ref, z_ref, out_ref):
    blocks = z_ref.shape[0]
    lanes = z_ref.shape[2]
    me = lax.axis_index("dom")
    for k in range(blocks):
        z_ref[k] = jnp.exp(term_ref[:, k * lanes : (k + 1) * lanes])
    pack(out_ref, me, count, reach, width, 1, lambda o, m: z_ref[send_ref[o, m]])


def gather_split(count, reach, width, z_ref, got_ref, split_ref):
    blocks, rows, _ = z_ref.shape
    me = lax.axis_index("dom")
    for k in range(blocks):
        store_split(split_ref, k, z_ref[k])
    for o in range(2 * reach):
        _, there = neighbour(me, count, -offset_of(o, reach))
        for m in range(width):
            store_split(
                split_ref, blocks + o * width + m, got_ref[there, m * rows : (m + 1) * rows]
            )


def backed_up(rows_ref, cols_ref, w_ref, split_ref, sum_ref, blocks):
    for k in range(blocks):
        sum_ref[k] = product(split_ref[k], w_ref[k], NT)
    for t in range(blocks, w_ref.shape[0]):
        r = rows_ref[t]
        sum_ref[r] = sum_ref[r] + product(split_ref[cols_ref[t]], w_ref[t], NT)


def with_goal(k, growth_ref, sum_ref, dest, me):
    blocks, rows, lanes = sum_ref.shape
    node = (me * blocks + k) * lanes + lax.broadcasted_iota(jnp.int32, (rows, lanes), 1)
    return growth_ref[k] * sum_ref[k] + jnp.where(node == dest, GOAL_GAIN, 0.0)


def backup_kernel(
    count, reach, width, rows_ref, cols_ref, send_ref, w_ref, z_ref, got_ref, growth_ref, dest_ref,
    next_ref, out_ref, split_ref, sum_ref,
):
    blocks = z_ref.shape[0]
    me = lax.axis_index("dom")
    gather_split(count, reach, width, z_ref, got_ref, split_ref)
    backed_up(rows_ref, cols_ref, w_ref, split_ref, sum_ref, blocks)
    dest = jnp.broadcast_to(dest_ref[...], sum_ref.shape[1:])
    for k in range(blocks):
        next_ref[k] = with_goal(k, growth_ref, sum_ref, dest, me)
    pack(out_ref, me, count, reach, width, 1, lambda o, m: next_ref[send_ref[o, m]])


def spread_out(rows_ref, cols_ref, w_ref, split_ref, ext_ref, blocks):
    slots = ext_ref.shape[0] - blocks
    for k in range(slots):
        ext_ref[blocks + k] = jnp.zeros(ext_ref.shape[1:], jnp.float32)
    for k in range(blocks):
        ext_ref[k] = product(split_ref[k], w_ref[k], NN)
    for t in range(blocks, w_ref.shape[0]):
        c = cols_ref[t]
        ext_ref[c] = ext_ref[c] + product(split_ref[rows_ref[t]], w_ref[t], NN)


def turn_kernel(
    count, reach, width, rows_ref, cols_ref, w_ref, z_ref, got_ref, growth_ref, dest_ref, start_ref,
    values_ref, local_ref, out_ref, split_ref, sum_ref, ext_ref,
):
    blocks, rows, lanes = z_ref.shape
    me = lax.axis_index("dom")
    gather_split(count, reach, width, z_ref, got_ref, split_ref)
    backed_up(rows_ref, cols_ref, w_ref, split_ref, sum_ref, blocks)
    dest = jnp.broadcast_to(dest_ref[...], (rows, lanes))
    for k in range(blocks):
        z = with_goal(k, growth_ref, sum_ref, dest, me)
        span = slice(k * lanes, (k + 1) * lanes)
        values_ref[:, span] = jnp.log(z)
        store_split(split_ref, k, growth_ref[k] * start_ref[:, span].astype(jnp.float32) / z)
    spread_out(rows_ref, cols_ref, w_ref, split_ref, ext_ref, blocks)
    for k in range(blocks):
        local_ref[k] = ext_ref[k]
    pack(out_ref, me, count, reach, width, -1, lambda o, m: ext_ref[blocks + o * width + m])


def take_returned(count, reach, width, send_ref, got_ref, into_ref):
    rows = into_ref.shape[1]
    me = lax.axis_index("dom")
    for o in range(2 * reach):
        present, there = neighbour(me, count, offset_of(o, reach))
        for m in range(width):
            piece = got_ref[there, m * rows : (m + 1) * rows]
            b = send_ref[o, m]
            into_ref[b] = into_ref[b] + jnp.where(present, piece, 0.0)


def spread_kernel(
    count, reach, width, rows_ref, cols_ref, send_ref, w_ref, flow_ref, got_ref, growth_ref,
    full_ref, local_ref, out_ref, split_ref, ext_ref,
):
    blocks = flow_ref.shape[0]
    me = lax.axis_index("dom")
    full_ref[...] = flow_ref[...]
    take_returned(count, reach, width, send_ref, got_ref, full_ref)
    for k in range(blocks):
        store_split(split_ref, k, growth_ref[k] * full_ref[k])
    spread_out(rows_ref, cols_ref, w_ref, split_ref, ext_ref, blocks)
    for k in range(blocks):
        local_ref[k] = ext_ref[k]
    pack(out_ref, me, count, reach, width, -1, lambda o, m: ext_ref[blocks + o * width + m])


def last_kernel(
    count, reach, width, rows_ref, cols_ref, send_ref, w_ref, flow_ref, got_ref, growth_ref,
    z0_ref, z1_ref, z2_ref, first_ref, visit_ref, far_ref,
    node_ref, out_ref, split_ref, ext_ref, full_ref,
):
    blocks, rows, lanes = flow_ref.shape
    me = lax.axis_index("dom")
    full_ref[...] = flow_ref[...]
    take_returned(count, reach, width, send_ref, got_ref, full_ref)
    for k in range(blocks):
        store_split(split_ref, k, growth_ref[k] * full_ref[k])
    spread_out(rows_ref, cols_ref, w_ref, split_ref, ext_ref, blocks)
    for k in range(blocks):
        left = (
            visit_ref[:, k * lanes : (k + 1) * lanes].astype(jnp.float32)
            - z2_ref[k] * first_ref[k]
            - z1_ref[k] * full_ref[k]
            - z0_ref[k] * ext_ref[k]
        )
        node_ref[k] = jnp.sum(left, axis=0, keepdims=True)

    for o in range(2 * reach):
        _, back = neighbour(me, count, -offset_of(o, reach))
        pieces = [
            jnp.sum(
                far_ref[back, m * rows : (m + 1) * rows] * ext_ref[blocks + o * width + m],
                axis=0,
                keepdims=True,
            )
            for m in range(width)
        ]
        out_ref[back] = jnp.concatenate(
            pieces + [jnp.zeros((8 - width, lanes), jnp.float32)], axis=0
        )


def gradient_kernel(
    count, reach, width, scale, send_ref, v_ref, f_ref, act_ref, node_ref, got_ref,
    grad_ref, side_ref, total_ref,
):
    blocks, _, lanes = node_ref.shape
    me = lax.axis_index("dom")
    for k in range(blocks):
        total_ref[k] = node_ref[k]
    for o in range(2 * reach):
        present, there = neighbour(me, count, offset_of(o, reach))
        piece = got_ref[there]
        for m in range(width):
            b = send_ref[o, m]
            total_ref[b] = total_ref[b] - jnp.where(present, piece[m : m + 1], 0.0)
    hidden = act_ref.shape[0]
    out_sum = jnp.zeros((hidden, lanes), jnp.float32)
    bias_sum = jnp.zeros((hidden, lanes), jnp.float32)
    grad = jnp.zeros((hidden, f_ref.shape[1]), jnp.float32)
    group = 4
    for c in range(blocks // group):
        highs = []
        lows = []
        for k in range(c * group, (c + 1) * group):
            act = act_ref[:, k * lanes : (k + 1) * lanes]
            node = total_ref[k] * scale
            weighted = act * node
            pre = node - weighted * act
            out_sum = out_sum + weighted
            bias_sum = bias_sum + pre
            high = pre.astype(jnp.bfloat16)
            highs.append(high)
            lows.append((pre - high.astype(jnp.float32)).astype(jnp.bfloat16))
        f = f_ref[c * group * lanes : (c + 1) * group * lanes]
        grad = grad + lax.dot_general(
            jnp.concatenate(highs, axis=1), f, NN, preferred_element_type=jnp.float32
        )
        grad = grad + lax.dot_general(
            jnp.concatenate(lows, axis=1), f, NN, preferred_element_type=jnp.float32
        )
    v = v_ref[...]
    grad_ref[...] = grad * v
    side_ref[:, 0:1] = jnp.sum(bias_sum, axis=1, keepdims=True) * v
    side_ref[:, 1:2] = jnp.sum(out_sum, axis=1, keepdims=True)


def local(
    features, w_input, b_input, w_output, terminal, start_counts, visit_counts, dest_nodes,
    tile_rows, tile_cols, send_blocks, tile_weight,
):
    f32, bf16 = jnp.float32, jnp.bfloat16
    nodes = features.shape[0]
    tiles, lanes, _ = tile_weight.shape
    blocks = nodes // lanes
    rows = terminal.shape[0]
    hidden = w_input.shape[1]
    feat = features.shape[1]
    reach = send_blocks.shape[0] // 2
    width = send_blocks.shape[1]
    slots = 2 * reach * width
    count = lax.axis_size("dom")
    shape = lambda *s: jax.ShapeDtypeStruct(s, f32)
    geometry = (count, reach, width)
    bind = lambda kernel: functools.partial(kernel, *geometry)
    swap = lambda x: lax.all_to_all(x, "dom", 0, 0, tiled=True)
    dest = dest_nodes[:, None]
    column_v = w_output[:, None]

    field = shape(blocks, rows, lanes)
    parcel = shape(count, width * rows, lanes)
    split = pltpu.VMEM((blocks + slots, 2 * rows, lanes), bf16)
    total = pltpu.VMEM((blocks, rows, lanes), f32)
    wide = pltpu.VMEM((blocks + slots, rows, lanes), f32)
    step_flops = 2 * tiles * lanes * lanes * 2 * rows
    step_bytes = tiles * lanes * lanes * 2

    z0, out = call(
        bind(first_kernel), (field, parcel), [], (send_blocks, terminal), 1, nodes * rows, nodes * rows * 8
    )
    far = swap(out)
    act, growth = call(
        network_kernel,
        (shape(hidden, nodes), shape(blocks, 1, lanes)),
        [],
        (w_input.T, b_input[:, None], column_v, features),
        0,
        2 * nodes * hidden * feat,
        nodes * hidden * 4,
    )
    z1, out = call(
        bind(backup_kernel),
        (field, parcel),
        [split, total],
        (tile_rows, tile_cols, send_blocks, tile_weight, z0, far, growth, dest),
        3,
        step_flops,
        step_bytes,
    )
    got = swap(out)
    z2, out = call(
        bind(backup_kernel),
        (field, parcel),
        [split, total],
        (tile_rows, tile_cols, send_blocks, tile_weight, z1, got, growth, dest),
        3,
        step_flops,
        step_bytes,
    )
    got = swap(out)
    values, flow, out = call(
        bind(turn_kernel),
        (shape(rows, nodes), field, parcel),
        [split, total, wide],
        (tile_rows, tile_cols, tile_weight, z2, got, growth, dest, start_counts),
        2,
        2 * step_flops,
        step_bytes,
    )
    got = swap(out)
    first, flow, out = call(
        bind(spread_kernel),
        (field, field, parcel),
        [split, wide],
        (tile_rows, tile_cols, send_blocks, tile_weight, flow, got, growth),
        3,
        step_flops,
        step_bytes,
    )
    got = swap(out)
    node, out = call(
        bind(last_kernel),
        (shape(blocks, 1, lanes), shape(count, 8, lanes)),
        [split, wide, total],
        (
            tile_rows, tile_cols, send_blocks, tile_weight, flow, got, growth,
            z0, z1, z2, first, visit_counts, far,
        ),
        3,
        step_flops,
        step_bytes,
    )
    got = swap(out)
    scale = 1.0 / math.sqrt(nodes * count * rows * lax.axis_size("dest"))
    grad, side = call(
        functools.partial(gradient_kernel, *geometry, scale),
        (shape(hidden, feat), shape(hidden, 2)),
        [pltpu.VMEM((blocks, 1, lanes), f32)],
        (send_blocks, column_v, features, act, node, got),
        1,
        4 * nodes * hidden * feat,
        nodes * hidden * 4,
    )
    every = ("dest", "dom")
    members = count * lax.axis_size("dest")
    packed = jnp.concatenate([grad, side.T.reshape(-1, feat)], axis=0)
    height = packed.shape[0]
    share = -(-height // members)
    share = -(-share // 8) * 8
    packed = jnp.pad(packed, ((0, share * members - height), (0, 0)))
    mine = lax.all_to_all(packed.reshape(members, share, feat), every, 0, 0, tiled=True).sum(axis=0)
    spread = jnp.broadcast_to(mine[None], (members, share, feat))
    summed = lax.all_to_all(spread, every, 0, 0, tiled=True).reshape(members * share, feat)
    side = summed[hidden : hidden + 2 * hidden // feat].reshape(2, hidden)
    return values, summed[:hidden].T, side[0], side[1]


def solution(mesh):
    in_specs = (
        P("dom", None),
        P(),
        P(),
        P(),
        P("dest", "dom"),
        P("dest", "dom"),
        P("dest", "dom"),
        P("dest"),
        P("dom"),
        P("dom"),
        P("dom", None),
        P("dom", None, None),
    )
    out_specs = (P("dest", "dom"), P(), P(), P())
    return jax.shard_map(local, mesh=mesh, in_specs=in_specs, out_specs=out_specs, check_vma=False)
```

profile of v0, /device:TPU:0, one launch (start us, length us, event | category | flops | bytes accessed | tf_op | source)
XLA Modules:
  0.0 138.0 jit_solution(6784141500544183866)
XLA Ops:
  0.6 0.9 copy.32.send_ref
  1.5 0.9 copy-done.7
  2.5 1.4 shard_map.147
  3.9 7.4 %all-to-all-start = ((f32[16,32,128]{2,1,0:T(8,128)}), f32[16,32,128]{2,1,0:T(8,128)S(1)}, u32[]{:S(2)}, u32[]{:S(2)}) async-start(f32[16,32,128]{2,1,0:T(8,128)} %get-tuple-element.23), calls=%async_computation | async-start | bytes 524288 | tf_op jit(solution)/shard_map/all_to_all | solution.py:289
  11.3 0.7 copy.31.dest_ref
  12.0 1.6 %copy.27 = bf16[128,512]{0,1:T(8,128)(2,1)} copy(bf16[128,512]{1,0:T(8,128)(2,1)} %param.13) | data formatting | bytes 262144 | tf_op args[1]
  13.7 0.8 copy.29.v_ref
  14.5 1.5 %copy.28.b_ref = f32[512,1]{1,0:T(8,128)} copy(f32[512,1]{0,1:T(1,128)} %bitcast.21) | data formatting | bytes 4096 | tf_op jit(solution)/shard_map/broadcast_in_dim | solution.py:309
  16.0 1.2 copy-done.3
  17.2 0.9 copy-done.8
  18.2 0.9 copy-done.9
  19.1 1.4 shard_map.148
  20.5 3.3 %copy-done.2 = f32[512,4096]{1,0:T(8,128)} copy-done((f32[512,4096]{1,0:T(8,128)}, f32[512,4096]{1,0:T(8,128)S(1)}, u32[]{:S(2)}) %copy-start.2) | copy-done | bytes 8388632
  23.7 1.7 %copy-done = bf16[80,128,128]{2,1,0:T(8,128)(2,1)S(1)} copy-done((bf16[80,128,128]{2,1,0:T(8,128)(2,1)S(1)}, bf16[80,128,128]{2,1,0:T(8,128)(2,1)}, u32[]{:S(2)}) %copy-start) | copy-done | bytes 2621464
  25.5 0.7 copy-done.10
  26.1 0.7 copy-done.11
  26.8 2.1 %shard_map.149 = (f32[32,16,128]{2,1,0:T(8,128)S(1)}, f32[16,32,128]{2,1,0:T(8,128)S(1)}) custom-call(s32[80]{0:T(128)S(1)} %copy-done.10, s32[80]{0:T(128)S(1)} %copy-done.11, s32[8,2]{1,0:T(8,128)S(1)} %copy.32.send_ref, bf16[80,128,128]{2,1,0:T(8,128)(2,1)S(1)} %copy-done, f32[32,16,128]{2,1,0:T(8,128)S(1)} %get-tuple-element.22.z_ref.z0_ref, ...), custom_call_target="tpu_custom_call" | custom-call | flops 83886080 | bytes 2621440 | tf_op jit(solution)/shard_map/pallas_call | solution.py:30
  29.0 16.1 %all_to_all.40.got_ref = f32[16,32,128]{2,1,0:T(8,128)S(1)} all-to-all(f32[16,32,128]{2,1,0:T(8,128)S(1)} %get-tuple-element.26), channel_id=1, replica_groups=mesh['dom'=16,'dest'=2] {'dom'}, dimensions={0} | all-to-all | bytes 524288 | tf_op jit(solution)/shard_map/all_to_all | solution.py:289
  45.0 2.1 %shard_map.150 = (f32[32,16,128]{2,1,0:T(8,128)S(1)}, f32[16,32,128]{2,1,0:T(8,128)S(1)}) custom-call(s32[80]{0:T(128)S(1)} %copy-done.10, s32[80]{0:T(128)S(1)} %copy-done.11, s32[8,2]{1,0:T(8,128)S(1)} %copy.32.send_ref, bf16[80,128,128]{2,1,0:T(8,128)(2,1)S(1)} %copy-done.1, f32[32,16,128]{2,1,0:T(8,128)S(1)} %get-tuple-element.25.z_ref.z1_ref, ...), custom_call_target="tpu_custom_call" | custom-call | flops 83886080 | bytes 2621440 | tf_op jit(solution)/shard_map/pallas_call | solution.py:30
  47.2 12.7 %all_to_all.41.got_ref = f32[16,32,128]{2,1,0:T(8,128)S(1)} all-to-all(f32[16,32,128]{2,1,0:T(8,128)S(1)} %get-tuple-element.28), channel_id=1, replica_groups=mesh['dom'=16,'dest'=2] {'dom'}, dimensions={0} | all-to-all | bytes 524288 | tf_op jit(solution)/shard_map/all_to_all | solution.py:289
  59.9 0.9 copy-done.5
  60.8 3.4 %shard_map.151 = (f32[16,4096]{1,0:T(8,128)}, f32[32,16,128]{2,1,0:T(8,128)S(1)}, f32[16,32,128]{2,1,0:T(8,128)S(1)}) custom-call(s32[80]{0:T(128)S(1)} %copy-done.10, s32[80]{0:T(128)S(1)} %copy-done.11, bf16[80,128,128]{2,1,0:T(8,128)(2,1)S(1)} %copy-done.1, f32[32,16,128]{2,1,0:T(8,128)S(1)} %get-tuple-element.27.z_ref.z2_ref, ...), custom_call_target="tpu_custom_call" | custom-call | flops 167772160 | bytes 2621440 | tf_op jit(solution)/shard_map/pallas_call | solution.py:30
  64.3 12.7 %all_to_all.42.got_ref = f32[16,32,128]{2,1,0:T(8,128)S(1)} all-to-all(f32[16,32,128]{2,1,0:T(8,128)S(1)} %get-tuple-element.32), channel_id=1, replica_groups=mesh['dom'=16,'dest'=2] {'dom'}, dimensions={0} | all-to-all | bytes 524288 | tf_op jit(solution)/shard_map/all_to_all | solution.py:289
  77.0 1.5 %shard_map.152 = (f32[32,16,128]{2,1,0:T(8,128)S(1)}, f32[32,16,128]{2,1,0:T(8,128)S(1)}, f32[16,32,128]{2,1,0:T(8,128)S(1)}) custom-call(s32[80]{0:T(128)S(1)} %copy-done.10, s32[80]{0:T(128)S(1)} %copy-done.11, s32[8,2]{1,0:T(8,128)S(1)} %copy.32.send_ref, bf16[80,128,128]{2,1,0:T(8,128)(2,1)S(1)} %copy-done.1, ...), custom_call_target="tpu_custom_call" | custom-call | flops 83886080 | bytes 2621440 | tf_op jit(solution)/shard_map/pallas_call | solution.py:30
  78.5 12.7 %all_to_all.43.got_ref = f32[16,32,128]{2,1,0:T(8,128)S(1)} all-to-all(f32[16,32,128]{2,1,0:T(8,128)S(1)} %get-tuple-element.34), channel_id=1, replica_groups=mesh['dom'=16,'dest'=2] {'dom'}, dimensions={0} | all-to-all | bytes 524288 | tf_op jit(solution)/shard_map/all_to_all | solution.py:289
  91.2 1.6 %shard_map.153 = (f32[32,1,128]{2,1,0:T(1,128)S(1)}, f32[16,8,128]{2,1,0:T(8,128)S(1)}) custom-call(s32[80]{0:T(128)S(1)} %copy-done.10, s32[80]{0:T(128)S(1)} %copy-done.12, s32[8,2]{1,0:T(8,128)S(1)} %copy.32.send_ref, bf16[80,128,128]{2,1,0:T(8,128)(2,1)S(1)} %copy-done.1, f32[32,16,128]{2,1,0:T(8,128)S(1)} %get-tuple-element.33.flow_ref, ...), custom_call_target="tpu_custom_call" | custom-call | flops 83886080 | bytes 2621440 | tf_op jit(solution)/shard_map/pallas_call | solution.py:30
  92.8 9.6 %all_to_all.44.got_ref = f32[16,8,128]{2,1,0:T(8,128)S(1)} all-to-all(f32[16,8,128]{2,1,0:T(8,128)S(1)} %get-tuple-element.37), channel_id=1, replica_groups=mesh['dom'=16,'dest'=2] {'dom'}, dimensions={0} | all-to-all | bytes 131072 | tf_op jit(solution)/shard_map/all_to_all | solution.py:289
  102.4 3.9 %shard_map.154 = (f32[512,128]{1,0:T(8,128)S(1)}, f32[512,2]{1,0:T(8,128)S(1)}) custom-call(s32[8,2]{1,0:T(8,128)S(1)} %copy.32.send_ref, f32[512,1]{1,0:T(8,128)S(1)} %copy.29.v_ref, bf16[4096,128]{1,0:T(8,128)(2,1)S(1)} %copy-done.4, f32[512,4096]{1,0:T(8,128)S(1)} %bitcast.14, f32[32,1,128]{2,1,0:T(1,128)S(1)} %get-tuple-element.36.node_ref, ...), custom_call_target="tpu_custom_call" | custom-call | flops 1073741824 | bytes 8388608 | tf_op jit(solution)/shard_map/pallas_call | solution.py:30
  106.4 14.8 %all_to_all.45 = f32[32,24,128]{2,1,0:T(8,128)S(1)} all-to-all(f32[32,24,128]{2,1,0:T(8,128)S(1)} %bitcast.17), channel_id=1, replica_groups=mesh['dom'=16,'dest'=2] {'dest','dom'}, dimensions={0} | all-to-all | bytes 786432 | tf_op jit(solution)/shard_map/all_to_all | solution.py:384
  121.3 15.2 %all_to_all.46 = f32[32,24,128]{2,1,0:T(8,128)S(1)} all-to-all(f32[32,24,128]{2,1,0:T(8,128)S(1)} %broadcast_in_dim.18), channel_id=1, replica_groups=mesh['dom'=16,'dest'=2] {'dest','dom'}, dimensions={0} | all-to-all | bytes 786432 | tf_op jit(solution)/shard_map/all_to_all | solution.py:386
  136.5 0.6 slice_bitcast_fusion.1
  137.2 0.8 copy.40
  (29 shorter events, 0.3 us)
Async XLA Ops:
  0.6 44.4 %copy-start.1 = (bf16[80,128,128]{2,1,0:T(8,128)(2,1)S(1)}, bf16[80,128,128]{2,1,0:T(8,128)(2,1)}, u32[]{:S(2)}) copy-start(bf16[80,128,128]{2,1,0:T(8,128)(2,1)} %w_ref.9) | copy-start | bytes 7864324
  1.5 0.9 copy-start.7
  3.9 19.9 %all-to-all-start = ((f32[16,32,128]{2,1,0:T(8,128)}), f32[16,32,128]{2,1,0:T(8,128)S(1)}, u32[]{:S(2)}, u32[]{:S(2)}) async-start(f32[16,32,128]{2,1,0:T(8,128)} %get-tuple-element.23), calls=%async_computation | async-start | bytes 524288 | tf_op jit(solution)/shard_map/all_to_all | solution.py:289
  16.0 1.2 copy-start.3
  17.2 0.9 copy-start.8
  18.2 0.9 copy-start.9
  19.1 72.1 %copy-start.12 = (s32[80]{0:T(128)S(1)}, s32[80]{0:T(128)}, u32[]{:S(2)}) copy-start(s32[80]{0:T(128)} %cols_ref.9) | copy-start | bytes 964
  20.5 3.3 %copy-start.2 = (f32[512,4096]{1,0:T(8,128)}, f32[512,4096]{1,0:T(8,128)S(1)}, u32[]{:S(2)}) copy-start(f32[512,4096]{1,0:T(8,128)S(1)} %get-tuple-element.30.act_ref) | copy-start | bytes 25165828
  23.7 1.7 %copy-start = (bf16[80,128,128]{2,1,0:T(8,128)(2,1)S(1)}, bf16[80,128,128]{2,1,0:T(8,128)(2,1)}, u32[]{:S(2)}) copy-start(bf16[80,128,128]{2,1,0:T(8,128)(2,1)} %w_ref.9) | copy-start | bytes 7864324
  25.5 0.7 copy-start.10
  26.1 0.7 copy-start.11
  26.8 64.4 %copy-start.6 = (s32[16,4096]{1,0:T(8,128)S(1)}, s32[16,4096]{1,0:T(8,128)}, u32[]{:S(2)}) copy-start(s32[16,4096]{1,0:T(8,128)} %visit_ref.1) | copy-start | bytes 786436
  28.9 73.4 %slice-start = ((s8[8388608]{0:T(1024)(128)(4,1)}), s8[4194304]{0:T(1024)(128)(4,1)S(1)}, s32[]{:S(2)}) async-start(s8[8388608]{0:T(1024)(128)(4,1)} %bitcast.13), calls=%async_computation.8 | async-start | bytes 8388608
  28.9 73.4 %copy-start.4 = (bf16[4096,128]{1,0:T(8,128)(2,1)S(1)}, bf16[4096,128]{1,0:T(8,128)(2,1)}, u32[]{:S(2)}) copy-start(bf16[4096,128]{1,0:T(8,128)(2,1)} %f_ref.3) | copy-start | bytes 3145732
  59.9 1.0 copy-start.5
  77.0 25.4 %slice-start.1 = ((s8[8388608]{0:T(1024)(128)(4,1)}), s8[4194304]{0:T(1024)(128)(4,1)S(1)}, s32[]{:S(2)}) async-start(s8[8388608]{0:T(1024)(128)(4,1)} %bitcast.13), calls=%async_computation.9 | async-start | bytes 8388608
where the time goes:
time: 139 us; the launch traced here: 138 us
  blocking collectives  93.8 us (67%)
  local copies, waits for them, and re-layouts  18.5 us (13%)
  Pallas kernels  17.4 us (13%)
  starting transfers between devices  7.41 us (5%)
    all_to_all x5, blocking collectives, local(): swap = lambda x: lax.all_to_all(x, 'dom', 0, 0, tiled=True)  63.7 us
    pallas_call x8, Pallas kernels, call(): pl.pallas_call(kernel, out_shape=out_shape, in_specs=[pl.BlockSpec(memory...  17.4 us
    all_to_all x1, blocking collectives, local(): lax.all_to_all(spread, every, 0, 0, tiled=True)  15.2 us
    all_to_all x1, blocking collectives, local(): lax.all_to_all(packed.reshape(members, share, feat), every, 0, 0, tiled=T...  14.8 us
    unnamed x33, local copies, waits for them, and re-layouts  14.7 us
    all_to_all x1, starting transfers between devices, local(): swap = lambda x: lax.all_to_all(x, 'dom', 0, 0, tiled=True)  7.41 us
  transfers between devices with their start and end apart: 1, of which 0 were waited for; matrix products, arithmetic and copies ran while one was open for 3% of the time, Pallas kernels for 1%

commit v1 on v0

v1 whole, which is shorter than its diff:
```python
import functools
import math

import jax
import jax.numpy as jnp
from jax import lax
from jax.experimental import pallas as pl
from jax.experimental.pallas import tpu as pltpu
from jax.sharding import PartitionSpec as P

STEPS = 3
GOAL_GAIN = 32.0
VMEM_GRANT = 20 << 20

NT = (((1,), (1,)), ((), ()))
NN = (((1,), (0,)), ((), ()))


def offset_of(o, reach):
    return o - reach if o < reach else o - reach + 1


def present(me, count, shift):
    there = me + shift
    return jnp.logical_and(there >= 0, there < count)


def place(me, shift):
    origin = me - shift
    k = jnp.bitwise_xor(origin, me) & 3
    core, side, odd = me & 1, (me >> 1) & 1, (me >> 2) & 1
    apart = (origin >> 2) - (me >> 2)
    here = jnp.where(k == 1, 1 + core, jnp.where(k == 2, 5 - side, 7 - side))
    below = jnp.where(odd == 1, 8, 12) + k
    above = jnp.where(odd == 1, 12, 8) + k
    return jnp.where(apart == 0, here, jnp.where(apart < 0, below, above))


def exchange(odd, even):
    me = lax.axis_index("dom")
    devices = range(lax.axis_size("dom"))
    core_zero = me % 2 == 0
    group_even = (me // 4) % 2 == 0

    def partner(i, flip):
        j = (i // 4 + (1 if (i // 4) % 2 == 1 else -1)) * 4 + i % 4
        return j if j in devices else i ^ 1

    flip = lambda x, bit: lax.ppermute(x, "dom", [(i, i ^ bit) for i in devices])
    near = flip(odd, 1)
    side = flip(
        jnp.stack(
            [
                even[2],
                even[1],
                jnp.where(core_zero, near[2], near[3]),
                jnp.where(core_zero, near[0], near[1]),
            ]
        ),
        2,
    )
    up = jnp.stack([even[3], near[3], side[0], side[2]])
    down = jnp.stack([even[0], near[0], side[1], side[3]])
    first = flip(jnp.where(group_even, up, down), 4)
    second = lax.ppermute(
        jnp.where(group_even, down, up), "dom", [(i, partner(i, 1)) for i in devices]
    )
    return near, side, first, second


def call(kernel, out_shape, scratch, smem, vmem, flops, moved):
    space = lambda kind: pl.BlockSpec(memory_space=kind)
    return pl.pallas_call(
        kernel,
        out_shape=out_shape,
        in_specs=[space(pltpu.SMEM)] * len(smem) + [space(pltpu.VMEM)] * len(vmem),
        out_specs=jax.tree.map(lambda _: space(pltpu.VMEM), out_shape),
        scratch_shapes=scratch,
        compiler_params=pltpu.CompilerParams(vmem_limit_bytes=VMEM_GRANT),
        cost_estimate=pl.CostEstimate(flops=flops, bytes_accessed=moved, transcendentals=0),
    )(*smem, *vmem)


def store_split(ref, k, x):
    rows = x.shape[0]
    high = x.astype(jnp.bfloat16)
    low = (x - high.astype(jnp.float32)).astype(jnp.bfloat16)
    ref[k, :rows] = high
    ref[k, rows:] = low


def product(lhs, rhs, dims):
    both = lax.dot_general(lhs, rhs, dims, preferred_element_type=jnp.float32)
    rows = both.shape[0] // 2
    return both[:rows] + both[rows:]


def offsets(reach):
    return [offset_of(o, reach) for o in range(2 * reach)]


def send_items(odd_ref, even_ref, reach, width, sign, item):
    ways = offsets(reach)
    odds = [f for f in ways if f % 2]
    evens = [f for f in ways if f % 2 == 0]
    for o, f in enumerate(ways):
        shift = sign * f
        ref, at = (odd_ref, odds.index(shift)) if shift % 2 else (even_ref, evens.index(shift))
        for m in range(width):
            piece = item(o, m)
            rows = piece.shape[0]
            ref[at, m * rows : (m + 1) * rows] = piece


def collect(all_ref, parts):
    at = 0
    for part in parts:
        for k in range(part.shape[0]):
            all_ref[at] = part[k]
            at += 1


def network_kernel(w_ref, b_ref, v_ref, f_ref, act_ref, growth_ref):
    lanes = growth_ref.shape[2]
    hidden = act_ref.shape[0]
    group = 2
    w = w_ref[...].T
    b = jnp.broadcast_to(b_ref[...], (lanes, hidden)).T
    v = jnp.broadcast_to(v_ref[...], (lanes, hidden)).T
    for c in range(growth_ref.shape[0] // group):
        f = f_ref[c * group * lanes : (c + 1) * group * lanes]
        pre = lax.dot_general(w, f, NT, preferred_element_type=jnp.float32)
        for k in range(group):
            at = c * group + k
            act = jnp.tanh(pre[:, k * lanes : (k + 1) * lanes] + b)
            act_ref[:, at * lanes : (at + 1) * lanes] = act
            growth_ref[at] = jnp.exp(jnp.sum(act * v, axis=0, keepdims=True))


def first_kernel(reach, width, send_ref, term_ref, z_ref, split_ref, odd_ref, even_ref):
    blocks, _, lanes = z_ref.shape
    for k in range(blocks):
        z = jnp.exp(term_ref[:, k * lanes : (k + 1) * lanes])
        z_ref[k] = z
        store_split(split_ref, k, z)
    send_items(odd_ref, even_ref, reach, width, 1, lambda o, m: z_ref[send_ref[o, m]])


def diagonal_kernel(w_ref, split_ref, sum_ref):
    for k in range(split_ref.shape[0]):
        sum_ref[k] = product(split_ref[k], w_ref[k], NT)


def back_diagonal_kernel(w_ref, split_ref, part_ref, sum_ref):
    for k in range(split_ref.shape[0]):
        sum_ref[k] = part_ref[k] + product(split_ref[k], w_ref[k], NN)


def backed_up(
    reach, width, rows_ref, cols_ref, w_ref, split_ref, part_ref, parts, all_ref, ext_ref, sum_ref
):
    blocks, rows, _ = part_ref.shape
    me = lax.axis_index("dom")
    collect(all_ref, parts)
    for o, f in enumerate(offsets(reach)):
        at = place(me, f)
        for m in range(width):
            store_split(
                ext_ref, blocks + o * width + m, all_ref[at, m * rows : (m + 1) * rows]
            )
    for k in range(blocks):
        ext_ref[k] = split_ref[k]
        sum_ref[k] = part_ref[k]
    for t in range(blocks, w_ref.shape[0]):
        r = rows_ref[t]
        sum_ref[r] = sum_ref[r] + product(ext_ref[cols_ref[t]], w_ref[t], NT)


def goal_of(dest_ref, rows, lanes):
    row = lax.broadcasted_iota(jnp.int32, (rows, lanes), 0)
    dest = jnp.zeros((rows, lanes), jnp.int32)
    for d in range(rows):
        dest = jnp.where(row == d, dest_ref[d], dest)
    return dest


def with_goal(k, growth_ref, sum_ref, dest, me):
    blocks, rows, lanes = sum_ref.shape
    node = (me * blocks + k) * lanes + lax.broadcasted_iota(jnp.int32, (rows, lanes), 1)
    return growth_ref[k] * sum_ref[k] + jnp.where(node == dest, GOAL_GAIN, 0.0)


def backup_kernel(
    reach, width, rows_ref, cols_ref, send_ref, dest_ref, w_ref, split_ref, part_ref, growth_ref,
    near_ref, side_ref, first_ref, second_ref,
    z_ref, next_ref, odd_ref, even_ref, all_ref, ext_ref, sum_ref,
):
    blocks, rows, lanes = z_ref.shape
    me = lax.axis_index("dom")
    backed_up(
        reach, width, rows_ref, cols_ref, w_ref, split_ref, part_ref,
        (near_ref, side_ref, first_ref, second_ref), all_ref, ext_ref, sum_ref,
    )
    dest = goal_of(dest_ref, rows, lanes)
    for k in range(blocks):
        z = with_goal(k, growth_ref, sum_ref, dest, me)
        z_ref[k] = z
        store_split(next_ref, k, z)
    send_items(odd_ref, even_ref, reach, width, 1, lambda o, m: z_ref[send_ref[o, m]])


def spread_out(rows_ref, cols_ref, w_ref, split_ref, ext_ref, blocks):
    for k in range(ext_ref.shape[0]):
        ext_ref[k] = jnp.zeros(ext_ref.shape[1:], jnp.float32)
    for t in range(blocks, w_ref.shape[0]):
        c = cols_ref[t]
        ext_ref[c] = ext_ref[c] + product(split_ref[rows_ref[t]], w_ref[t], NN)


def turn_kernel(
    reach, width, rows_ref, cols_ref, dest_ref, w_ref, split_ref, part_ref, growth_ref,
    near_ref, side_ref, first_ref, second_ref, start_ref,
    values_ref, next_ref, rest_ref, odd_ref, even_ref, all_ref, ext_ref, sum_ref, flow_ref,
):
    blocks, rows, lanes = part_ref.shape
    me = lax.axis_index("dom")
    backed_up(
        reach, width, rows_ref, cols_ref, w_ref, split_ref, part_ref,
        (near_ref, side_ref, first_ref, second_ref), all_ref, ext_ref, sum_ref,
    )
    dest = goal_of(dest_ref, rows, lanes)
    for k in range(blocks):
        z = with_goal(k, growth_ref, sum_ref, dest, me)
        span = slice(k * lanes, (k + 1) * lanes)
        values_ref[:, span] = jnp.log(z)
        store_split(next_ref, k, growth_ref[k] * start_ref[:, span].astype(jnp.float32) / z)
    spread_out(rows_ref, cols_ref, w_ref, next_ref, flow_ref, blocks)
    for k in range(blocks):
        rest_ref[k] = flow_ref[k]
    send_items(
        odd_ref, even_ref, reach, width, -1, lambda o, m: flow_ref[blocks + o * width + m]
    )


def take_returned(count, reach, width, send_ref, parts, all_ref, into_ref):
    rows = into_ref.shape[1]
    me = lax.axis_index("dom")
    collect(all_ref, parts)
    for o, f in enumerate(offsets(reach)):
        there = present(me, count, f)
        at = place(me, -f)
        for m in range(width):
            b = send_ref[o, m]
            piece = all_ref[at, m * rows : (m + 1) * rows]
            into_ref[b] = into_ref[b] + jnp.where(there, piece, 0.0)


def flows(
    count, reach, width, rows_ref, cols_ref, send_ref, w_ref, growth_ref, sum_ref, parts,
    u_ref, next_ref, rest_ref, all_ref, flow_ref,
):
    blocks = u_ref.shape[0]
    for k in range(blocks):
        u_ref[k] = sum_ref[k]
    take_returned(count, reach, width, send_ref, parts, all_ref, u_ref)
    for k in range(blocks):
        store_split(next_ref, k, growth_ref[k] * u_ref[k])
    spread_out(rows_ref, cols_ref, w_ref, next_ref, flow_ref, blocks)
    for k in range(blocks):
        rest_ref[k] = flow_ref[k]


def spread_kernel(
    count, reach, width, rows_ref, cols_ref, send_ref, w_ref, growth_ref, sum_ref,
    near_ref, side_ref, first_ref, second_ref,
    u_ref, next_ref, rest_ref, odd_ref, even_ref, all_ref, flow_ref,
):
    blocks = u_ref.shape[0]
    flows(
        count, reach, width, rows_ref, cols_ref, send_ref, w_ref, growth_ref, sum_ref,
        (near_ref, side_ref, first_ref, second_ref), u_ref, next_ref, rest_ref, all_ref, flow_ref,
    )
    send_items(
        odd_ref, even_ref, reach, width, -1, lambda o, m: flow_ref[blocks + o * width + m]
    )


def last_kernel(
    count, reach, width, rows_ref, cols_ref, send_ref, w_ref, growth_ref, sum_ref,
    near_ref, side_ref, first_ref, second_ref, z_near_ref, z_side_ref, z_first_ref, z_second_ref,
    u_ref, next_ref, rest_ref, odd_ref, even_ref, all_ref, flow_ref, far_ref,
):
    blocks, rows, lanes = u_ref.shape
    me = lax.axis_index("dom")
    flows(
        count, reach, width, rows_ref, cols_ref, send_ref, w_ref, growth_ref, sum_ref,
        (near_ref, side_ref, first_ref, second_ref), u_ref, next_ref, rest_ref, all_ref, flow_ref,
    )
    collect(far_ref, (z_near_ref, z_side_ref, z_first_ref, z_second_ref))
    ways = offsets(reach)
    odds = [f for f in ways if f % 2]
    evens = [f for f in ways if f % 2 == 0]
    row = lax.broadcasted_iota(jnp.int32, odd_ref.shape[1:], 0)
    for o, f in enumerate(ways):
        at = place(me, f)
        item = jnp.zeros(odd_ref.shape[1:], jnp.float32)
        for m in range(width):
            lost = far_ref[at, m * rows : (m + 1) * rows] * flow_ref[blocks + o * width + m]
            item = jnp.where(row == m, jnp.sum(lost, axis=0, keepdims=True), item)
        if f % 2:
            odd_ref[odds.index(-f)] = item
        else:
            even_ref[evens.index(-f)] = item


def node_kernel(
    w_ref, split_ref, part_ref, z0_ref, z1_ref, z2_ref, u1_ref, u2_ref, visit_ref, node_ref
):
    blocks, _, lanes = part_ref.shape
    for k in range(blocks):
        u3 = part_ref[k] + product(split_ref[k], w_ref[k], NN)
        left = (
            visit_ref[:, k * lanes : (k + 1) * lanes].astype(jnp.float32)
            - z2_ref[k] * u1_ref[k]
            - z1_ref[k] * u2_ref[k]
            - z0_ref[k] * u3
        )
        node_ref[k] = jnp.sum(left, axis=0, keepdims=True)


def gradient_kernel(
    count, reach, width, scale, send_ref, v_ref, f_ref, act_ref, node_ref,
    near_ref, side_ref, first_ref, second_ref, grad_ref, total_ref, all_ref,
):
    blocks, _, lanes = node_ref.shape
    me = lax.axis_index("dom")
    collect(all_ref, (near_ref, side_ref, first_ref, second_ref))
    for k in range(blocks):
        total_ref[k] = node_ref[k]
    for o, f in enumerate(offsets(reach)):
        there = present(me, count, f)
        at = place(me, -f)
        for m in range(width):
            b = send_ref[o, m]
            total_ref[b] = total_ref[b] - jnp.where(there, all_ref[at, m : m + 1], 0.0)
    hidden = act_ref.shape[0]
    out_sum = jnp.zeros((hidden, lanes), jnp.float32)
    bias_sum = jnp.zeros((hidden, lanes), jnp.float32)
    grad = jnp.zeros((hidden, f_ref.shape[1]), jnp.float32)
    group = 4
    for c in range(blocks // group):
        highs = []
        lows = []
        for k in range(c * group, (c + 1) * group):
            act = act_ref[:, k * lanes : (k + 1) * lanes]
            node = total_ref[k] * scale
            weighted = act * node
            pre = node - weighted * act
            out_sum = out_sum + weighted
            bias_sum = bias_sum + pre
            high = pre.astype(jnp.bfloat16)
            highs.append(high)
            lows.append((pre - high.astype(jnp.float32)).astype(jnp.bfloat16))
        f = f_ref[c * group * lanes : (c + 1) * group * lanes]
        grad = grad + lax.dot_general(
            jnp.concatenate(highs, axis=1), f, NN, preferred_element_type=jnp.float32
        )
        grad = grad + lax.dot_general(
            jnp.concatenate(lows, axis=1), f, NN, preferred_element_type=jnp.float32
        )
    v = v_ref[...]
    parts = hidden // lanes
    for j in range(parts):
        span = slice(j * lanes, (j + 1) * lanes)
        turned = grad[span].T * v[:, span]
        for i in range(f_ref.shape[1] // 8):
            at = (i * parts + j) * 8
            grad_ref[at : at + 8] = turned[i * 8 : (i + 1) * 8]
    ones = jnp.ones((8, lanes), jnp.float32)
    across = lambda x: lax.dot_general(
        ones, x, NT, precision=lax.Precision.HIGHEST, preferred_element_type=jnp.float32
    )[:1]
    bias = across(bias_sum) * v
    out = across(out_sum)
    at = hidden * f_ref.shape[1] // lanes
    for j in range(parts):
        span = slice(j * lanes, (j + 1) * lanes)
        grad_ref[at + j : at + j + 1] = bias[:, span]
        grad_ref[at + parts + j : at + parts + j + 1] = out[:, span]
    grad_ref[at + 2 * parts :] = jnp.zeros_like(grad_ref[at + 2 * parts :])


def local(
    features, w_input, b_input, w_output, terminal, start_counts, visit_counts, dest_nodes,
    tile_rows, tile_cols, send_blocks, tile_weight,
):
    f32, bf16 = jnp.float32, jnp.bfloat16
    nodes, feat = features.shape
    tiles, lanes, _ = tile_weight.shape
    blocks = nodes // lanes
    rows = terminal.shape[0]
    hidden = w_input.shape[1]
    reach = send_blocks.shape[0] // 2
    width = send_blocks.shape[1]
    slots = 2 * reach * width
    count = lax.axis_size("dom")
    assert reach == 4 and count % 8 == 0
    shape = lambda *s: jax.ShapeDtypeStruct(s, f32)
    row_v = w_output[None, :]

    field = shape(blocks, rows, lanes)
    halves = jax.ShapeDtypeStruct((blocks, 2 * rows, lanes), bf16)
    parcel = shape(reach, width * rows, lanes)
    small = shape(reach, 8, lanes)
    all_s = pltpu.VMEM((4 * reach, width * rows, lanes), f32)
    ext_s = pltpu.VMEM((blocks + slots, 2 * rows, lanes), bf16)
    sum_s = pltpu.VMEM((blocks, rows, lanes), f32)
    flow_s = pltpu.VMEM((blocks + slots, rows, lanes), f32)
    bind = lambda kernel, *lead: functools.partial(kernel, *lead, reach, width)
    flops = 2 * tiles * lanes * lanes * 2 * rows
    moved = tiles * lanes * lanes * 2

    def diagonal(split):
        return call(diagonal_kernel, field, [], (), (tile_weight, split), flops, moved)

    def back_diagonal(split, rest):
        return call(back_diagonal_kernel, field, [], (), (tile_weight, split, rest), flops, moved)

    z0, split, odd, even = call(
        bind(first_kernel), (field, halves, parcel, parcel), [], (send_blocks,), (terminal,), flops, moved
    )
    far = exchange(odd, even)
    act, growth = call(
        network_kernel,
        (shape(hidden, nodes), shape(blocks, 1, lanes)),
        [],
        (),
        (w_input, b_input[None, :], row_v, features),
        2 * nodes * hidden * feat,
        nodes * hidden * 4,
    )

    def backup(split, got):
        return call(
            bind(backup_kernel),
            (field, halves, parcel, parcel),
            [all_s, ext_s, sum_s],
            (tile_rows, tile_cols, send_blocks, dest_nodes),
            (tile_weight, split, diagonal(split), growth, *got),
            flops,
            moved,
        )

    z1, split, odd, even = backup(split, far)
    z2, split, odd, even = backup(split, exchange(odd, even))
    got = exchange(odd, even)
    values, split, rest, odd, even = call(
        bind(turn_kernel),
        (shape(rows, nodes), halves, field, parcel, parcel),
        [all_s, ext_s, sum_s, flow_s],
        (tile_rows, tile_cols, dest_nodes),
        (tile_weight, split, diagonal(split), growth, *got, start_counts),
        2 * flops,
        moved,
    )
    got = exchange(odd, even)
    u1, split, rest, odd, even = call(
        bind(spread_kernel, count),
        (field, halves, field, parcel, parcel),
        [all_s, flow_s],
        (tile_rows, tile_cols, send_blocks),
        (tile_weight, growth, back_diagonal(split, rest), *got),
        flops,
        moved,
    )
    got = exchange(odd, even)
    u2, split, rest, odd, even = call(
        bind(last_kernel, count),
        (field, halves, field, small, small),
        [all_s, flow_s, all_s],
        (tile_rows, tile_cols, send_blocks),
        (tile_weight, growth, back_diagonal(split, rest), *got, *far),
        flops,
        moved,
    )
    got = exchange(odd, even)
    node = call(
        node_kernel,
        shape(blocks, 1, lanes),
        [],
        (),
        (tile_weight, split, rest, z0, z1, z2, u1, u2, visit_counts),
        flops,
        moved,
    )
    every = ("dest", "dom")
    members = count * lax.axis_size("dest")
    used = hidden * feat // lanes + 2 * hidden // lanes
    share = -(-used // members)
    scale = 1.0 / math.sqrt(nodes * count * rows * lax.axis_size("dest"))
    packed = call(
        functools.partial(gradient_kernel, count, reach, width, scale),
        shape(share * members, lanes),
        [pltpu.VMEM((blocks, 1, lanes), f32), pltpu.VMEM((4 * reach, 8, lanes), f32)],
        (send_blocks,),
        (row_v, features, act, node, *got),
        4 * nodes * hidden * feat,
        nodes * hidden * 4,
    )
    packed = packed.reshape(members, 1, share * lanes)
    mine = lax.all_to_all(packed, every, 0, 0, tiled=True).sum(axis=0, keepdims=True)
    spread = jnp.broadcast_to(mine, packed.shape)
    summed = lax.all_to_all(spread, every, 0, 0, tiled=True).reshape(share * members, lanes)
    side = summed[hidden * feat // lanes : used].reshape(2, hidden)
    grad = summed[: hidden * feat // lanes].reshape(feat // 8, hidden // lanes, 8, lanes)
    return values, grad.transpose(0, 2, 1, 3).reshape(feat, hidden), side[0], side[1]


def solution(mesh):
    in_specs = (
        P("dom", None),
        P(),
        P(),
        P(),
        P("dest", "dom"),
        P("dest", "dom"),
        P("dest", "dom"),
        P("dest"),
        P("dom"),
        P("dom"),
        P("dom", None),
        P("dom", None, None),
    )
    out_specs = (P("dest", "dom"), P(), P(), P())
    return jax.shard_map(local, mesh=mesh, in_specs=in_specs, out_specs=out_specs, check_vma=False)
```

time: 139 us -> 120 us (0.86)
  blocking collectives: 93.8 us -> 27.6 us
  waiting for transfers between devices: 0.01 us -> 31.8 us
  starting transfers between devices: 7.41 us -> 28.2 us
  local copies, waits for them, and re-layouts: 18.5 us -> 12.3 us
    all_to_all x6 -> x1, blocking collectives: 78.6 us -> 14.7 us  [local(): lax.all_to_all(packed, every, 0, 0, tiled=True).sum(axis=0, keepdims=True)]
    ppermute x0 -> x24, waiting for transfers between devices: none -> 31.8 us  [the longest x18 31.8 us: exchange(): lax.ppermute(x, 'dom', [(i, i ^ bit) for i in devices])]
    ppermute x0 -> x24, starting transfers between devices: none -> 28.2 us  [the longest x18 27.8 us: exchange(): lax.ppermute(x, 'dom', [(i, i ^ bit) for i in devices])]
    all_to_all x1 -> x0, starting transfers between devices: 7.41 us -> none  [local(): swap = lambda x: lax.all_to_all(x, 'dom', 0, 0, tiled=True)]
    unnamed x33 -> x37, local copies, waits for them, and re-layouts: 14.7 us -> 10.8 us
    broadcast_in_dim x4 -> x1, local copies, waits for them, and re-layouts: 3.12 us -> 0.14 us  [local(): spread = jnp.broadcast_to(mine, packed.shape)]
    all_to_all x1, blocking collectives: 15.2 us -> 12.9 us  [local(): lax.all_to_all(spread, every, 0, 0, tiled=True)]
    pallas_call x8 -> x14, Pallas kernels: 17.4 us -> 18.2 us  [call(): pl.pallas_call(kernel, out_shape=out_shape, in_specs=[space(pltpu.SMEM)]...]
  transfers between devices with their start and end apart: 1 -> 24, of which waited for: 0 -> 17; matrix products, arithmetic and copies ran while one was open for 3% -> 0% of each run, Pallas kernels for 1% -> 4%
where the time goes in v1:
time: 120 us; the launch traced here: 119 us
  waiting for transfers between devices  31.8 us (26%)
  starting transfers between devices  28.2 us (24%)
  blocking collectives  27.6 us (23%)
  Pallas kernels  18.2 us (15%)
  local copies, waits for them, and re-layouts  12.3 us (10%)
    ppermute x18, waiting for transfers between devices, exchange(): lax.ppermute(x, 'dom', [(i, i ^ bit) for i in devices])  31.8 us
    ppermute x18, starting transfers between devices, exchange(): lax.ppermute(x, 'dom', [(i, i ^ bit) for i in devices])  27.8 us
    pallas_call x14, Pallas kernels, call(): pl.pallas_call(kernel, out_shape=out_shape, in_specs=[space(pltpu.SMEM)]...  18.2 us
    all_to_all x1, blocking collectives, local(): lax.all_to_all(packed, every, 0, 0, tiled=True).sum(axis=0, keepdims=True)  14.7 us
    all_to_all x1, blocking collectives, local(): lax.all_to_all(spread, every, 0, 0, tiled=True)  12.9 us
    unnamed x37, local copies, waits for them, and re-layouts  10.8 us
  transfers between devices with their start and end apart: 24, of which 17 were waited for; matrix products, arithmetic and copies ran while one was open for 0% of the time, Pallas kernels for 4%

profile of v1, /device:TPU:0, one launch (start us, length us, event | category | flops | bytes accessed | tf_op | source)
XLA Modules:
  0.0 119.5 jit_solution(1342782534899183668)
XLA Ops:
  4.5 2.9 %collective-permute-start.1 = (f32[4,32,128]{2,1,0:T(8,128)S(1)}, f32[4,32,128]{2,1,0:T(8,128)S(1)}, u32[]{:S(2)}, u32[]{:S(2)}) collective-permute-start(f32[4,32,128]{2,1,0:T(8,128)S(1)} %pad_maximum_fusion), channel_id=1, source_target_pairs={{0,4},{2,6},{4,0},{6,2},{8,12},{10,14},{12,8},{14,10},{16,20},{18,... | collective-permute-start | bytes 196616 | tf_op jit(solution)/shard_map/ppermute | solution.py:49
  7.4 2.4 %collective-permute-done.1.side_ref.z_side_ref = f32[4,32,128]{2,1,0:T(8,128)S(1)} collective-permute-done((f32[4,32,128]{2,1,0:T(8,128)S(1)}, f32[4,32,128]{2,1,0:T(8,128)S(1)}, u32[]{:S(2)}, u32[]{:S(2)}) %collective-permute-start.1) | collective-permute-done | bytes 65568 | tf_op jit(solution)/shard_map/ppermute | solution.py:49
  9.9 3.5 %collective-permute-start.2 = (f32[4,32,128]{2,1,0:T(8,128)S(1)}, f32[4,32,128]{2,1,0:T(8,128)S(1)}, u32[]{:S(2)}, u32[]{:S(2)}) collective-permute-start(f32[4,32,128]{2,1,0:T(8,128)S(1)} %get-tuple-element.73), channel_id=1, source_target_pairs={{0,8},{2,10},{4,12},{6,14},{8,0},{10,2},{12,4},{14,6},{16,24},{18,... | collective-permute-start | bytes 196616 | tf_op jit(solution)/shard_map/ppermute | solution.py:49
  13.4 1.7 %copy-done = bf16[80,128,128]{2,1,0:T(8,128)(2,1)S(1)} copy-done((bf16[80,128,128]{2,1,0:T(8,128)(2,1)S(1)}, bf16[80,128,128]{2,1,0:T(8,128)(2,1)}, u32[]{:S(2)}) %copy-start) | copy-done | bytes 2621464
  15.8 1.4 %copy-done.3 = bf16[4096,128]{1,0:T(8,128)(2,1)S(1)} copy-done((bf16[4096,128]{1,0:T(8,128)(2,1)S(1)}, bf16[4096,128]{1,0:T(8,128)(2,1)}, u32[]{:S(2)}) %copy-start.3) | copy-done | bytes 1048600
  19.4 1.4 %shard_map.149 = (f32[512,4096]{1,0:T(8,128)S(1)}, f32[32,1,128]{2,1,0:T(1,128)S(1)}) custom-call(bf16[128,512]{1,0:T(8,128)(2,1)S(1)} %copy-done.16, f32[1,512]{1,0:T(1,128)S(1)} %bitcast.16, f32[1,512]{1,0:T(1,128)S(1)} %bitcast.14, bf16[4096,128]{1,0:T(8,128)(2,1)S(1)} %copy-done.3), custom_call_target="tpu_custom_call" | custom-call | flops 536870912 | bytes 8388608 | tf_op jit(solution)/shard_map/pallas_call | solution.py:73
  20.9 1.7 %copy-done.1 = bf16[80,128,128]{2,1,0:T(8,128)(2,1)S(1)} copy-done((bf16[80,128,128]{2,1,0:T(8,128)(2,1)S(1)}, bf16[80,128,128]{2,1,0:T(8,128)(2,1)}, u32[]{:S(2)}) %copy-start.1) | copy-done | bytes 2621464
  24.6 1.7 %shard_map.150 = (f32[32,16,128]{2,1,0:T(8,128)S(1)}, bf16[32,32,128]{2,1,0:T(8,128)(2,1)S(1)}, f32[4,32,128]{2,1,0:T(8,128)S(1)}, f32[4,32,128]{2,1,0:T(8,128)S(1)}) custom-call(s32[80]{0:T(128)S(1)} %copy-done.7, s32[80]{0:T(128)S(1)} %copy-done.9, s32[8,2]{1,0:T(8,128)S(1)} %copy.24.send_ref, s32[16]{0:T(128)S(1)} %copy-done.11, ...), custom_call_target="tpu_custom_call" | custom-call | flops 83886080 | bytes 2621440 | tf_op jit(solution)/shard_map/pallas_call | solution.py:73
  27.6 1.6 %collective-permute-start.5 = (f32[4,32,128]{2,1,0:T(8,128)S(1)}, f32[4,32,128]{2,1,0:T(8,128)S(1)}, u32[]{:S(2)}, u32[]{:S(2)}) collective-permute-start(f32[4,32,128]{2,1,0:T(8,128)S(1)} %pad_maximum_fusion.3), channel_id=1, source_target_pairs={{0,4},{2,6},{4,0},{6,2},{8,12},{10,14},{12,8},{14,10},{16,20},{18,... | collective-permute-start | bytes 196616 | tf_op jit(solution)/shard_map/ppermute | solution.py:49
  29.2 2.7 %collective-permute-done.5.side_ref = f32[4,32,128]{2,1,0:T(8,128)S(1)} collective-permute-done((f32[4,32,128]{2,1,0:T(8,128)S(1)}, f32[4,32,128]{2,1,0:T(8,128)S(1)}, u32[]{:S(2)}, u32[]{:S(2)}) %collective-permute-start.5) | collective-permute-done | bytes 65568 | tf_op jit(solution)/shard_map/ppermute | solution.py:49
  32.0 1.6 %collective-permute-start.6 = (f32[4,32,128]{2,1,0:T(8,128)S(1)}, f32[4,32,128]{2,1,0:T(8,128)S(1)}, u32[]{:S(2)}, u32[]{:S(2)}) collective-permute-start(f32[4,32,128]{2,1,0:T(8,128)S(1)} %get-tuple-element.71), channel_id=1, source_target_pairs={{0,8},{2,10},{4,12},{6,14},{8,0},{10,2},{12,4},{14,6},{16,24},{18,... | collective-permute-start | bytes 196616 | tf_op jit(solution)/shard_map/ppermute | solution.py:49
  34.3 2.2 %collective-permute-done.6.first_ref = f32[4,32,128]{2,1,0:T(8,128)S(1)} collective-permute-done((f32[4,32,128]{2,1,0:T(8,128)S(1)}, f32[4,32,128]{2,1,0:T(8,128)S(1)}, u32[]{:S(2)}, u32[]{:S(2)}) %collective-permute-start.6) | collective-permute-done | bytes 65568 | tf_op jit(solution)/shard_map/ppermute | solution.py:49
  36.5 1.7 %shard_map.152 = (f32[32,16,128]{2,1,0:T(8,128)S(1)}, bf16[32,32,128]{2,1,0:T(8,128)(2,1)S(1)}, f32[4,32,128]{2,1,0:T(8,128)S(1)}, f32[4,32,128]{2,1,0:T(8,128)S(1)}) custom-call(s32[80]{0:T(128)S(1)} %copy-done.7, s32[80]{0:T(128)S(1)} %copy-done.9, s32[8,2]{1,0:T(8,128)S(1)} %copy.24.send_ref, s32[16]{0:T(128)S(1)} %copy-done.12, ...), custom_call_target="tpu_custom_call" | custom-call | flops 83886080 | bytes 2621440 | tf_op jit(solution)/shard_map/pallas_call | solution.py:73
  39.5 1.6 %collective-permute-start.9 = (f32[4,32,128]{2,1,0:T(8,128)S(1)}, f32[4,32,128]{2,1,0:T(8,128)S(1)}, u32[]{:S(2)}, u32[]{:S(2)}) collective-permute-start(f32[4,32,128]{2,1,0:T(8,128)S(1)} %pad_maximum_fusion.6), channel_id=1, source_target_pairs={{0,4},{2,6},{4,0},{6,2},{8,12},{10,14},{12,8},{14,10},{16,20},{18,... | collective-permute-start | bytes 196616 | tf_op jit(solution)/shard_map/ppermute | solution.py:49
  41.1 2.7 %collective-permute-done.9.side_ref = f32[4,32,128]{2,1,0:T(8,128)S(1)} collective-permute-done((f32[4,32,128]{2,1,0:T(8,128)S(1)}, f32[4,32,128]{2,1,0:T(8,128)S(1)}, u32[]{:S(2)}, u32[]{:S(2)}) %collective-permute-start.9) | collective-permute-done | bytes 65568 | tf_op jit(solution)/shard_map/ppermute | solution.py:49
  44.0 1.8 %collective-permute-start.10 = (f32[4,32,128]{2,1,0:T(8,128)S(1)}, f32[4,32,128]{2,1,0:T(8,128)S(1)}, u32[]{:S(2)}, u32[]{:S(2)}) collective-permute-start(f32[4,32,128]{2,1,0:T(8,128)S(1)} %get-tuple-element.69), channel_id=1, source_target_pairs={{0,8},{2,10},{4,12},{6,14},{8,0},{10,2},{12,4},{14,6},{16,24},{18,... | collective-permute-start | bytes 196616 | tf_op jit(solution)/shard_map/ppermute | solution.py:49
  46.4 2.1 %collective-permute-done.10.first_ref = f32[4,32,128]{2,1,0:T(8,128)S(1)} collective-permute-done((f32[4,32,128]{2,1,0:T(8,128)S(1)}, f32[4,32,128]{2,1,0:T(8,128)S(1)}, u32[]{:S(2)}, u32[]{:S(2)}) %collective-permute-start.10) | collective-permute-done | bytes 65568 | tf_op jit(solution)/shard_map/ppermute | solution.py:49
  48.5 2.8 %shard_map.154 = (f32[16,4096]{1,0:T(8,128)}, bf16[32,32,128]{2,1,0:T(8,128)(2,1)S(1)}, f32[32,16,128]{2,1,0:T(8,128)S(1)}, f32[4,32,128]{2,1,0:T(8,128)S(1)}, f32[4,32,128]{2,1,0:T(8,128)S(1)}) custom-call(s32[80]{0:T(128)S(1)} %copy-done.8, s32[80]{0:T(128)S(1)} %copy-done.10, s32[16]{0:T(128)S(1)} %copy-done.12, bf16[80,128,128]{2,1,0:T(8,128)(2,1)S(1)} %copy-done.2, ...), custom_call_target="tpu_custom_call" | custom-call | flops 167772160 | bytes 2621440 | tf_op jit(solution)/shard_map/pallas_call | solution.py:73
  52.5 1.6 %collective-permute-start.13 = (f32[4,32,128]{2,1,0:T(8,128)S(1)}, f32[4,32,128]{2,1,0:T(8,128)S(1)}, u32[]{:S(2)}, u32[]{:S(2)}) collective-permute-start(f32[4,32,128]{2,1,0:T(8,128)S(1)} %pad_maximum_fusion.9), channel_id=1, source_target_pairs={{0,4},{2,6},{4,0},{6,2},{8,12},{10,14},{12,8},{14,10},{16,20},{18,... | collective-permute-start | bytes 196616 | tf_op jit(solution)/shard_map/ppermute | solution.py:49
  54.1 2.7 %collective-permute-done.13.side_ref = f32[4,32,128]{2,1,0:T(8,128)S(1)} collective-permute-done((f32[4,32,128]{2,1,0:T(8,128)S(1)}, f32[4,32,128]{2,1,0:T(8,128)S(1)}, u32[]{:S(2)}, u32[]{:S(2)}) %collective-permute-start.13) | collective-permute-done | bytes 65568 | tf_op jit(solution)/shard_map/ppermute | solution.py:49
  56.9 3.2 %collective-permute-start.14 = (f32[4,32,128]{2,1,0:T(8,128)S(1)}, f32[4,32,128]{2,1,0:T(8,128)S(1)}, u32[]{:S(2)}, u32[]{:S(2)}) collective-permute-start(f32[4,32,128]{2,1,0:T(8,128)S(1)} %get-tuple-element.67), channel_id=1, source_target_pairs={{0,8},{2,10},{4,12},{6,14},{8,0},{10,2},{12,4},{14,6},{16,24},{18,... | collective-permute-start | bytes 196616 | tf_op jit(solution)/shard_map/ppermute | solution.py:49
  60.6 1.8 %collective-permute-done.14.first_ref = f32[4,32,128]{2,1,0:T(8,128)S(1)} collective-permute-done((f32[4,32,128]{2,1,0:T(8,128)S(1)}, f32[4,32,128]{2,1,0:T(8,128)S(1)}, u32[]{:S(2)}, u32[]{:S(2)}) %collective-permute-start.14) | collective-permute-done | bytes 65568 | tf_op jit(solution)/shard_map/ppermute | solution.py:49
  65.0 1.6 %collective-permute-start.17 = (f32[4,32,128]{2,1,0:T(8,128)S(1)}, f32[4,32,128]{2,1,0:T(8,128)S(1)}, u32[]{:S(2)}, u32[]{:S(2)}) collective-permute-start(f32[4,32,128]{2,1,0:T(8,128)S(1)} %pad_maximum_fusion.12), channel_id=1, source_target_pairs={{0,4},{2,6},{4,0},{6,2},{8,12},{10,14},{12,8},{14,10},{16,20},{18,... | collective-permute-start | bytes 196616 | tf_op jit(solution)/shard_map/ppermute | solution.py:49
  66.6 2.8 %collective-permute-done.17.side_ref = f32[4,32,128]{2,1,0:T(8,128)S(1)} collective-permute-done((f32[4,32,128]{2,1,0:T(8,128)S(1)}, f32[4,32,128]{2,1,0:T(8,128)S(1)}, u32[]{:S(2)}, u32[]{:S(2)}) %collective-permute-start.17) | collective-permute-done | bytes 65568 | tf_op jit(solution)/shard_map/ppermute | solution.py:49
  69.5 2.4 %collective-permute-start.18 = (f32[4,32,128]{2,1,0:T(8,128)S(1)}, f32[4,32,128]{2,1,0:T(8,128)S(1)}, u32[]{:S(2)}, u32[]{:S(2)}) collective-permute-start(f32[4,32,128]{2,1,0:T(8,128)S(1)} %get-tuple-element.65), channel_id=1, source_target_pairs={{0,8},{2,10},{4,12},{6,14},{8,0},{10,2},{12,4},{14,6},{16,24},{18,... | collective-permute-start | bytes 196616 | tf_op jit(solution)/shard_map/ppermute | solution.py:49
  72.2 1.8 %collective-permute-done.18.first_ref = f32[4,32,128]{2,1,0:T(8,128)S(1)} collective-permute-done((f32[4,32,128]{2,1,0:T(8,128)S(1)}, f32[4,32,128]{2,1,0:T(8,128)S(1)}, u32[]{:S(2)}, u32[]{:S(2)}) %collective-permute-start.18) | collective-permute-done | bytes 65568 | tf_op jit(solution)/shard_map/ppermute | solution.py:49
  76.7 1.6 %collective-permute-start.21 = (f32[4,8,128]{2,1,0:T(8,128)S(1)}, f32[4,8,128]{2,1,0:T(8,128)S(1)}, u32[]{:S(2)}, u32[]{:S(2)}) collective-permute-start(f32[4,8,128]{2,1,0:T(8,128)S(1)} %pad_maximum_fusion.15), channel_id=1, source_target_pairs={{0,4},{2,6},{4,0},{6,2},{8,12},{10,14},{12,8},{14,10},{16,20},{18,... | collective-permute-start | bytes 49160 | tf_op jit(solution)/shard_map/ppermute | solution.py:49
  78.2 2.2 %collective-permute-done.21.side_ref = f32[4,8,128]{2,1,0:T(8,128)S(1)} collective-permute-done((f32[4,8,128]{2,1,0:T(8,128)S(1)}, f32[4,8,128]{2,1,0:T(8,128)S(1)}, u32[]{:S(2)}, u32[]{:S(2)}) %collective-permute-start.21) | collective-permute-done | bytes 16416 | tf_op jit(solution)/shard_map/ppermute | solution.py:49
  80.6 3.7 %collective-permute-start.22 = (f32[4,8,128]{2,1,0:T(8,128)S(1)}, f32[4,8,128]{2,1,0:T(8,128)S(1)}, u32[]{:S(2)}, u32[]{:S(2)}) collective-permute-start(f32[4,8,128]{2,1,0:T(8,128)S(1)} %get-tuple-element.135), channel_id=1, source_target_pairs={{0,8},{2,10},{4,12},{6,14},{8,0},{10,2},{12,4},{14,6},{16,24},{18,... | collective-permute-start | bytes 49160 | tf_op jit(solution)/shard_map/ppermute | solution.py:49
  85.9 4.3 %shard_map.160 = f32[544,128]{1,0:T(8,128)S(1)} custom-call(s32[8,2]{1,0:T(8,128)S(1)} %copy.24.send_ref, f32[1,512]{1,0:T(1,128)S(1)} %bitcast.15, bf16[4096,128]{1,0:T(8,128)(2,1)S(1)} %copy-done.4, f32[512,4096]{1,0:T(8,128)S(1)} %get-tuple-element.44.act_ref, f32[32,1,128]{2,1,0:T(1,128)S(1)} %shard_map.159.node_ref, ...), custom_call_target="tpu_custom_call" | custom-call | flops 1073741824 | bytes 8388608 | tf_op jit(solution)/shard_map/pallas_call | solution.py:73
  90.2 14.7 %all_to_all.10 = f32[32,1,2176]{2,1,0:T(1,128)S(1)} all-to-all(f32[32,1,2176]{2,1,0:T(1,128)S(1)} %bitcast.13), channel_id=1, replica_groups=mesh['dom'=16,'dest'=2] {'dest','dom'}, dimensions={0} | all-to-all | bytes 557056 | tf_op jit(solution)/shard_map/all_to_all | solution.py:511
  105.2 12.9 %all_to_all.11 = f32[32,1,2176]{2,1,0:T(1,128)S(1)} all-to-all(f32[32,1,2176]{2,1,0:T(1,128)S(1)} %broadcast_in_dim.14), channel_id=1, replica_groups=mesh['dom'=16,'dest'=2] {'dest','dom'}, dimensions={0} | all-to-all | bytes 557056 | tf_op jit(solution)/shard_map/all_to_all | solution.py:513
  (103 shorter events, 23.8 us)
Async XLA Ops:
  0.6 35.9 %copy-start.12 = (s32[16]{0:T(128)S(1)}, s32[16]{0:T(128)}, u32[]{:S(2)}) copy-start(s32[16]{0:T(128)} %dest_ref.5) | copy-start | bytes 196
  3.0 1.5 %collective-permute-start = (f32[4,32,128]{2,1,0:T(8,128)S(1)}, f32[4,32,128]{2,1,0:T(8,128)S(1)}, u32[]{:S(2)}, u32[]{:S(2)}) collective-permute-start(f32[4,32,128]{2,1,0:T(8,128)S(1)} %get-tuple-element.35), channel_id=1, source_target_pairs={{0,2},{2,0},{4,6},{6,4},{8,10},{10,8},{12,14},{14,12},{16,18},{18,... | collective-permute-start | bytes 196616 | tf_op jit(solution)/shard_map/ppermute | solution.py:49
  4.5 5.3 %collective-permute-start.1 = (f32[4,32,128]{2,1,0:T(8,128)S(1)}, f32[4,32,128]{2,1,0:T(8,128)S(1)}, u32[]{:S(2)}, u32[]{:S(2)}) collective-permute-start(f32[4,32,128]{2,1,0:T(8,128)S(1)} %pad_maximum_fusion), channel_id=1, source_target_pairs={{0,4},{2,6},{4,0},{6,2},{8,12},{10,14},{12,8},{14,10},{16,20},{18,... | collective-permute-start | bytes 196616 | tf_op jit(solution)/shard_map/ppermute | solution.py:49
  9.9 11.0 %collective-permute-start.3 = (f32[4,32,128]{2,1,0:T(8,128)S(1)}, f32[4,32,128]{2,1,0:T(8,128)S(1)}, u32[]{:S(2)}, u32[]{:S(2)}) collective-permute-start(f32[4,32,128]{2,1,0:T(8,128)S(1)} %get-tuple-element.72), channel_id=1, source_target_pairs={{0,2},{2,0},{4,6},{6,4},{8,16},{10,18},{12,20},{14,22},{16,8},{18,... | collective-permute-start | bytes 196616 | tf_op jit(solution)/shard_map/ppermute | solution.py:65
  9.9 10.9 %collective-permute-start.2 = (f32[4,32,128]{2,1,0:T(8,128)S(1)}, f32[4,32,128]{2,1,0:T(8,128)S(1)}, u32[]{:S(2)}, u32[]{:S(2)}) collective-permute-start(f32[4,32,128]{2,1,0:T(8,128)S(1)} %get-tuple-element.73), channel_id=1, source_target_pairs={{0,8},{2,10},{4,12},{6,14},{8,0},{10,2},{12,4},{14,6},{16,24},{18,... | collective-permute-start | bytes 196616 | tf_op jit(solution)/shard_map/ppermute | solution.py:49
  15.2 18.5 %copy-start.2 = (bf16[80,128,128]{2,1,0:T(8,128)(2,1)S(1)}, bf16[80,128,128]{2,1,0:T(8,128)(2,1)}, u32[]{:S(2)}) copy-start(bf16[80,128,128]{2,1,0:T(8,128)(2,1)} %w_ref.23) | copy-start | bytes 7864324
  19.4 29.0 %copy-start.5 = (s32[16,4096]{1,0:T(8,128)S(1)}, s32[16,4096]{1,0:T(8,128)}, u32[]{:S(2)}) copy-start(s32[16,4096]{1,0:T(8,128)} %start_ref.1) | copy-start | bytes 786436
  19.4 29.0 %copy-start.8 = (s32[80]{0:T(128)S(1)}, s32[80]{0:T(128)}, u32[]{:S(2)}) copy-start(s32[80]{0:T(128)} %rows_ref.9) | copy-start | bytes 964
  19.4 29.0 %copy-start.10 = (s32[80]{0:T(128)S(1)}, s32[80]{0:T(128)}, u32[]{:S(2)}) copy-start(s32[80]{0:T(128)} %cols_ref.9) | copy-start | bytes 964
  26.3 1.3 %collective-permute-start.4 = (f32[4,32,128]{2,1,0:T(8,128)S(1)}, f32[4,32,128]{2,1,0:T(8,128)S(1)}, u32[]{:S(2)}, u32[]{:S(2)}) collective-permute-start(f32[4,32,128]{2,1,0:T(8,128)S(1)} %get-tuple-element.38), channel_id=1, source_target_pairs={{0,2},{2,0},{4,6},{6,4},{8,10},{10,8},{12,14},{14,12},{16,18},{18,... | collective-permute-start | bytes 196616 | tf_op jit(solution)/shard_map/ppermute | solution.py:49
  27.6 4.3 %collective-permute-start.5 = (f32[4,32,128]{2,1,0:T(8,128)S(1)}, f32[4,32,128]{2,1,0:T(8,128)S(1)}, u32[]{:S(2)}, u32[]{:S(2)}) collective-permute-start(f32[4,32,128]{2,1,0:T(8,128)S(1)} %pad_maximum_fusion.3), channel_id=1, source_target_pairs={{0,4},{2,6},{4,0},{6,2},{8,12},{10,14},{12,8},{14,10},{16,20},{18,... | collective-permute-start | bytes 196616 | tf_op jit(solution)/shard_map/ppermute | solution.py:49
  32.0 2.4 %collective-permute-start.7 = (f32[4,32,128]{2,1,0:T(8,128)S(1)}, f32[4,32,128]{2,1,0:T(8,128)S(1)}, u32[]{:S(2)}, u32[]{:S(2)}) collective-permute-start(f32[4,32,128]{2,1,0:T(8,128)S(1)} %get-tuple-element.70), channel_id=1, source_target_pairs={{0,2},{2,0},{4,6},{6,4},{8,16},{10,18},{12,20},{14,22},{16,8},{18,... | collective-permute-start | bytes 196616 | tf_op jit(solution)/shard_map/ppermute | solution.py:65
  32.0 4.5 %collective-permute-start.6 = (f32[4,32,128]{2,1,0:T(8,128)S(1)}, f32[4,32,128]{2,1,0:T(8,128)S(1)}, u32[]{:S(2)}, u32[]{:S(2)}) collective-permute-start(f32[4,32,128]{2,1,0:T(8,128)S(1)} %get-tuple-element.71), channel_id=1, source_target_pairs={{0,8},{2,10},{4,12},{6,14},{8,0},{10,2},{12,4},{14,6},{16,24},{18,... | collective-permute-start | bytes 196616 | tf_op jit(solution)/shard_map/ppermute | solution.py:49
  38.2 1.3 %collective-permute-start.8 = (f32[4,32,128]{2,1,0:T(8,128)S(1)}, f32[4,32,128]{2,1,0:T(8,128)S(1)}, u32[]{:S(2)}, u32[]{:S(2)}) collective-permute-start(f32[4,32,128]{2,1,0:T(8,128)S(1)} %get-tuple-element.41), channel_id=1, source_target_pairs={{0,2},{2,0},{4,6},{6,4},{8,10},{10,8},{12,14},{14,12},{16,18},{18,... | collective-permute-start | bytes 196616 | tf_op jit(solution)/shard_map/ppermute | solution.py:49
  39.5 4.3 %collective-permute-start.9 = (f32[4,32,128]{2,1,0:T(8,128)S(1)}, f32[4,32,128]{2,1,0:T(8,128)S(1)}, u32[]{:S(2)}, u32[]{:S(2)}) collective-permute-start(f32[4,32,128]{2,1,0:T(8,128)S(1)} %pad_maximum_fusion.6), channel_id=1, source_target_pairs={{0,4},{2,6},{4,0},{6,2},{8,12},{10,14},{12,8},{14,10},{16,20},{18,... | collective-permute-start | bytes 196616 | tf_op jit(solution)/shard_map/ppermute | solution.py:49
  43.9 2.5 %collective-permute-start.11 = (f32[4,32,128]{2,1,0:T(8,128)S(1)}, f32[4,32,128]{2,1,0:T(8,128)S(1)}, u32[]{:S(2)}, u32[]{:S(2)}) collective-permute-start(f32[4,32,128]{2,1,0:T(8,128)S(1)} %get-tuple-element.68), channel_id=1, source_target_pairs={{0,2},{2,0},{4,6},{6,4},{8,16},{10,18},{12,20},{14,22},{16,8},{18,... | collective-permute-start | bytes 196616 | tf_op jit(solution)/shard_map/ppermute | solution.py:65
  44.0 4.5 %collective-permute-start.10 = (f32[4,32,128]{2,1,0:T(8,128)S(1)}, f32[4,32,128]{2,1,0:T(8,128)S(1)}, u32[]{:S(2)}, u32[]{:S(2)}) collective-permute-start(f32[4,32,128]{2,1,0:T(8,128)S(1)} %get-tuple-element.69), channel_id=1, source_target_pairs={{0,8},{2,10},{4,12},{6,14},{8,0},{10,2},{12,4},{14,6},{16,24},{18,... | collective-permute-start | bytes 196616 | tf_op jit(solution)/shard_map/ppermute | solution.py:49
  51.2 33.0 %copy-start.6 = (s32[16,4096]{1,0:T(8,128)S(1)}, s32[16,4096]{1,0:T(8,128)}, u32[]{:S(2)}) copy-start(s32[16,4096]{1,0:T(8,128)} %visit_ref.1) | copy-start | bytes 786436
  51.2 1.3 %collective-permute-start.12 = (f32[4,32,128]{2,1,0:T(8,128)S(1)}, f32[4,32,128]{2,1,0:T(8,128)S(1)}, u32[]{:S(2)}, u32[]{:S(2)}) collective-permute-start(f32[4,32,128]{2,1,0:T(8,128)S(1)} %get-tuple-element.47), channel_id=1, source_target_pairs={{0,2},{2,0},{4,6},{6,4},{8,10},{10,8},{12,14},{14,12},{16,18},{18,... | collective-permute-start | bytes 196616 | tf_op jit(solution)/shard_map/ppermute | solution.py:49
  52.5 4.3 %collective-permute-start.13 = (f32[4,32,128]{2,1,0:T(8,128)S(1)}, f32[4,32,128]{2,1,0:T(8,128)S(1)}, u32[]{:S(2)}, u32[]{:S(2)}) collective-permute-start(f32[4,32,128]{2,1,0:T(8,128)S(1)} %pad_maximum_fusion.9), channel_id=1, source_target_pairs={{0,4},{2,6},{4,0},{6,2},{8,12},{10,14},{12,8},{14,10},{16,20},{18,... | collective-permute-start | bytes 196616 | tf_op jit(solution)/shard_map/ppermute | solution.py:49
  56.9 3.7 %collective-permute-start.15 = (f32[4,32,128]{2,1,0:T(8,128)S(1)}, f32[4,32,128]{2,1,0:T(8,128)S(1)}, u32[]{:S(2)}, u32[]{:S(2)}) collective-permute-start(f32[4,32,128]{2,1,0:T(8,128)S(1)} %get-tuple-element.66), channel_id=1, source_target_pairs={{0,2},{2,0},{4,6},{6,4},{8,16},{10,18},{12,20},{14,22},{16,8},{18,... | collective-permute-start | bytes 196616 | tf_op jit(solution)/shard_map/ppermute | solution.py:65
  56.9 5.4 %collective-permute-start.14 = (f32[4,32,128]{2,1,0:T(8,128)S(1)}, f32[4,32,128]{2,1,0:T(8,128)S(1)}, u32[]{:S(2)}, u32[]{:S(2)}) collective-permute-start(f32[4,32,128]{2,1,0:T(8,128)S(1)} %get-tuple-element.67), channel_id=1, source_target_pairs={{0,8},{2,10},{4,12},{6,14},{8,0},{10,2},{12,4},{14,6},{16,24},{18,... | collective-permute-start | bytes 196616 | tf_op jit(solution)/shard_map/ppermute | solution.py:49
  60.5 25.4 %copy-start.4 = (bf16[4096,128]{1,0:T(8,128)(2,1)S(1)}, bf16[4096,128]{1,0:T(8,128)(2,1)}, u32[]{:S(2)}) copy-start(bf16[4096,128]{1,0:T(8,128)(2,1)} %f_ref.3) | copy-start | bytes 3145732
  60.5 25.4 %copy-start.14 = (f32[512]{0:T(512)S(1)}, f32[512]{0:T(512)}, u32[]{:S(2)}) copy-start(f32[512]{0:T(512)} %param.15) | copy-start | bytes 6148
  63.7 1.3 %collective-permute-start.16 = (f32[4,32,128]{2,1,0:T(8,128)S(1)}, f32[4,32,128]{2,1,0:T(8,128)S(1)}, u32[]{:S(2)}, u32[]{:S(2)}) collective-permute-start(f32[4,32,128]{2,1,0:T(8,128)S(1)} %get-tuple-element.51), channel_id=1, source_target_pairs={{0,2},{2,0},{4,6},{6,4},{8,10},{10,8},{12,14},{14,12},{16,18},{18,... | collective-permute-start | bytes 196616 | tf_op jit(solution)/shard_map/ppermute | solution.py:49
  65.0 4.3 %collective-permute-start.17 = (f32[4,32,128]{2,1,0:T(8,128)S(1)}, f32[4,32,128]{2,1,0:T(8,128)S(1)}, u32[]{:S(2)}, u32[]{:S(2)}) collective-permute-start(f32[4,32,128]{2,1,0:T(8,128)S(1)} %pad_maximum_fusion.12), channel_id=1, source_target_pairs={{0,4},{2,6},{4,0},{6,2},{8,12},{10,14},{12,8},{14,10},{16,20},{18,... | collective-permute-start | bytes 196616 | tf_op jit(solution)/shard_map/ppermute | solution.py:49
  69.4 2.8 %collective-permute-start.19 = (f32[4,32,128]{2,1,0:T(8,128)S(1)}, f32[4,32,128]{2,1,0:T(8,128)S(1)}, u32[]{:S(2)}, u32[]{:S(2)}) collective-permute-start(f32[4,32,128]{2,1,0:T(8,128)S(1)} %get-tuple-element.64), channel_id=1, source_target_pairs={{0,2},{2,0},{4,6},{6,4},{8,16},{10,18},{12,20},{14,22},{16,8},{18,... | collective-permute-start | bytes 196616 | tf_op jit(solution)/shard_map/ppermute | solution.py:65
  69.5 4.6 %collective-permute-start.18 = (f32[4,32,128]{2,1,0:T(8,128)S(1)}, f32[4,32,128]{2,1,0:T(8,128)S(1)}, u32[]{:S(2)}, u32[]{:S(2)}) collective-permute-start(f32[4,32,128]{2,1,0:T(8,128)S(1)} %get-tuple-element.65), channel_id=1, source_target_pairs={{0,8},{2,10},{4,12},{6,14},{8,0},{10,2},{12,4},{14,6},{16,24},{18,... | collective-permute-start | bytes 196616 | tf_op jit(solution)/shard_map/ppermute | solution.py:49
  75.4 1.2 %collective-permute-start.20 = (f32[4,8,128]{2,1,0:T(8,128)S(1)}, f32[4,8,128]{2,1,0:T(8,128)S(1)}, u32[]{:S(2)}, u32[]{:S(2)}) collective-permute-start(f32[4,8,128]{2,1,0:T(8,128)S(1)} %get-tuple-element.60), channel_id=1, source_target_pairs={{0,2},{2,0},{4,6},{6,4},{8,10},{10,8},{12,14},{14,12},{16,18},{18,... | collective-permute-start | bytes 49160 | tf_op jit(solution)/shard_map/ppermute | solution.py:49
  76.7 3.8 %collective-permute-start.21 = (f32[4,8,128]{2,1,0:T(8,128)S(1)}, f32[4,8,128]{2,1,0:T(8,128)S(1)}, u32[]{:S(2)}, u32[]{:S(2)}) collective-permute-start(f32[4,8,128]{2,1,0:T(8,128)S(1)} %pad_maximum_fusion.15), channel_id=1, source_target_pairs={{0,4},{2,6},{4,0},{6,2},{8,12},{10,14},{12,8},{14,10},{16,20},{18,... | collective-permute-start | bytes 49160 | tf_op jit(solution)/shard_map/ppermute | solution.py:49
  80.5 4.2 %collective-permute-start.23 = (f32[4,8,128]{2,1,0:T(8,128)S(1)}, f32[4,8,128]{2,1,0:T(8,128)S(1)}, u32[]{:S(2)}, u32[]{:S(2)}) collective-permute-start(f32[4,8,128]{2,1,0:T(8,128)S(1)} %get-tuple-element.134), channel_id=1, source_target_pairs={{0,2},{2,0},{4,6},{6,4},{8,16},{10,18},{12,20},{14,22},{16,8},{18,... | collective-permute-start | bytes 49160 | tf_op jit(solution)/shard_map/ppermute | solution.py:65
  80.6 5.4 %collective-permute-start.22 = (f32[4,8,128]{2,1,0:T(8,128)S(1)}, f32[4,8,128]{2,1,0:T(8,128)S(1)}, u32[]{:S(2)}, u32[]{:S(2)}) collective-permute-start(f32[4,8,128]{2,1,0:T(8,128)S(1)} %get-tuple-element.135), channel_id=1, source_target_pairs={{0,8},{2,10},{4,12},{6,14},{8,0},{10,2},{12,4},{14,6},{16,24},{18,... | collective-permute-start | bytes 49160 | tf_op jit(solution)/shard_map/ppermute | solution.py:49
  (10 other events, 10.0 us)

commit v2 on v1

v2 whole, which is shorter than its diff:
```python
import functools
import math

import jax
import jax.numpy as jnp
from jax import lax
from jax.experimental import pallas as pl
from jax.experimental.pallas import tpu as pltpu
from jax.sharding import PartitionSpec as P

STEPS = 3
GOAL_GAIN = 32.0
VMEM_GRANT = 20 << 20

HOLD = lambda x: pltpu.with_memory_space_constraint(x, pltpu.HBM)
NT = (((1,), (1,)), ((), ()))
NN = (((1,), (0,)), ((), ()))


def offset_of(o, reach):
    return o - reach if o < reach else o - reach + 1


def present(me, count, shift):
    there = me + shift
    return jnp.logical_and(there >= 0, there < count)


def place(me, shift):
    origin = me - shift
    k = jnp.bitwise_xor(origin, me) & 3
    core, side, odd = me & 1, (me >> 1) & 1, (me >> 2) & 1
    apart = (origin >> 2) - (me >> 2)
    here = jnp.where(k == 1, 1 + core, jnp.where(k == 2, 5 - side, 7 - side))
    below = jnp.where(odd == 1, 8, 12) + k
    above = jnp.where(odd == 1, 12, 8) + k
    return jnp.where(apart == 0, here, jnp.where(apart < 0, below, above))


def exchange(odd, even, work=None):
    me = lax.axis_index("dom")
    devices = range(lax.axis_size("dom"))
    core_zero = me % 2 == 0
    group_even = (me // 4) % 2 == 0

    def partner(i, flip):
        j = (i // 4 + (1 if (i // 4) % 2 == 1 else -1)) * 4 + i % 4
        return j if j in devices else i ^ 1

    flip = lambda x, bit: lax.ppermute(x, "dom", [(i, i ^ bit) for i in devices])
    near = flip(odd, 1)
    side = flip(
        jnp.stack(
            [
                even[2],
                even[1],
                jnp.where(core_zero, near[2], near[3]),
                jnp.where(core_zero, near[0], near[1]),
            ]
        ),
        2,
    )
    done = None
    if work is not None:
        side, done = lax.optimization_barrier((side, work(near)))
    up = jnp.stack([even[3], near[3], side[0], side[2]])
    down = jnp.stack([even[0], near[0], side[1], side[3]])
    first = flip(jnp.where(group_even, up, down), 4)
    second = lax.ppermute(
        jnp.where(group_even, down, up), "dom", [(i, partner(i, 1)) for i in devices]
    )
    return (near, side, first, second), done


def call(kernel, out_shape, scratch, smem, vmem, flops, moved, hbm=(), smem_out=False, after=()):
    space = lambda kind: pl.BlockSpec(memory_space=kind)
    out_specs = jax.tree.map(lambda _: space(pltpu.VMEM), out_shape)
    if smem_out:
        out_specs = (space(pltpu.SMEM), *out_specs[1:])
    if after:
        inner, lead, span = kernel, len(hbm) + len(smem) + len(vmem), len(after)
        kernel = lambda *refs: inner(*refs[:lead], *refs[lead + span :])
    hbm = [HOLD(x) for x in hbm]
    return pl.pallas_call(
        kernel,
        out_shape=out_shape,
        in_specs=[space(pltpu.HBM)] * len(hbm)
        + [space(pltpu.SMEM)] * len(smem)
        + [space(pltpu.VMEM)] * len(vmem)
        + [space(pl.ANY)] * len(after),
        out_specs=out_specs,
        scratch_shapes=scratch,
        compiler_params=pltpu.CompilerParams(vmem_limit_bytes=VMEM_GRANT),
        cost_estimate=pl.CostEstimate(flops=flops, bytes_accessed=moved, transcendentals=0),
    )(*hbm, *smem, *vmem, *after)


def store_split(ref, k, x):
    rows = x.shape[0]
    high = x.astype(jnp.bfloat16)
    low = (x - high.astype(jnp.float32)).astype(jnp.bfloat16)
    ref[k, :rows] = high
    ref[k, rows:] = low


def product(lhs, rhs, dims):
    both = lax.dot_general(lhs, rhs, dims, preferred_element_type=jnp.float32)
    rows = both.shape[0] // 2
    return both[:rows] + both[rows:]


def offsets(reach):
    return [offset_of(o, reach) for o in range(2 * reach)]


def send_items(odd_ref, even_ref, reach, width, sign, item):
    ways = offsets(reach)
    odds = [f for f in ways if f % 2]
    evens = [f for f in ways if f % 2 == 0]
    for o, f in enumerate(ways):
        shift = sign * f
        ref, at = (odd_ref, odds.index(shift)) if shift % 2 else (even_ref, evens.index(shift))
        for m in range(width):
            piece = item(o, m)
            rows = piece.shape[0]
            ref[at, m * rows : (m + 1) * rows] = piece


def collect(all_ref, parts):
    at = 0
    for part in parts:
        for k in range(part.shape[0]):
            all_ref[at] = part[k]
            at += 1


class Plan:
    def __init__(self, blocks, tiles, slots, rows):
        at = 0
        for name, size in (
            ("far_t", slots), ("far_r", slots), ("far_c", slots),
            ("near_t", tiles - blocks), ("near_r", tiles - blocks), ("near_c", tiles - blocks),
            ("send", slots), ("dest", rows), ("near", 1), ("far", 1),
        ):
            setattr(self, name, at)
            at += size
        self.size = at
        self.blocks, self.slots, self.extra = blocks, slots, tiles - blocks


def load_kernel(
    plan, rows_hbm, cols_hbm, send_hbm, dest_hbm, tile_hbm, f_hbm, w_hbm, b_hbm, v_hbm,
    plan_ref, tile_ref, f_ref, w_ref, b_ref, v_ref, rows_ref, cols_ref, send_ref, dest_ref, sem, small,
):
    smalls = [
        pltpu.make_async_copy(src, dst, small.at[k])
        for k, (src, dst) in enumerate(
            ((rows_hbm, rows_ref), (cols_hbm, cols_ref), (send_hbm, send_ref), (dest_hbm, dest_ref))
        )
    ]
    larges = [
        pltpu.make_async_copy(src, dst, sem.at[k])
        for k, (src, dst) in enumerate(
            ((f_hbm, f_ref), (w_hbm, w_ref), (b_hbm, b_ref), (v_hbm, v_ref), (tile_hbm, tile_ref))
        )
    ]
    for copy in smalls + larges:
        copy.start()
    for copy in smalls:
        copy.wait()
    for k in range(plan.size):
        plan_ref[k] = 0
    width = send_ref.shape[0]
    for k in range(plan.slots):
        plan_ref[plan.far_c + k] = plan.blocks
        plan_ref[plan.send + k] = send_ref[k % width, k // width]
    for k in range(dest_ref.shape[0]):
        plan_ref[plan.dest + k] = dest_ref[k]

    def sort_tile(k, counts):
        near, far = counts
        t = plan.blocks + k
        r, c = rows_ref[t], cols_ref[t]
        apart = c >= plan.blocks
        at = jnp.where(apart, plan.far_t + far, plan.near_t + near)
        step = jnp.where(apart, plan.slots, plan.extra)
        plan_ref[at] = t
        plan_ref[at + step] = r
        plan_ref[at + 2 * step] = c
        one = apart.astype(jnp.int32)
        return near + 1 - one, far + one

    near, far = lax.fori_loop(0, plan.extra, sort_tile, (jnp.int32(0), jnp.int32(0)))
    plan_ref[plan.near] = near
    plan_ref[plan.far] = far
    for copy in larges:
        copy.wait()


def network_kernel(w_ref, b_ref, v_ref, f_ref, act_ref, growth_ref):
    lanes = growth_ref.shape[2]
    hidden = act_ref.shape[0]
    group = 2
    w = w_ref[...].T
    b = jnp.broadcast_to(b_ref[...], (lanes, hidden)).T
    v = jnp.broadcast_to(v_ref[...], (lanes, hidden)).T
    for c in range(growth_ref.shape[0] // group):
        f = f_ref[c * group * lanes : (c + 1) * group * lanes]
        pre = lax.dot_general(w, f, NT, preferred_element_type=jnp.float32)
        for k in range(group):
            at = c * group + k
            act = jnp.tanh(pre[:, k * lanes : (k + 1) * lanes] + b)
            act_ref[:, at * lanes : (at + 1) * lanes] = act
            growth_ref[at] = jnp.exp(jnp.sum(act * v, axis=0, keepdims=True))


def first_kernel(
    reach, width, send_hbm, term_hbm, z_ref, split_ref, odd_ref, even_ref, send_ref, term_ref, sem, small
):
    blocks, _, lanes = z_ref.shape
    parts = sem.shape[0]
    span = blocks // parts
    asked = pltpu.make_async_copy(send_hbm, send_ref, small)
    cut = lambda ref, i: ref.at[:, i * span * lanes : (i + 1) * span * lanes]
    copies = [
        pltpu.make_async_copy(cut(term_hbm, i), cut(term_ref, i), sem.at[i]) for i in range(parts)
    ]
    asked.start()
    for copy in copies:
        copy.start()
    for i, copy in enumerate(copies):
        copy.wait()
        for k in range(i * span, (i + 1) * span):
            z = jnp.exp(term_ref[:, k * lanes : (k + 1) * lanes])
            z_ref[k] = z
            store_split(split_ref, k, z)
    asked.wait()
    send_items(odd_ref, even_ref, reach, width, 1, lambda o, m: z_ref[send_ref[m, o]])


def near_products(plan, plan_ref, w_ref, split_ref, sum_ref, forward):
    dims = NT if forward else NN
    for k in range(plan.blocks):
        sum_ref[k] = product(split_ref[k], w_ref[k], dims)
    count = plan_ref[plan.near]
    for k in range(plan.extra):
        r, c = plan_ref[plan.near_r + k], plan_ref[plan.near_c + k]
        source, into = (c, r) if forward else (r, c)
        into = jnp.where(k < count, into, plan.blocks)
        sum_ref[into] = sum_ref[into] + product(
            split_ref[source], w_ref[plan_ref[plan.near_t + k]], dims
        )


def near_kernel(plan, forward, plan_ref, w_ref, split_ref, sum_ref):
    near_products(plan, plan_ref, w_ref, split_ref, sum_ref, forward)


def backed_up(
    plan, reach, width, plan_ref, w_ref, part_ref, parts, all_ref, ext_ref, sum_ref
):
    rows = part_ref.shape[1]
    me = lax.axis_index("dom")
    collect(all_ref, parts)
    for o, f in enumerate(offsets(reach)):
        at = place(me, f)
        for m in range(width):
            store_split(ext_ref, o * width + m, all_ref[at, m * rows : (m + 1) * rows])
    for k in range(plan.blocks):
        sum_ref[k] = part_ref[k]
    count = plan_ref[plan.far]
    for k in range(plan.slots):
        slot = plan_ref[plan.far_c + k] - plan.blocks
        into = jnp.where(k < count, plan_ref[plan.far_r + k], plan.blocks)
        sum_ref[into] = sum_ref[into] + product(
            ext_ref[slot], w_ref[plan_ref[plan.far_t + k]], NT
        )


def goal_of(plan, plan_ref, rows, lanes):
    row = lax.broadcasted_iota(jnp.int32, (rows, lanes), 0)
    dest = jnp.zeros((rows, lanes), jnp.int32)
    for d in range(rows):
        dest = jnp.where(row == d, plan_ref[plan.dest + d], dest)
    return dest


def with_goal(k, blocks, growth_ref, sum_ref, dest, me):
    _, rows, lanes = sum_ref.shape
    node = (me * blocks + k) * lanes + lax.broadcasted_iota(jnp.int32, (rows, lanes), 1)
    return growth_ref[k] * sum_ref[k] + jnp.where(node == dest, GOAL_GAIN, 0.0)


def backup_kernel(
    plan, reach, width, plan_ref, w_ref, part_ref, growth_ref,
    near_ref, side_ref, first_ref, second_ref,
    z_ref, next_ref, odd_ref, even_ref, all_ref, ext_ref, sum_ref,
):
    blocks, rows, lanes = z_ref.shape
    me = lax.axis_index("dom")
    backed_up(
        plan, reach, width, plan_ref, w_ref, part_ref,
        (near_ref, side_ref, first_ref, second_ref), all_ref, ext_ref, sum_ref,
    )
    dest = goal_of(plan, plan_ref, rows, lanes)
    for k in range(blocks):
        z = with_goal(k, blocks, growth_ref, sum_ref, dest, me)
        z_ref[k] = z
        store_split(next_ref, k, z)
    send_items(
        odd_ref, even_ref, reach, width, 1,
        lambda o, m: z_ref[plan_ref[plan.send + o * width + m]],
    )


def far_flows(plan, plan_ref, w_ref, split_ref, flow_ref):
    for k in range(plan.slots + 1):
        flow_ref[k] = jnp.zeros(flow_ref.shape[1:], jnp.float32)
    count = plan_ref[plan.far]
    for k in range(plan.slots):
        slot = plan_ref[plan.far_c + k] - plan.blocks
        into = jnp.where(k < count, slot, plan.slots)
        flow_ref[into] = flow_ref[into] + product(
            split_ref[plan_ref[plan.far_r + k]], w_ref[plan_ref[plan.far_t + k]], NN
        )


def turn_kernel(
    plan, reach, width, plan_ref, w_ref, part_ref, growth_ref,
    near_ref, side_ref, first_ref, second_ref, start_ref,
    values_ref, next_ref, odd_ref, even_ref, all_ref, ext_ref, sum_ref, flow_ref,
):
    blocks = plan.blocks
    _, rows, lanes = part_ref.shape
    me = lax.axis_index("dom")
    backed_up(
        plan, reach, width, plan_ref, w_ref, part_ref,
        (near_ref, side_ref, first_ref, second_ref), all_ref, ext_ref, sum_ref,
    )
    dest = goal_of(plan, plan_ref, rows, lanes)
    for k in range(blocks):
        z = with_goal(k, blocks, growth_ref, sum_ref, dest, me)
        span = slice(k * lanes, (k + 1) * lanes)
        values_ref[:, span] = jnp.log(z)
        store_split(next_ref, k, growth_ref[k] * start_ref[:, span].astype(jnp.float32) / z)
    far_flows(plan, plan_ref, w_ref, next_ref, flow_ref)
    send_items(odd_ref, even_ref, reach, width, -1, lambda o, m: flow_ref[o * width + m])


def flows(
    plan, count, reach, width, plan_ref, w_ref, growth_ref, sum_ref, parts,
    u_ref, next_ref, all_ref, flow_ref,
):
    blocks, rows, _ = u_ref.shape
    me = lax.axis_index("dom")
    for k in range(blocks):
        u_ref[k] = sum_ref[k]
    collect(all_ref, parts)
    for o, f in enumerate(offsets(reach)):
        there = present(me, count, f)
        at = place(me, -f)
        for m in range(width):
            b = plan_ref[plan.send + o * width + m]
            piece = all_ref[at, m * rows : (m + 1) * rows]
            u_ref[b] = u_ref[b] + jnp.where(there, piece, 0.0)
    for k in range(blocks):
        store_split(next_ref, k, growth_ref[k] * u_ref[k])
    far_flows(plan, plan_ref, w_ref, next_ref, flow_ref)


def spread_kernel(
    plan, count, reach, width, plan_ref, w_ref, growth_ref, sum_ref,
    near_ref, side_ref, first_ref, second_ref,
    u_ref, next_ref, odd_ref, even_ref, all_ref, flow_ref,
):
    flows(
        plan, count, reach, width, plan_ref, w_ref, growth_ref, sum_ref,
        (near_ref, side_ref, first_ref, second_ref), u_ref, next_ref, all_ref, flow_ref,
    )
    send_items(odd_ref, even_ref, reach, width, -1, lambda o, m: flow_ref[o * width + m])


def last_kernel(
    plan, count, reach, width, plan_ref, w_ref, growth_ref, sum_ref,
    near_ref, side_ref, first_ref, second_ref, z_near_ref, z_side_ref, z_first_ref, z_second_ref,
    u_ref, next_ref, odd_ref, even_ref, all_ref, flow_ref, far_ref,
):
    rows = u_ref.shape[1]
    me = lax.axis_index("dom")
    flows(
        plan, count, reach, width, plan_ref, w_ref, growth_ref, sum_ref,
        (near_ref, side_ref, first_ref, second_ref), u_ref, next_ref, all_ref, flow_ref,
    )
    collect(far_ref, (z_near_ref, z_side_ref, z_first_ref, z_second_ref))
    ways = offsets(reach)
    odds = [f for f in ways if f % 2]
    evens = [f for f in ways if f % 2 == 0]
    row = lax.broadcasted_iota(jnp.int32, odd_ref.shape[1:], 0)
    for o, f in enumerate(ways):
        at = place(me, f)
        item = jnp.zeros(odd_ref.shape[1:], jnp.float32)
        for m in range(width):
            lost = far_ref[at, m * rows : (m + 1) * rows] * flow_ref[o * width + m]
            item = jnp.where(row == m, jnp.sum(lost, axis=0, keepdims=True), item)
        if f % 2:
            odd_ref[odds.index(-f)] = item
        else:
            even_ref[evens.index(-f)] = item


def node_kernel(
    plan, plan_ref, w_ref, split_ref, z0_ref, z1_ref, z2_ref, u1_ref, u2_ref, visit_ref,
    node_ref, sum_ref,
):
    blocks, _, lanes = z0_ref.shape
    near_products(plan, plan_ref, w_ref, split_ref, sum_ref, False)
    for k in range(blocks):
        left = (
            visit_ref[:, k * lanes : (k + 1) * lanes].astype(jnp.float32)
            - z2_ref[k] * u1_ref[k]
            - z1_ref[k] * u2_ref[k]
            - z0_ref[k] * sum_ref[k]
        )
        node_ref[k] = jnp.sum(left, axis=0, keepdims=True)


def gradient_kernel(
    plan, count, reach, width, scale, plan_ref, v_ref, f_ref, act_ref, node_ref,
    near_ref, side_ref, first_ref, second_ref, grad_ref, total_ref, all_ref,
):
    blocks, _, lanes = node_ref.shape
    me = lax.axis_index("dom")
    collect(all_ref, (near_ref, side_ref, first_ref, second_ref))
    for k in range(blocks):
        total_ref[k] = node_ref[k]
    for o, f in enumerate(offsets(reach)):
        there = present(me, count, f)
        at = place(me, -f)
        for m in range(width):
            b = plan_ref[plan.send + o * width + m]
            total_ref[b] = total_ref[b] - jnp.where(there, all_ref[at, m : m + 1], 0.0)
    hidden = act_ref.shape[0]
    out_sum = jnp.zeros((hidden, lanes), jnp.float32)
    bias_sum = jnp.zeros((hidden, lanes), jnp.float32)
    grad = jnp.zeros((hidden, f_ref.shape[1]), jnp.float32)
    group = 4
    for c in range(blocks // group):
        highs = []
        lows = []
        for k in range(c * group, (c + 1) * group):
            act = act_ref[:, k * lanes : (k + 1) * lanes]
            node = total_ref[k] * scale
            weighted = act * node
            pre = node - weighted * act
            out_sum = out_sum + weighted
            bias_sum = bias_sum + pre
            high = pre.astype(jnp.bfloat16)
            highs.append(high)
            lows.append((pre - high.astype(jnp.float32)).astype(jnp.bfloat16))
        f = f_ref[c * group * lanes : (c + 1) * group * lanes]
        grad = grad + lax.dot_general(
            jnp.concatenate(highs, axis=1), f, NN, preferred_element_type=jnp.float32
        )
        grad = grad + lax.dot_general(
            jnp.concatenate(lows, axis=1), f, NN, preferred_element_type=jnp.float32
        )
    v = v_ref[...]
    parts = hidden // lanes
    for j in range(parts):
        span = slice(j * lanes, (j + 1) * lanes)
        turned = grad[span].T * v[:, span]
        for i in range(f_ref.shape[1] // 8):
            at = (i * parts + j) * 8
            grad_ref[at : at + 8] = turned[i * 8 : (i + 1) * 8]
    ones = jnp.ones((8, lanes), jnp.float32)
    across = lambda x: lax.dot_general(
        ones, x, NT, precision=lax.Precision.HIGHEST, preferred_element_type=jnp.float32
    )[:1]
    bias = across(bias_sum) * v
    out = across(out_sum)
    at = hidden * f_ref.shape[1] // lanes
    for j in range(parts):
        span = slice(j * lanes, (j + 1) * lanes)
        grad_ref[at + j : at + j + 1] = bias[:, span]
        grad_ref[at + parts + j : at + parts + j + 1] = out[:, span]
    grad_ref[at + 2 * parts :] = jnp.zeros_like(grad_ref[at + 2 * parts :])


def local(
    features, w_input, b_input, w_output, terminal, start_counts, visit_counts, dest_nodes,
    tile_rows, tile_cols, send_blocks, tile_weight,
):
    f32, bf16 = jnp.float32, jnp.bfloat16
    nodes, feat = features.shape
    tiles, lanes, _ = tile_weight.shape
    blocks = nodes // lanes
    rows = terminal.shape[0]
    hidden = w_input.shape[1]
    reach = send_blocks.shape[0] // 2
    width = send_blocks.shape[1]
    slots = 2 * reach * width
    count = lax.axis_size("dom")
    assert reach == 4 and count % 8 == 0
    shape = lambda *s: jax.ShapeDtypeStruct(s, f32)
    row_v = w_output[None, :]

    plan = Plan(blocks, tiles, slots, rows)
    like = lambda x: jax.ShapeDtypeStruct(x.shape, x.dtype)
    field = shape(blocks, rows, lanes)
    padded = shape(blocks + 1, rows, lanes)
    halves = jax.ShapeDtypeStruct((blocks, 2 * rows, lanes), bf16)
    parcel = shape(reach, width * rows, lanes)
    small = shape(reach, 8, lanes)
    all_s = pltpu.VMEM((4 * reach, width * rows, lanes), f32)
    ext_s = pltpu.VMEM((slots, 2 * rows, lanes), bf16)
    sum_s = pltpu.VMEM((blocks + 1, rows, lanes), f32)
    flow_s = pltpu.VMEM((slots + 1, rows, lanes), f32)
    bind = lambda kernel, *lead: functools.partial(kernel, *lead, reach, width)
    flops = 2 * tiles * lanes * lanes * 2 * rows
    moved = tiles * lanes * lanes * 2
    send_t = send_blocks.T
    row_b = b_input[None, :]

    z0, split, odd, even = call(
        bind(first_kernel),
        (field, halves, parcel, parcel),
        [
            pltpu.SMEM(send_t.shape, jnp.int32),
            pltpu.VMEM(terminal.shape, f32),
            pltpu.SemaphoreType.DMA((4,)),
            pltpu.SemaphoreType.DMA,
        ],
        (),
        (),
        flops,
        moved,
        hbm=(send_t, terminal),
    )

    def load(arrived):
        return call(
            functools.partial(load_kernel, plan),
            (
                jax.ShapeDtypeStruct((plan.size,), jnp.int32),
                *map(like, (tile_weight, features, w_input, row_b, row_v)),
            ),
            [
                pltpu.SMEM(tile_rows.shape, jnp.int32),
                pltpu.SMEM(tile_cols.shape, jnp.int32),
                pltpu.SMEM(send_t.shape, jnp.int32),
                pltpu.SMEM(dest_nodes.shape, jnp.int32),
                pltpu.SemaphoreType.DMA((5,)),
                pltpu.SemaphoreType.DMA((4,)),
            ],
            (),
            (),
            flops,
            moved,
            hbm=(tile_rows, tile_cols, send_t, dest_nodes, tile_weight, features, w_input, row_b, row_v),
            smem_out=True,
            after=(arrived,),
        )

    far, (plans, weight, feature, w_in, b_in, v_out) = exchange(odd, even, load)

    def near(split, forward, *after):
        kernel = functools.partial(near_kernel, plan, forward)
        return call(kernel, padded, [], (plans,), (weight, split), flops, moved, after=after)

    act, growth = call(
        network_kernel,
        (shape(hidden, nodes), shape(blocks, 1, lanes)),
        [],
        (),
        (w_in, b_in, v_out, feature),
        2 * nodes * hidden * feat,
        nodes * hidden * 4,
    )

    def backup(part, got):
        return call(
            bind(backup_kernel, plan),
            (field, halves, parcel, parcel),
            [all_s, ext_s, sum_s],
            (plans,),
            (weight, part, growth, *got),
            flops,
            moved,
        )

    z1, split, odd, even = backup(near(split, True), far)
    got, part = exchange(odd, even, lambda arrived: near(split, True, arrived))
    z2, split2, odd, even = backup(part, got)
    got, part = exchange(odd, even, lambda arrived: near(split2, True, arrived))
    values, split3, odd, even = call(
        bind(turn_kernel, plan),
        (shape(rows, nodes), halves, parcel, parcel),
        [all_s, ext_s, sum_s, flow_s],
        (plans,),
        (weight, part, growth, *got, start_counts),
        2 * flops,
        moved,
    )
    got, part = exchange(odd, even, lambda arrived: near(split3, False, arrived))
    u1, split4, odd, even = call(
        bind(spread_kernel, plan, count),
        (field, halves, parcel, parcel),
        [all_s, flow_s],
        (plans,),
        (weight, growth, part, *got),
        flops,
        moved,
    )
    got, part = exchange(odd, even, lambda arrived: near(split4, False, arrived))
    u2, split5, odd, even = call(
        bind(last_kernel, plan, count),
        (field, halves, small, small),
        [all_s, flow_s, all_s],
        (plans,),
        (weight, growth, part, *got, *far),
        flops,
        moved,
    )
    got, node = exchange(
        odd,
        even,
        lambda arrived: call(
            functools.partial(node_kernel, plan),
            shape(blocks, 1, lanes),
            [sum_s],
            (plans,),
            (weight, split5, z0, z1, z2, u1, u2, visit_counts),
            flops,
            moved,
            after=(arrived,),
        ),
    )
    every = ("dest", "dom")
    members = count * lax.axis_size("dest")
    used = hidden * feat // lanes + 2 * hidden // lanes
    share = -(-used // members)
    scale = 1.0 / math.sqrt(nodes * count * rows * lax.axis_size("dest"))
    packed = call(
        functools.partial(gradient_kernel, plan, count, reach, width, scale),
        shape(share * members, lanes),
        [pltpu.VMEM((blocks, 1, lanes), f32), pltpu.VMEM((4 * reach, 8, lanes), f32)],
        (plans,),
        (v_out, feature, act, node, *got),
        4 * nodes * hidden * feat,
        nodes * hidden * 4,
    )
    packed = packed.reshape(members, 1, share * lanes)
    mine = lax.all_to_all(packed, every, 0, 0, tiled=True).sum(axis=0, keepdims=True)
    spread = jnp.broadcast_to(mine, packed.shape)
    summed = lax.all_to_all(spread, every, 0, 0, tiled=True).reshape(share * members, lanes)
    side = summed[hidden * feat // lanes : used].reshape(2, hidden)
    grad = summed[: hidden * feat // lanes].reshape(feat // 8, hidden // lanes, 8, lanes)
    return values, grad.transpose(0, 2, 1, 3).reshape(feat, hidden), side[0], side[1]


def solution(mesh):
    in_specs = (
        P("dom", None),
        P(),
        P(),
        P(),
        P("dest", "dom"),
        P("dest", "dom"),
        P("dest", "dom"),
        P("dest"),
        P("dom"),
        P("dom"),
        P("dom", None),
        P("dom", None, None),
    )
    out_specs = (P("dest", "dom"), P(), P(), P())
    return jax.shard_map(local, mesh=mesh, in_specs=in_specs, out_specs=out_specs, check_vma=False)
```

time: 120 us -> 108 us (0.900)
  local copies, waits for them, and re-layouts: 12.3 us -> 1.53 us
  waiting for transfers between devices: 31.8 us -> 23.8 us
  Pallas kernels: 18.2 us -> 25.6 us
    unnamed x37 -> x4, local copies, waits for them, and re-layouts: 10.8 us -> 0.01 us
    ppermute x18, waiting for transfers between devices: 31.8 us -> 23.7 us  [exchange(): lax.ppermute(x, 'dom', [(i, i ^ bit) for i in devices])]
    pallas_call x14 -> x15, Pallas kernels: 18.2 us -> 25.6 us  [call(): pl.pallas_call(kernel, out_shape=out_shape, in_specs=[space(pltpu.HBM)] *...]
  transfers between devices with their start and end apart: 24 -> 24, of which waited for: 17 -> 16; matrix products, arithmetic and copies ran while one was open for 0% -> 0% of each run, Pallas kernels for 4% -> 13%
where the time goes in v2:
time: 108 us
  blocking collectives  28.1 us (26%)
  starting transfers between devices  27.9 us (26%)
  Pallas kernels  25.6 us (24%)
  waiting for transfers between devices  23.8 us (22%)
  local copies, waits for them, and re-layouts  1.53 us (1%)
    ppermute x18, starting transfers between devices, exchange(): lax.ppermute(x, 'dom', [(i, i ^ bit) for i in devices])  27.4 us
    pallas_call x15, Pallas kernels, call(): pl.pallas_call(kernel, out_shape=out_shape, in_specs=[space(pltpu.HBM)] *...  25.6 us
    ppermute x18, waiting for transfers between devices, exchange(): lax.ppermute(x, 'dom', [(i, i ^ bit) for i in devices])  23.7 us
    all_to_all x1, blocking collectives, local(): lax.all_to_all(packed, every, 0, 0, tiled=True).sum(axis=0, keepdims=True)  15.2 us
    all_to_all x1, blocking collectives, local(): lax.all_to_all(spread, every, 0, 0, tiled=True)  12.9 us
  transfers between devices with their start and end apart: 24, of which 16 were waited for; matrix products, arithmetic and copies ran while one was open for 0% of the time, Pallas kernels for 13%

profile of v2, /device:TPU:0, one launch (start us, length us, event | category | flops | bytes accessed | tf_op | source)
XLA Modules:
  0.0 108.1 jit_solution(15585393938299524007)
XLA Ops:
  3.1 2.9 %collective-permute-start.1 = (f32[4,32,128]{2,1,0:T(8,128)S(1)}, f32[4,32,128]{2,1,0:T(8,128)S(1)}, u32[]{:S(2)}, u32[]{:S(2)}) collective-permute-start(f32[4,32,128]{2,1,0:T(8,128)S(1)} %pad_maximum_fusion), channel_id=1, source_target_pairs={{0,4},{2,6},{4,0},{6,2},{8,12},{10,14},{12,8},{14,10},{16,20},{18,... | collective-permute-start | bytes 196616 | tf_op jit(solution)/shard_map/ppermute | solution.py:50
  6.1 2.8 %shard_map.148 = (s32[226]{0:T(256)S(1)}, bf16[80,128,128]{2,1,0:T(8,128)(2,1)S(1)}, bf16[4096,128]{1,0:T(8,128)(2,1)S(1)}, bf16[128,512]{1,0:T(8,128)(2,1)S(1)}...) custom-call(s32[80]{0:T(128)} %refs_0_.1, s32[80]{0:T(128)} %refs_1_.1, s32[2,8]{1,0:T(2,128)} %bitcast.21, s32[16]{0:T(128)} %refs_3_.1, ...), custom_call_target="tpu_custom_call" | custom-call | flops 83886080 | bytes 2621440 | tf_op jit(solution)/shard_map/pallas_call | solution.py:84
  9.0 3.1 %collective-permute-start.2 = (f32[4,32,128]{2,1,0:T(8,128)S(1)}, f32[4,32,128]{2,1,0:T(8,128)S(1)}, u32[]{:S(2)}, u32[]{:S(2)}) collective-permute-start(f32[4,32,128]{2,1,0:T(8,128)S(1)} %get-tuple-element.113), channel_id=1, source_target_pairs={{0,8},{2,10},{4,12},{6,14},{8,0},{10,2},{12,4},{14,6},{16,24},{18,... | collective-permute-start | bytes 196616 | tf_op jit(solution)/shard_map/ppermute | solution.py:50
  12.2 2.0 %shard_map.149.part_ref = f32[33,16,128]{2,1,0:T(8,128)S(1)} custom-call(s32[226]{0:T(256)S(1)} %get-tuple-element.61.plan_ref.refs_0_, bf16[80,128,128]{2,1,0:T(8,128)(2,1)S(1)} %get-tuple-element.62.w_ref.refs_1_, bf16[32,32,128]{2,1,0:T(8,128)(2,1)S(1)} %get-tuple-element.63.split_ref), custom_call_target="tpu_custom_call" | custom-call | flops 83886080 | bytes 2621440 | tf_op jit(solution)/shard_map/pallas_call | solution.py:84
  14.2 1.4 %shard_map.150 = (f32[512,4096]{1,0:T(8,128)S(1)}, f32[32,1,128]{2,1,0:T(1,128)S(1)}) custom-call(bf16[128,512]{1,0:T(8,128)(2,1)S(1)} %get-tuple-element.64.w_ref, f32[1,512]{1,0:T(1,128)S(1)} %get-tuple-element.65.b_ref, f32[1,512]{1,0:T(1,128)S(1)} %get-tuple-element.66.v_ref, bf16[4096,128]{1,0:T(8,128)(2,1)S(1)} %get-tuple-element.67.f_ref), custom_call_target="tpu_custom_call" | custom-call | flops 536870912 | bytes 8388608 | tf_op jit(solution)/shard_map/pallas_call | solution.py:84
  18.0 1.5 %collective-permute-start.5 = (f32[4,32,128]{2,1,0:T(8,128)S(1)}, f32[4,32,128]{2,1,0:T(8,128)S(1)}, u32[]{:S(2)}, u32[]{:S(2)}) collective-permute-start(f32[4,32,128]{2,1,0:T(8,128)S(1)} %pad_maximum_fusion.3), channel_id=1, source_target_pairs={{0,4},{2,6},{4,0},{6,2},{8,12},{10,14},{12,8},{14,10},{16,20},{18,... | collective-permute-start | bytes 196616 | tf_op jit(solution)/shard_map/ppermute | solution.py:50
  19.5 2.0 %shard_map.152.part_ref = f32[33,16,128]{2,1,0:T(8,128)S(1)} custom-call(s32[226]{0:T(256)S(1)} %get-tuple-element.61.plan_ref.refs_0_, bf16[80,128,128]{2,1,0:T(8,128)(2,1)S(1)} %get-tuple-element.62.w_ref.refs_1_, bf16[32,32,128]{2,1,0:T(8,128)(2,1)S(1)} %get-tuple-element.72.refs_2_, f32[4,32,128]{2,1,0:T(8,128)S(1)} %collective-permute-done.4.refs_3_.near_ref), custom_call_target="tpu_custom_call" | custom-call | flops 83886080 | bytes 2621440 | tf_op jit(solution)/shard_map/pallas_call | solution.py:84
  22.4 1.6 %collective-permute-start.6 = (f32[4,32,128]{2,1,0:T(8,128)S(1)}, f32[4,32,128]{2,1,0:T(8,128)S(1)}, u32[]{:S(2)}, u32[]{:S(2)}) collective-permute-start(f32[4,32,128]{2,1,0:T(8,128)S(1)} %get-tuple-element.111), channel_id=1, source_target_pairs={{0,8},{2,10},{4,12},{6,14},{8,0},{10,2},{12,4},{14,6},{16,24},{18,... | collective-permute-start | bytes 196616 | tf_op jit(solution)/shard_map/ppermute | solution.py:50
  24.1 2.8 %collective-permute-done.6.first_ref = f32[4,32,128]{2,1,0:T(8,128)S(1)} collective-permute-done((f32[4,32,128]{2,1,0:T(8,128)S(1)}, f32[4,32,128]{2,1,0:T(8,128)S(1)}, u32[]{:S(2)}, u32[]{:S(2)}) %collective-permute-start.6) | collective-permute-done | bytes 65568 | tf_op jit(solution)/shard_map/ppermute | solution.py:50
  29.3 1.5 %collective-permute-start.9 = (f32[4,32,128]{2,1,0:T(8,128)S(1)}, f32[4,32,128]{2,1,0:T(8,128)S(1)}, u32[]{:S(2)}, u32[]{:S(2)}) collective-permute-start(f32[4,32,128]{2,1,0:T(8,128)S(1)} %pad_maximum_fusion.6), channel_id=1, source_target_pairs={{0,4},{2,6},{4,0},{6,2},{8,12},{10,14},{12,8},{14,10},{16,20},{18,... | collective-permute-start | bytes 196616 | tf_op jit(solution)/shard_map/ppermute | solution.py:50
  30.8 2.0 %shard_map.154.part_ref = f32[33,16,128]{2,1,0:T(8,128)S(1)} custom-call(s32[226]{0:T(256)S(1)} %get-tuple-element.61.plan_ref.refs_0_, bf16[80,128,128]{2,1,0:T(8,128)(2,1)S(1)} %get-tuple-element.62.w_ref.refs_1_, bf16[32,32,128]{2,1,0:T(8,128)(2,1)S(1)} %get-tuple-element.77.refs_2_, f32[4,32,128]{2,1,0:T(8,128)S(1)} %collective-permute-done.8.refs_3_.near_ref), custom_call_target="tpu_custom_call" | custom-call | flops 83886080 | bytes 2621440 | tf_op jit(solution)/shard_map/pallas_call | solution.py:84
  33.8 2.6 %collective-permute-start.10 = (f32[4,32,128]{2,1,0:T(8,128)S(1)}, f32[4,32,128]{2,1,0:T(8,128)S(1)}, u32[]{:S(2)}, u32[]{:S(2)}) collective-permute-start(f32[4,32,128]{2,1,0:T(8,128)S(1)} %get-tuple-element.109), channel_id=1, source_target_pairs={{0,8},{2,10},{4,12},{6,14},{8,0},{10,2},{12,4},{14,6},{16,24},{18,... | collective-permute-start | bytes 196616 | tf_op jit(solution)/shard_map/ppermute | solution.py:50
  36.3 2.2 %collective-permute-done.10.first_ref = f32[4,32,128]{2,1,0:T(8,128)S(1)} collective-permute-done((f32[4,32,128]{2,1,0:T(8,128)S(1)}, f32[4,32,128]{2,1,0:T(8,128)S(1)}, u32[]{:S(2)}, u32[]{:S(2)}) %collective-permute-start.10) | collective-permute-done | bytes 65568 | tf_op jit(solution)/shard_map/ppermute | solution.py:50
  38.6 1.9 %shard_map.155 = (f32[16,4096]{1,0:T(8,128)}, bf16[32,32,128]{2,1,0:T(8,128)(2,1)S(1)}, f32[4,32,128]{2,1,0:T(8,128)S(1)}, f32[4,32,128]{2,1,0:T(8,128)S(1)}) custom-call(s32[226]{0:T(256)S(1)} %get-tuple-element.61.plan_ref.refs_0_, bf16[80,128,128]{2,1,0:T(8,128)(2,1)S(1)} %get-tuple-element.62.w_ref.refs_1_, f32[33,16,128]{2,1,0:T(8,128)S(1)} %shard_map.154.part_ref, ...), custom_call_target="tpu_custom_call" | custom-call | flops 167772160 | bytes 2621440 | tf_op jit(solution)/shard_map/pallas_call | solution.py:84
  40.5 1.2 %collective-permute-done.12.refs_3_.near_ref = f32[4,32,128]{2,1,0:T(8,128)S(1)} collective-permute-done((f32[4,32,128]{2,1,0:T(8,128)S(1)}, f32[4,32,128]{2,1,0:T(8,128)S(1)}, u32[]{:S(2)}, u32[]{:S(2)}) %collective-permute-start.12) | collective-permute-done | bytes 65568 | tf_op jit(solution)/shard_map/ppermute | solution.py:50
  41.7 1.5 %collective-permute-start.13 = (f32[4,32,128]{2,1,0:T(8,128)S(1)}, f32[4,32,128]{2,1,0:T(8,128)S(1)}, u32[]{:S(2)}, u32[]{:S(2)}) collective-permute-start(f32[4,32,128]{2,1,0:T(8,128)S(1)} %pad_maximum_fusion.9), channel_id=1, source_target_pairs={{0,4},{2,6},{4,0},{6,2},{8,12},{10,14},{12,8},{14,10},{16,20},{18,... | collective-permute-start | bytes 196616 | tf_op jit(solution)/shard_map/ppermute | solution.py:50
  43.2 1.4 %shard_map.156.sum_ref = f32[33,16,128]{2,1,0:T(8,128)S(1)} custom-call(s32[226]{0:T(256)S(1)} %get-tuple-element.61.plan_ref.refs_0_, bf16[80,128,128]{2,1,0:T(8,128)(2,1)S(1)} %get-tuple-element.62.w_ref.refs_1_, bf16[32,32,128]{2,1,0:T(8,128)(2,1)S(1)} %get-tuple-element.84.refs_2_, f32[4,32,128]{2,1,0:T(8,128)S(1)} %collective-permute-done.12.refs_3_.near_ref), custom_call_target="tpu_custom_call" | custom-call | flops 83886080 | bytes 2621440 | tf_op jit(solution)/shard_map/pallas_call | solution.py:84
  44.6 1.5 %collective-permute-done.13.side_ref = f32[4,32,128]{2,1,0:T(8,128)S(1)} collective-permute-done((f32[4,32,128]{2,1,0:T(8,128)S(1)}, f32[4,32,128]{2,1,0:T(8,128)S(1)}, u32[]{:S(2)}, u32[]{:S(2)}) %collective-permute-start.13) | collective-permute-done | bytes 65568 | tf_op jit(solution)/shard_map/ppermute | solution.py:50
  46.2 2.9 %collective-permute-start.14 = (f32[4,32,128]{2,1,0:T(8,128)S(1)}, f32[4,32,128]{2,1,0:T(8,128)S(1)}, u32[]{:S(2)}, u32[]{:S(2)}) collective-permute-start(f32[4,32,128]{2,1,0:T(8,128)S(1)} %get-tuple-element.107), channel_id=1, source_target_pairs={{0,8},{2,10},{4,12},{6,14},{8,0},{10,2},{12,4},{14,6},{16,24},{18,... | collective-permute-start | bytes 196616 | tf_op jit(solution)/shard_map/ppermute | solution.py:50
  49.1 2.2 %collective-permute-done.14.first_ref = f32[4,32,128]{2,1,0:T(8,128)S(1)} collective-permute-done((f32[4,32,128]{2,1,0:T(8,128)S(1)}, f32[4,32,128]{2,1,0:T(8,128)S(1)}, u32[]{:S(2)}, u32[]{:S(2)}) %collective-permute-start.14) | collective-permute-done | bytes 65568 | tf_op jit(solution)/shard_map/ppermute | solution.py:50
  53.6 1.5 %collective-permute-start.17 = (f32[4,32,128]{2,1,0:T(8,128)S(1)}, f32[4,32,128]{2,1,0:T(8,128)S(1)}, u32[]{:S(2)}, u32[]{:S(2)}) collective-permute-start(f32[4,32,128]{2,1,0:T(8,128)S(1)} %pad_maximum_fusion.12), channel_id=1, source_target_pairs={{0,4},{2,6},{4,0},{6,2},{8,12},{10,14},{12,8},{14,10},{16,20},{18,... | collective-permute-start | bytes 196616 | tf_op jit(solution)/shard_map/ppermute | solution.py:50
  55.1 1.3 %shard_map.158.sum_ref = f32[33,16,128]{2,1,0:T(8,128)S(1)} custom-call(s32[226]{0:T(256)S(1)} %get-tuple-element.61.plan_ref.refs_0_, bf16[80,128,128]{2,1,0:T(8,128)(2,1)S(1)} %get-tuple-element.62.w_ref.refs_1_, bf16[32,32,128]{2,1,0:T(8,128)(2,1)S(1)} %get-tuple-element.89.refs_2_, f32[4,32,128]{2,1,0:T(8,128)S(1)} %collective-permute-done.16.refs_3_.near_ref), custom_call_target="tpu_custom_call" | custom-call | flops 83886080 | bytes 2621440 | tf_op jit(solution)/shard_map/pallas_call | solution.py:84
  56.4 1.5 %collective-permute-done.17.side_ref = f32[4,32,128]{2,1,0:T(8,128)S(1)} collective-permute-done((f32[4,32,128]{2,1,0:T(8,128)S(1)}, f32[4,32,128]{2,1,0:T(8,128)S(1)}, u32[]{:S(2)}, u32[]{:S(2)}) %collective-permute-start.17) | collective-permute-done | bytes 65568 | tf_op jit(solution)/shard_map/ppermute | solution.py:50
  58.0 3.2 %collective-permute-start.18 = (f32[4,32,128]{2,1,0:T(8,128)S(1)}, f32[4,32,128]{2,1,0:T(8,128)S(1)}, u32[]{:S(2)}, u32[]{:S(2)}) collective-permute-start(f32[4,32,128]{2,1,0:T(8,128)S(1)} %get-tuple-element.105), channel_id=1, source_target_pairs={{0,8},{2,10},{4,12},{6,14},{8,0},{10,2},{12,4},{14,6},{16,24},{18,... | collective-permute-start | bytes 196616 | tf_op jit(solution)/shard_map/ppermute | solution.py:50
  61.2 2.2 %collective-permute-done.18.first_ref = f32[4,32,128]{2,1,0:T(8,128)S(1)} collective-permute-done((f32[4,32,128]{2,1,0:T(8,128)S(1)}, f32[4,32,128]{2,1,0:T(8,128)S(1)}, u32[]{:S(2)}, u32[]{:S(2)}) %collective-permute-start.18) | collective-permute-done | bytes 65568 | tf_op jit(solution)/shard_map/ppermute | solution.py:50
  65.7 1.5 %collective-permute-start.21 = (f32[4,8,128]{2,1,0:T(8,128)S(1)}, f32[4,8,128]{2,1,0:T(8,128)S(1)}, u32[]{:S(2)}, u32[]{:S(2)}) collective-permute-start(f32[4,8,128]{2,1,0:T(8,128)S(1)} %pad_maximum_fusion.15), channel_id=1, source_target_pairs={{0,4},{2,6},{4,0},{6,2},{8,12},{10,14},{12,8},{14,10},{16,20},{18,... | collective-permute-start | bytes 49160 | tf_op jit(solution)/shard_map/ppermute | solution.py:50
  67.2 1.5 %shard_map.160.node_ref = f32[32,1,128]{2,1,0:T(1,128)S(1)} custom-call(s32[226]{0:T(256)S(1)} %get-tuple-element.61.plan_ref.refs_0_, bf16[80,128,128]{2,1,0:T(8,128)(2,1)S(1)} %get-tuple-element.62.w_ref.refs_1_, bf16[32,32,128]{2,1,0:T(8,128)(2,1)S(1)} %get-tuple-element.94.refs_2_, f32[32,16,128]{2,1,0:T(8,128)S(1)} %get-tuple-element.95.refs_3_, ...), custom_call_target="tpu_custom_call" | custom-call | flops 83886080 | bytes 2621440 | tf_op jit(solution)/shard_map/pallas_call | solution.py:84
  69.6 2.9 %collective-permute-start.22 = (f32[4,8,128]{2,1,0:T(8,128)S(1)}, f32[4,8,128]{2,1,0:T(8,128)S(1)}, u32[]{:S(2)}, u32[]{:S(2)}) collective-permute-start(f32[4,8,128]{2,1,0:T(8,128)S(1)} %get-tuple-element.175), channel_id=1, source_target_pairs={{0,8},{2,10},{4,12},{6,14},{8,0},{10,2},{12,4},{14,6},{16,24},{18,... | collective-permute-start | bytes 49160 | tf_op jit(solution)/shard_map/ppermute | solution.py:50
  72.5 1.7 %collective-permute-done.22.first_ref = f32[4,8,128]{2,1,0:T(8,128)S(1)} collective-permute-done((f32[4,8,128]{2,1,0:T(8,128)S(1)}, f32[4,8,128]{2,1,0:T(8,128)S(1)}, u32[]{:S(2)}, u32[]{:S(2)}) %collective-permute-start.22) | collective-permute-done | bytes 16416 | tf_op jit(solution)/shard_map/ppermute | solution.py:50
  74.2 4.2 %shard_map.161 = f32[544,128]{1,0:T(8,128)S(1)} custom-call(s32[226]{0:T(256)S(1)} %get-tuple-element.61.plan_ref.refs_0_, f32[1,512]{1,0:T(1,128)S(1)} %get-tuple-element.66.v_ref, bf16[4096,128]{1,0:T(8,128)(2,1)S(1)} %get-tuple-element.67.f_ref, f32[512,4096]{1,0:T(8,128)S(1)} %get-tuple-element.81.act_ref, f32[32,1,128]{2,1,0:T(1,128)S(1)} %shard_map.160.node_ref, ...), custom_call_target="tpu_custom_call" | custom-call | flops 1073741824 | bytes 8388608 | tf_op jit(solution)/shard_map/pallas_call | solution.py:84
  78.4 15.2 %all_to_all.10 = f32[32,1,2176]{2,1,0:T(1,128)S(1)} all-to-all(f32[32,1,2176]{2,1,0:T(1,128)S(1)} %bitcast.14), channel_id=1, replica_groups=mesh['dom'=16,'dest'=2] {'dest','dom'}, dimensions={0} | all-to-all | bytes 557056 | tf_op jit(solution)/shard_map/all_to_all | solution.py:653
  93.9 12.9 %all_to_all.11 = f32[32,1,2176]{2,1,0:T(1,128)S(1)} all-to-all(f32[32,1,2176]{2,1,0:T(1,128)S(1)} %broadcast_in_dim.14), channel_id=1, replica_groups=mesh['dom'=16,'dest'=2] {'dest','dom'}, dimensions={0} | all-to-all | bytes 557056 | tf_op jit(solution)/shard_map/all_to_all | solution.py:655
  (71 shorter events, 16.4 us)
Async XLA Ops:
  1.7 1.5 %collective-permute-start = (f32[4,32,128]{2,1,0:T(8,128)S(1)}, f32[4,32,128]{2,1,0:T(8,128)S(1)}, u32[]{:S(2)}, u32[]{:S(2)}) collective-permute-start(f32[4,32,128]{2,1,0:T(8,128)S(1)} %get-tuple-element.54), channel_id=1, source_target_pairs={{0,2},{2,0},{4,6},{6,4},{8,10},{10,8},{12,14},{14,12},{16,18},{18,... | collective-permute-start | bytes 196616 | tf_op jit(solution)/shard_map/ppermute | solution.py:50
  3.1 5.7 %collective-permute-start.1 = (f32[4,32,128]{2,1,0:T(8,128)S(1)}, f32[4,32,128]{2,1,0:T(8,128)S(1)}, u32[]{:S(2)}, u32[]{:S(2)}) collective-permute-start(f32[4,32,128]{2,1,0:T(8,128)S(1)} %pad_maximum_fusion), channel_id=1, source_target_pairs={{0,4},{2,6},{4,0},{6,2},{8,12},{10,14},{12,8},{14,10},{16,20},{18,... | collective-permute-start | bytes 196616 | tf_op jit(solution)/shard_map/ppermute | solution.py:50
  8.9 6.7 %collective-permute-start.3 = (f32[4,32,128]{2,1,0:T(8,128)S(1)}, f32[4,32,128]{2,1,0:T(8,128)S(1)}, u32[]{:S(2)}, u32[]{:S(2)}) collective-permute-start(f32[4,32,128]{2,1,0:T(8,128)S(1)} %get-tuple-element.112), channel_id=1, source_target_pairs={{0,2},{2,0},{4,6},{6,4},{8,16},{10,18},{12,20},{14,22},{16,8},{18,... | collective-permute-start | bytes 196616 | tf_op jit(solution)/shard_map/ppermute | solution.py:69
  9.0 6.6 %collective-permute-start.2 = (f32[4,32,128]{2,1,0:T(8,128)S(1)}, f32[4,32,128]{2,1,0:T(8,128)S(1)}, u32[]{:S(2)}, u32[]{:S(2)}) collective-permute-start(f32[4,32,128]{2,1,0:T(8,128)S(1)} %get-tuple-element.113), channel_id=1, source_target_pairs={{0,8},{2,10},{4,12},{6,14},{8,0},{10,2},{12,4},{14,6},{16,24},{18,... | collective-permute-start | bytes 196616 | tf_op jit(solution)/shard_map/ppermute | solution.py:50
  16.7 1.3 %collective-permute-start.4 = (f32[4,32,128]{2,1,0:T(8,128)S(1)}, f32[4,32,128]{2,1,0:T(8,128)S(1)}, u32[]{:S(2)}, u32[]{:S(2)}) collective-permute-start(f32[4,32,128]{2,1,0:T(8,128)S(1)} %get-tuple-element.71), channel_id=1, source_target_pairs={{0,2},{2,0},{4,6},{6,4},{8,10},{10,8},{12,14},{14,12},{16,18},{18,... | collective-permute-start | bytes 196616 | tf_op jit(solution)/shard_map/ppermute | solution.py:50
  18.0 4.3 %collective-permute-start.5 = (f32[4,32,128]{2,1,0:T(8,128)S(1)}, f32[4,32,128]{2,1,0:T(8,128)S(1)}, u32[]{:S(2)}, u32[]{:S(2)}) collective-permute-start(f32[4,32,128]{2,1,0:T(8,128)S(1)} %pad_maximum_fusion.3), channel_id=1, source_target_pairs={{0,4},{2,6},{4,0},{6,2},{8,12},{10,14},{12,8},{14,10},{16,20},{18,... | collective-permute-start | bytes 196616 | tf_op jit(solution)/shard_map/ppermute | solution.py:50
  22.4 1.7 %collective-permute-start.7 = (f32[4,32,128]{2,1,0:T(8,128)S(1)}, f32[4,32,128]{2,1,0:T(8,128)S(1)}, u32[]{:S(2)}, u32[]{:S(2)}) collective-permute-start(f32[4,32,128]{2,1,0:T(8,128)S(1)} %get-tuple-element.110), channel_id=1, source_target_pairs={{0,2},{2,0},{4,6},{6,4},{8,16},{10,18},{12,20},{14,22},{16,8},{18,... | collective-permute-start | bytes 196616 | tf_op jit(solution)/shard_map/ppermute | solution.py:69
  22.4 4.5 %collective-permute-start.6 = (f32[4,32,128]{2,1,0:T(8,128)S(1)}, f32[4,32,128]{2,1,0:T(8,128)S(1)}, u32[]{:S(2)}, u32[]{:S(2)}) collective-permute-start(f32[4,32,128]{2,1,0:T(8,128)S(1)} %get-tuple-element.111), channel_id=1, source_target_pairs={{0,8},{2,10},{4,12},{6,14},{8,0},{10,2},{12,4},{14,6},{16,24},{18,... | collective-permute-start | bytes 196616 | tf_op jit(solution)/shard_map/ppermute | solution.py:50
  28.0 10.6 %copy-start = (s32[16,4096]{1,0:T(8,128)S(1)}, s32[16,4096]{1,0:T(8,128)}, u32[]{:S(2)}) copy-start(s32[16,4096]{1,0:T(8,128)} %start_ref.1) | copy-start | bytes 786436
  28.0 1.3 %collective-permute-start.8 = (f32[4,32,128]{2,1,0:T(8,128)S(1)}, f32[4,32,128]{2,1,0:T(8,128)S(1)}, u32[]{:S(2)}, u32[]{:S(2)}) collective-permute-start(f32[4,32,128]{2,1,0:T(8,128)S(1)} %get-tuple-element.76), channel_id=1, source_target_pairs={{0,2},{2,0},{4,6},{6,4},{8,10},{10,8},{12,14},{14,12},{16,18},{18,... | collective-permute-start | bytes 196616 | tf_op jit(solution)/shard_map/ppermute | solution.py:50
  29.3 4.3 %collective-permute-start.9 = (f32[4,32,128]{2,1,0:T(8,128)S(1)}, f32[4,32,128]{2,1,0:T(8,128)S(1)}, u32[]{:S(2)}, u32[]{:S(2)}) collective-permute-start(f32[4,32,128]{2,1,0:T(8,128)S(1)} %pad_maximum_fusion.6), channel_id=1, source_target_pairs={{0,4},{2,6},{4,0},{6,2},{8,12},{10,14},{12,8},{14,10},{16,20},{18,... | collective-permute-start | bytes 196616 | tf_op jit(solution)/shard_map/ppermute | solution.py:50
  33.7 2.6 %collective-permute-start.11 = (f32[4,32,128]{2,1,0:T(8,128)S(1)}, f32[4,32,128]{2,1,0:T(8,128)S(1)}, u32[]{:S(2)}, u32[]{:S(2)}) collective-permute-start(f32[4,32,128]{2,1,0:T(8,128)S(1)} %get-tuple-element.108), channel_id=1, source_target_pairs={{0,2},{2,0},{4,6},{6,4},{8,16},{10,18},{12,20},{14,22},{16,8},{18,... | collective-permute-start | bytes 196616 | tf_op jit(solution)/shard_map/ppermute | solution.py:69
  33.8 4.8 %collective-permute-start.10 = (f32[4,32,128]{2,1,0:T(8,128)S(1)}, f32[4,32,128]{2,1,0:T(8,128)S(1)}, u32[]{:S(2)}, u32[]{:S(2)}) collective-permute-start(f32[4,32,128]{2,1,0:T(8,128)S(1)} %get-tuple-element.109), channel_id=1, source_target_pairs={{0,8},{2,10},{4,12},{6,14},{8,0},{10,2},{12,4},{14,6},{16,24},{18,... | collective-permute-start | bytes 196616 | tf_op jit(solution)/shard_map/ppermute | solution.py:50
  40.5 1.3 %collective-permute-start.12 = (f32[4,32,128]{2,1,0:T(8,128)S(1)}, f32[4,32,128]{2,1,0:T(8,128)S(1)}, u32[]{:S(2)}, u32[]{:S(2)}) collective-permute-start(f32[4,32,128]{2,1,0:T(8,128)S(1)} %get-tuple-element.83), channel_id=1, source_target_pairs={{0,2},{2,0},{4,6},{6,4},{8,10},{10,8},{12,14},{14,12},{16,18},{18,... | collective-permute-start | bytes 196616 | tf_op jit(solution)/shard_map/ppermute | solution.py:50
  41.7 4.3 %collective-permute-start.13 = (f32[4,32,128]{2,1,0:T(8,128)S(1)}, f32[4,32,128]{2,1,0:T(8,128)S(1)}, u32[]{:S(2)}, u32[]{:S(2)}) collective-permute-start(f32[4,32,128]{2,1,0:T(8,128)S(1)} %pad_maximum_fusion.9), channel_id=1, source_target_pairs={{0,4},{2,6},{4,0},{6,2},{8,12},{10,14},{12,8},{14,10},{16,20},{18,... | collective-permute-start | bytes 196616 | tf_op jit(solution)/shard_map/ppermute | solution.py:50
  46.1 3.0 %collective-permute-start.15 = (f32[4,32,128]{2,1,0:T(8,128)S(1)}, f32[4,32,128]{2,1,0:T(8,128)S(1)}, u32[]{:S(2)}, u32[]{:S(2)}) collective-permute-start(f32[4,32,128]{2,1,0:T(8,128)S(1)} %get-tuple-element.106), channel_id=1, source_target_pairs={{0,2},{2,0},{4,6},{6,4},{8,16},{10,18},{12,20},{14,22},{16,8},{18,... | collective-permute-start | bytes 196616 | tf_op jit(solution)/shard_map/ppermute | solution.py:69
  46.2 5.1 %collective-permute-start.14 = (f32[4,32,128]{2,1,0:T(8,128)S(1)}, f32[4,32,128]{2,1,0:T(8,128)S(1)}, u32[]{:S(2)}, u32[]{:S(2)}) collective-permute-start(f32[4,32,128]{2,1,0:T(8,128)S(1)} %get-tuple-element.107), channel_id=1, source_target_pairs={{0,8},{2,10},{4,12},{6,14},{8,0},{10,2},{12,4},{14,6},{16,24},{18,... | collective-permute-start | bytes 196616 | tf_op jit(solution)/shard_map/ppermute | solution.py:50
  52.3 1.3 %collective-permute-start.16 = (f32[4,32,128]{2,1,0:T(8,128)S(1)}, f32[4,32,128]{2,1,0:T(8,128)S(1)}, u32[]{:S(2)}, u32[]{:S(2)}) collective-permute-start(f32[4,32,128]{2,1,0:T(8,128)S(1)} %get-tuple-element.88), channel_id=1, source_target_pairs={{0,2},{2,0},{4,6},{6,4},{8,10},{10,8},{12,14},{14,12},{16,18},{18,... | collective-permute-start | bytes 196616 | tf_op jit(solution)/shard_map/ppermute | solution.py:50
  53.6 4.3 %collective-permute-start.17 = (f32[4,32,128]{2,1,0:T(8,128)S(1)}, f32[4,32,128]{2,1,0:T(8,128)S(1)}, u32[]{:S(2)}, u32[]{:S(2)}) collective-permute-start(f32[4,32,128]{2,1,0:T(8,128)S(1)} %pad_maximum_fusion.12), channel_id=1, source_target_pairs={{0,4},{2,6},{4,0},{6,2},{8,12},{10,14},{12,8},{14,10},{16,20},{18,... | collective-permute-start | bytes 196616 | tf_op jit(solution)/shard_map/ppermute | solution.py:50
  56.4 10.7 %copy-start.1 = (s32[16,4096]{1,0:T(8,128)S(1)}, s32[16,4096]{1,0:T(8,128)}, u32[]{:S(2)}) copy-start(s32[16,4096]{1,0:T(8,128)} %refs_8_.1) | copy-start | bytes 786436
  58.0 3.2 %collective-permute-start.19 = (f32[4,32,128]{2,1,0:T(8,128)S(1)}, f32[4,32,128]{2,1,0:T(8,128)S(1)}, u32[]{:S(2)}, u32[]{:S(2)}) collective-permute-start(f32[4,32,128]{2,1,0:T(8,128)S(1)} %get-tuple-element.104), channel_id=1, source_target_pairs={{0,2},{2,0},{4,6},{6,4},{8,16},{10,18},{12,20},{14,22},{16,8},{18,... | collective-permute-start | bytes 196616 | tf_op jit(solution)/shard_map/ppermute | solution.py:69
  58.0 5.4 %collective-permute-start.18 = (f32[4,32,128]{2,1,0:T(8,128)S(1)}, f32[4,32,128]{2,1,0:T(8,128)S(1)}, u32[]{:S(2)}, u32[]{:S(2)}) collective-permute-start(f32[4,32,128]{2,1,0:T(8,128)S(1)} %get-tuple-element.105), channel_id=1, source_target_pairs={{0,8},{2,10},{4,12},{6,14},{8,0},{10,2},{12,4},{14,6},{16,24},{18,... | collective-permute-start | bytes 196616 | tf_op jit(solution)/shard_map/ppermute | solution.py:50
  64.4 1.2 %collective-permute-start.20 = (f32[4,8,128]{2,1,0:T(8,128)S(1)}, f32[4,8,128]{2,1,0:T(8,128)S(1)}, u32[]{:S(2)}, u32[]{:S(2)}) collective-permute-start(f32[4,8,128]{2,1,0:T(8,128)S(1)} %get-tuple-element.93), channel_id=1, source_target_pairs={{0,2},{2,0},{4,6},{6,4},{8,10},{10,8},{12,14},{14,12},{16,18},{18,... | collective-permute-start | bytes 49160 | tf_op jit(solution)/shard_map/ppermute | solution.py:50
  65.7 3.8 %collective-permute-start.21 = (f32[4,8,128]{2,1,0:T(8,128)S(1)}, f32[4,8,128]{2,1,0:T(8,128)S(1)}, u32[]{:S(2)}, u32[]{:S(2)}) collective-permute-start(f32[4,8,128]{2,1,0:T(8,128)S(1)} %pad_maximum_fusion.15), channel_id=1, source_target_pairs={{0,4},{2,6},{4,0},{6,2},{8,12},{10,14},{12,8},{14,10},{16,20},{18,... | collective-permute-start | bytes 49160 | tf_op jit(solution)/shard_map/ppermute | solution.py:50
  69.5 3.0 %collective-permute-start.23 = (f32[4,8,128]{2,1,0:T(8,128)S(1)}, f32[4,8,128]{2,1,0:T(8,128)S(1)}, u32[]{:S(2)}, u32[]{:S(2)}) collective-permute-start(f32[4,8,128]{2,1,0:T(8,128)S(1)} %get-tuple-element.174), channel_id=1, source_target_pairs={{0,2},{2,0},{4,6},{6,4},{8,16},{10,18},{12,20},{14,22},{16,8},{18,... | collective-permute-start | bytes 49160 | tf_op jit(solution)/shard_map/ppermute | solution.py:69
  69.6 4.6 %collective-permute-start.22 = (f32[4,8,128]{2,1,0:T(8,128)S(1)}, f32[4,8,128]{2,1,0:T(8,128)S(1)}, u32[]{:S(2)}, u32[]{:S(2)}) collective-permute-start(f32[4,8,128]{2,1,0:T(8,128)S(1)} %get-tuple-element.175), channel_id=1, source_target_pairs={{0,8},{2,10},{4,12},{6,14},{8,0},{10,2},{12,4},{14,6},{16,24},{18,... | collective-permute-start | bytes 49160 | tf_op jit(solution)/shard_map/ppermute | solution.py:50

commit v3 on v2

--- a/solution.py
+++ b/solution.py
@@ -29,47 +29,36 @@
 def place(me, shift):
     origin = me - shift
     k = jnp.bitwise_xor(origin, me) & 3
-    core, side, odd = me & 1, (me >> 1) & 1, (me >> 2) & 1
+    odd = (me >> 2) & 1
     apart = (origin >> 2) - (me >> 2)
-    here = jnp.where(k == 1, 1 + core, jnp.where(k == 2, 5 - side, 7 - side))
-    below = jnp.where(odd == 1, 8, 12) + k
-    above = jnp.where(odd == 1, 12, 8) + k
+    here = 2 * (k - 1) + (1 if shift > 0 else 0)
+    below = jnp.where(odd == 1, 6, 10) + k
+    above = jnp.where(odd == 1, 10, 6) + k
     return jnp.where(apart == 0, here, jnp.where(apart < 0, below, above))
 
 
-def exchange(odd, even, work=None):
+PLACES = 14
+
+
+def exchange(pairs, ends, work):
     me = lax.axis_index("dom")
     devices = range(lax.axis_size("dom"))
-    core_zero = me % 2 == 0
     group_even = (me // 4) % 2 == 0
 
-    def partner(i, flip):
+    def partner(i):
         j = (i // 4 + (1 if (i // 4) % 2 == 1 else -1)) * 4 + i % 4
         return j if j in devices else i ^ 1
 
-    flip = lambda x, bit: lax.ppermute(x, "dom", [(i, i ^ bit) for i in devices])
-    near = flip(odd, 1)
-    side = flip(
-        jnp.stack(
-            [
-                even[2],
-                even[1],
-                jnp.where(core_zero, near[2], near[3]),
-                jnp.where(core_zero, near[0], near[1]),
-            ]
-        ),
-        2,
-    )
-    done = None
-    if work is not None:
-        side, done = lax.optimization_barrier((side, work(near)))
-    up = jnp.stack([even[3], near[3], side[0], side[2]])
-    down = jnp.stack([even[0], near[0], side[1], side[3]])
+    flip = lambda x, bits: lax.ppermute(x, "dom", [(i, i ^ bits) for i in devices])
+    near = [flip(pairs[k - 1], k) for k in (1, 2, 3)]
+    near, done = lax.optimization_barrier((near, work()))
+    up = jnp.stack([ends[1], *(x[1] for x in near)])
+    down = jnp.stack([ends[0], *(x[0] for x in near)])
     first = flip(jnp.where(group_even, up, down), 4)
     second = lax.ppermute(
-        jnp.where(group_even, down, up), "dom", [(i, partner(i, 1)) for i in devices]
-    )
-    return (near, side, first, second), done
+        jnp.where(group_even, down, up), "dom", [(i, partner(i)) for i in devices]
+    )
+    return (*near, first, second), done
 
 
 def call(kernel, out_shape, scratch, smem, vmem, flops, moved, hbm=(), smem_out=False, after=()):
@@ -113,17 +102,28 @@
     return [offset_of(o, reach) for o in range(2 * reach)]
 
 
-def send_items(odd_ref, even_ref, reach, width, sign, item):
-    ways = offsets(reach)
-    odds = [f for f in ways if f % 2]
-    evens = [f for f in ways if f % 2 == 0]
-    for o, f in enumerate(ways):
+def send_items(pairs, ends_ref, reach, sign, item):
+    core = lax.axis_index("dom") & 1
+    for o, f in enumerate(offsets(reach)):
         shift = sign * f
-        ref, at = (odd_ref, odds.index(shift)) if shift % 2 else (even_ref, evens.index(shift))
+        side = 1 if shift > 0 else 0
+        if abs(shift) == reach:
+            item(o, ends_ref, (side,))
+        elif shift % 2 == 0:
+            item(o, pairs, (1, side))
+        else:
+            first = shift in (-3, 1)
+            item(o, pairs, (2 * core if first else 2 - 2 * core, side))
+
+
+def send_slots(width, source):
+    def item(o, ref, at):
         for m in range(width):
-            piece = item(o, m)
+            piece = source(o, m)
             rows = piece.shape[0]
-            ref[at, m * rows : (m + 1) * rows] = piece
+            ref[(*at, slice(m * rows, (m + 1) * rows))] = piece
+
+    return item
 
 
 def collect(all_ref, parts):
@@ -215,7 +215,7 @@
 
 
 def first_kernel(
-    reach, width, send_hbm, term_hbm, z_ref, split_ref, odd_ref, even_ref, send_ref, term_ref, sem, small
+    reach, width, send_hbm, term_hbm, z_ref, split_ref, pairs_ref, ends_ref, send_ref, term_ref, sem, small
 ):
     blocks, _, lanes = z_ref.shape
     parts = sem.shape[0]
@@ -235,7 +235,9 @@
             z_ref[k] = z
             store_split(split_ref, k, z)
     asked.wait()
-    send_items(odd_ref, even_ref, reach, width, 1, lambda o, m: z_ref[send_ref[m, o]])
+    send_items(
+        pairs_ref, ends_ref, reach, 1, send_slots(width, lambda o, m: z_ref[send_ref[m, o]])
+    )
 
 
 def near_products(plan, plan_ref, w_ref, split_ref, sum_ref, forward):
@@ -293,14 +295,14 @@
 
 def backup_kernel(
     plan, reach, width, plan_ref, w_ref, part_ref, growth_ref,
-    near_ref, side_ref, first_ref, second_ref,
-    z_ref, next_ref, odd_ref, even_ref, all_ref, ext_ref, sum_ref,
+    got1, got2, got3, got4, got5,
+    z_ref, next_ref, pairs_ref, ends_ref, all_ref, ext_ref, sum_ref,
 ):
     blocks, rows, lanes = z_ref.shape
     me = lax.axis_index("dom")
     backed_up(
         plan, reach, width, plan_ref, w_ref, part_ref,
-        (near_ref, side_ref, first_ref, second_ref), all_ref, ext_ref, sum_ref,
+        (got1, got2, got3, got4, got5), all_ref, ext_ref, sum_ref,
     )
     dest = goal_of(plan, plan_ref, rows, lanes)
     for k in range(blocks):
@@ -308,8 +310,8 @@
         z_ref[k] = z
         store_split(next_ref, k, z)
     send_items(
-        odd_ref, even_ref, reach, width, 1,
-        lambda o, m: z_ref[plan_ref[plan.send + o * width + m]],
+        pairs_ref, ends_ref, reach, 1,
+        send_slots(width, lambda o, m: z_ref[plan_ref[plan.send + o * width + m]]),
     )
 
 
@@ -327,24 +329,26 @@
 
 def turn_kernel(
     plan, reach, width, plan_ref, w_ref, part_ref, growth_ref,
-    near_ref, side_ref, first_ref, second_ref, start_ref,
-    values_ref, next_ref, odd_ref, even_ref, all_ref, ext_ref, sum_ref, flow_ref,
+    got1, got2, got3, got4, got5, start_ref,
+    z_ref, next_ref, pairs_ref, ends_ref, all_ref, ext_ref, sum_ref, flow_ref,
 ):
     blocks = plan.blocks
     _, rows, lanes = part_ref.shape
     me = lax.axis_index("dom")
     backed_up(
         plan, reach, width, plan_ref, w_ref, part_ref,
-        (near_ref, side_ref, first_ref, second_ref), all_ref, ext_ref, sum_ref,
+        (got1, got2, got3, got4, got5), all_ref, ext_ref, sum_ref,
     )
     dest = goal_of(plan, plan_ref, rows, lanes)
     for k in range(blocks):
         z = with_goal(k, blocks, growth_ref, sum_ref, dest, me)
         span = slice(k * lanes, (k + 1) * lanes)
-        values_ref[:, span] = jnp.log(z)
+        z_ref[k] = z
         store_split(next_ref, k, growth_ref[k] * start_ref[:, span].astype(jnp.float32) / z)
     far_flows(plan, plan_ref, w_ref, next_ref, flow_ref)
-    send_items(odd_ref, even_ref, reach, width, -1, lambda o, m: flow_ref[o * width + m])
+    send_items(
+        pairs_ref, ends_ref, reach, -1, send_slots(width, lambda o, m: flow_ref[o * width + m])
+    )
 
 
 def flows(
@@ -370,42 +374,41 @@
 
 def spread_kernel(
     plan, count, reach, width, plan_ref, w_ref, growth_ref, sum_ref,
-    near_ref, side_ref, first_ref, second_ref,
-    u_ref, next_ref, odd_ref, even_ref, all_ref, flow_ref,
+    got1, got2, got3, got4, got5,
+    u_ref, next_ref, pairs_ref, ends_ref, all_ref, flow_ref,
 ):
     flows(
         plan, count, reach, width, plan_ref, w_ref, growth_ref, sum_ref,
-        (near_ref, side_ref, first_ref, second_ref), u_ref, next_ref, all_ref, flow_ref,
-    )
-    send_items(odd_ref, even_ref, reach, width, -1, lambda o, m: flow_ref[o * width + m])
+        (got1, got2, got3, got4, got5), u_ref, next_ref, all_ref, flow_ref,
+    )
+    send_items(
+        pairs_ref, ends_ref, reach, -1, send_slots(width, lambda o, m: flow_ref[o * width + m])
+    )
 
 
 def last_kernel(
     plan, count, reach, width, plan_ref, w_ref, growth_ref, sum_ref,
-    near_ref, side_ref, first_ref, second_ref, z_near_ref, z_side_ref, z_first_ref, z_second_ref,
-    u_ref, next_ref, odd_ref, even_ref, all_ref, flow_ref, far_ref,
+    got1, got2, got3, got4, got5, z1_got, z2_got, z3_got, z4_got, z5_got,
+    u_ref, next_ref, pairs_ref, ends_ref, all_ref, flow_ref, far_ref,
 ):
     rows = u_ref.shape[1]
     me = lax.axis_index("dom")
     flows(
         plan, count, reach, width, plan_ref, w_ref, growth_ref, sum_ref,
-        (near_ref, side_ref, first_ref, second_ref), u_ref, next_ref, all_ref, flow_ref,
-    )
-    collect(far_ref, (z_near_ref, z_side_ref, z_first_ref, z_second_ref))
-    ways = offsets(reach)
-    odds = [f for f in ways if f % 2]
-    evens = [f for f in ways if f % 2 == 0]
-    row = lax.broadcasted_iota(jnp.int32, odd_ref.shape[1:], 0)
-    for o, f in enumerate(ways):
-        at = place(me, f)
-        item = jnp.zeros(odd_ref.shape[1:], jnp.float32)
+        (got1, got2, got3, got4, got5), u_ref, next_ref, all_ref, flow_ref,
+    )
+    collect(far_ref, (z1_got, z2_got, z3_got, z4_got, z5_got))
+    row = lax.broadcasted_iota(jnp.int32, ends_ref.shape[1:], 0)
+
+    def item(o, ref, where):
+        at = place(me, offset_of(o, reach))
+        sums = jnp.zeros(ends_ref.shape[1:], jnp.float32)
         for m in range(width):
             lost = far_ref[at, m * rows : (m + 1) * rows] * flow_ref[o * width + m]
-            item = jnp.where(row == m, jnp.sum(lost, axis=0, keepdims=True), item)
-        if f % 2:
-            odd_ref[odds.index(-f)] = item
-        else:
-            even_ref[evens.index(-f)] = item
+            sums = jnp.where(row == m, jnp.sum(lost, axis=0, keepdims=True), sums)
+        ref[where] = sums
+
+    send_items(pairs_ref, ends_ref, reach, -1, item)
 
 
 def node_kernel(
@@ -426,11 +429,11 @@
 
 def gradient_kernel(
     plan, count, reach, width, scale, plan_ref, v_ref, f_ref, act_ref, node_ref,
-    near_ref, side_ref, first_ref, second_ref, grad_ref, total_ref, all_ref,
+    got1, got2, got3, got4, got5, packed_ref, total_ref, all_ref,
 ):
     blocks, _, lanes = node_ref.shape
     me = lax.axis_index("dom")
-    collect(all_ref, (near_ref, side_ref, first_ref, second_ref))
+    collect(all_ref, (got1, got2, got3, got4, got5))
     for k in range(blocks):
         total_ref[k] = node_ref[k]
     for o, f in enumerate(offsets(reach)):
@@ -465,25 +468,55 @@
             jnp.concatenate(lows, axis=1), f, NN, preferred_element_type=jnp.float32
         )
     v = v_ref[...]
+    core = me & 1
+    half = packed_ref.shape[1]
     parts = hidden // lanes
+    tall = hidden * f_ref.shape[1] // lanes
+
+    def put(at, rows):
+        packed_ref[jnp.bitwise_xor(core, at // half), at % half : at % half + rows.shape[0]] = rows
+
     for j in range(parts):
         span = slice(j * lanes, (j + 1) * lanes)
         turned = grad[span].T * v[:, span]
         for i in range(f_ref.shape[1] // 8):
-            at = (i * parts + j) * 8
-            grad_ref[at : at + 8] = turned[i * 8 : (i + 1) * 8]
+            put((i * parts + j) * 8, turned[i * 8 : (i + 1) * 8])
     ones = jnp.ones((8, lanes), jnp.float32)
     across = lambda x: lax.dot_general(
         ones, x, NT, precision=lax.Precision.HIGHEST, preferred_element_type=jnp.float32
     )[:1]
-    bias = across(bias_sum) * v
-    out = across(out_sum)
-    at = hidden * f_ref.shape[1] // lanes
-    for j in range(parts):
-        span = slice(j * lanes, (j + 1) * lanes)
-        grad_ref[at + j : at + j + 1] = bias[:, span]
-        grad_ref[at + parts + j : at + parts + j + 1] = out[:, span]
-    grad_ref[at + 2 * parts :] = jnp.zeros_like(grad_ref[at + 2 * parts :])
+    bias, out = across(bias_sum) * v, across(out_sum)
+    cut = lambda x: [x[:, j * lanes : (j + 1) * lanes] for j in range(parts)]
+    put(tall, jnp.concatenate(cut(bias) + cut(out), axis=0))
+    for at in range(tall + 2 * parts, 2 * half, 8):
+        put(at, jnp.zeros((8, lanes), jnp.float32))
+
+
+def finish_kernel(mine_ref, other_ref, grad_hbm, bias_hbm, out_hbm, both_ref, bias_ref, out_ref, sem):
+    half = mine_ref.shape[0]
+    tall, parts = grad_hbm.shape[0], bias_hbm.shape[0]
+    core = lax.axis_index("dom") & 1
+    both_ref[core] = mine_ref[...]
+    both_ref[1 - core] = other_ref[...]
+    which, at = tall // half, tall % half
+    bias_ref[...] = both_ref[which, at : at + parts]
+    out_ref[...] = both_ref[which, at + parts : at + 2 * parts]
+    pieces = [(bias_ref, bias_hbm), (out_ref, out_hbm)]
+    for h in range(2):
+        start, stop = h * half, min((h + 1) * half, tall)
+        if start < stop:
+            pieces.append((both_ref.at[h, : stop - start], grad_hbm.at[start:stop]))
+    copies = [pltpu.make_async_copy(src, dst, sem.at[k]) for k, (src, dst) in enumerate(pieces)]
+    for copy in copies:
+        copy.start()
+    for copy in copies:
+        copy.wait()
+
+
+def values_kernel(z_ref, values_ref):
+    blocks, _, lanes = z_ref.shape
+    for k in range(blocks):
+        values_ref[:, k * lanes : (k + 1) * lanes] = jnp.log(z_ref[k])
 
 
 def local(
@@ -509,9 +542,9 @@
     field = shape(blocks, rows, lanes)
     padded = shape(blocks + 1, rows, lanes)
     halves = jax.ShapeDtypeStruct((blocks, 2 * rows, lanes), bf16)
-    parcel = shape(reach, width * rows, lanes)
-    small = shape(reach, 8, lanes)
-    all_s = pltpu.VMEM((4 * reach, width * rows, lanes), f32)
+    parcels = (shape(3, 2, width * rows, lanes), shape(2, width * rows, lanes))
+    smalls = (shape(3, 2, 8, lanes), shape(2, 8, lanes))
+    all_s = pltpu.VMEM((PLACES, width * rows, lanes), f32)
     ext_s = pltpu.VMEM((slots, 2 * rows, lanes), bf16)
     sum_s = pltpu.VMEM((blocks + 1, rows, lanes), f32)
     flow_s = pltpu.VMEM((slots + 1, rows, lanes), f32)
@@ -521,9 +554,9 @@
     send_t = send_blocks.T
     row_b = b_input[None, :]
 
-    z0, split, odd, even = call(
+    z0, split, pairs, ends = call(
         bind(first_kernel),
-        (field, halves, parcel, parcel),
+        (field, halves, *parcels),
         [
             pltpu.SMEM(send_t.shape, jnp.int32),
             pltpu.VMEM(terminal.shape, f32),
@@ -537,7 +570,7 @@
         hbm=(send_t, terminal),
     )
 
-    def load(arrived):
+    def load():
         return call(
             functools.partial(load_kernel, plan),
             (
@@ -558,14 +591,14 @@
             moved,
             hbm=(tile_rows, tile_cols, send_t, dest_nodes, tile_weight, features, w_input, row_b, row_v),
             smem_out=True,
-            after=(arrived,),
-        )
-
-    far, (plans, weight, feature, w_in, b_in, v_out) = exchange(odd, even, load)
-
-    def near(split, forward, *after):
+            after=(ends,),
+        )
+
+    far, (plans, weight, feature, w_in, b_in, v_out) = exchange(pairs, ends, load)
+
+    def near(split, forward):
         kernel = functools.partial(near_kernel, plan, forward)
-        return call(kernel, padded, [], (plans,), (weight, split), flops, moved, after=after)
+        return call(kernel, padded, [], (plans,), (weight, split), flops, moved)
 
     act, growth = call(
         network_kernel,
@@ -580,7 +613,7 @@
     def backup(part, got):
         return call(
             bind(backup_kernel, plan),
-            (field, halves, parcel, parcel),
+            (field, halves, *parcels),
             [all_s, ext_s, sum_s],
             (plans,),
             (weight, part, growth, *got),
@@ -588,33 +621,34 @@
             moved,
         )
 
-    z1, split, odd, even = backup(near(split, True), far)
-    got, part = exchange(odd, even, lambda arrived: near(split, True, arrived))
-    z2, split2, odd, even = backup(part, got)
-    got, part = exchange(odd, even, lambda arrived: near(split2, True, arrived))
-    values, split3, odd, even = call(
+    z1, split, pairs, ends = backup(near(split, True), far)
+    got, part = exchange(pairs, ends, lambda: near(split, True))
+    z2, split2, pairs, ends = backup(part, got)
+    got, part = exchange(pairs, ends, lambda: near(split2, True))
+    z3, split3, pairs, ends = call(
         bind(turn_kernel, plan),
-        (shape(rows, nodes), halves, parcel, parcel),
+        (field, halves, *parcels),
         [all_s, ext_s, sum_s, flow_s],
         (plans,),
         (weight, part, growth, *got, start_counts),
         2 * flops,
         moved,
     )
-    got, part = exchange(odd, even, lambda arrived: near(split3, False, arrived))
-    u1, split4, odd, even = call(
+    values = call(values_kernel, shape(rows, nodes), [], (), (z3,), flops // 8, nodes * rows * 8)
+    got, part = exchange(pairs, ends, lambda: near(split3, False))
+    u1, split4, pairs, ends = call(
         bind(spread_kernel, plan, count),
-        (field, halves, parcel, parcel),
+        (field, halves, *parcels),
         [all_s, flow_s],
         (plans,),
         (weight, growth, part, *got),
         flops,
         moved,
     )
-    got, part = exchange(odd, even, lambda arrived: near(split4, False, arrived))
-    u2, split5, odd, even = call(
+    got, part = exchange(pairs, ends, lambda: near(split4, False))
+    u2, split5, pairs, ends = call(
         bind(last_kernel, plan, count),
-        (field, halves, small, small),
+        (field, halves, *smalls),
         [all_s, flow_s, all_s],
         (plans,),
         (weight, growth, part, *got, *far),
@@ -622,9 +656,9 @@
         moved,
     )
     got, node = exchange(
-        odd,
-        even,
-        lambda arrived: call(
+        pairs,
+        ends,
+        lambda: call(
             functools.partial(node_kernel, plan),
             shape(blocks, 1, lanes),
             [sum_s],
@@ -632,30 +666,52 @@
             (weight, split5, z0, z1, z2, u1, u2, visit_counts),
             flops,
             moved,
-            after=(arrived,),
         ),
     )
     every = ("dest", "dom")
     members = count * lax.axis_size("dest")
-    used = hidden * feat // lanes + 2 * hidden // lanes
-    share = -(-used // members)
+    tall = hidden * feat // lanes
+    share = -(-(tall + 2 * hidden // lanes) // members)
+    half = share * members // 2
     scale = 1.0 / math.sqrt(nodes * count * rows * lax.axis_size("dest"))
     packed = call(
         functools.partial(gradient_kernel, plan, count, reach, width, scale),
-        shape(share * members, lanes),
-        [pltpu.VMEM((blocks, 1, lanes), f32), pltpu.VMEM((4 * reach, 8, lanes), f32)],
+        shape(2, half, lanes),
+        [
+            pltpu.VMEM((blocks, 1, lanes), f32),
+            pltpu.VMEM((PLACES, 8, lanes), f32),
+        ],
         (plans,),
         (v_out, feature, act, node, *got),
         4 * nodes * hidden * feat,
         nodes * hidden * 4,
     )
-    packed = packed.reshape(members, 1, share * lanes)
-    mine = lax.all_to_all(packed, every, 0, 0, tiled=True).sum(axis=0, keepdims=True)
-    spread = jnp.broadcast_to(mine, packed.shape)
-    summed = lax.all_to_all(spread, every, 0, 0, tiled=True).reshape(share * members, lanes)
-    side = summed[hidden * feat // lanes : used].reshape(2, hidden)
-    grad = summed[: hidden * feat // lanes].reshape(feat // 8, hidden // lanes, 8, lanes)
-    return values, grad.transpose(0, 2, 1, 3).reshape(feat, hidden), side[0], side[1]
+    twins = [(i, i ^ 1) for i in range(count)]
+    mine = packed[0] + lax.ppermute(packed[1], "dom", twins)
+    same_core = [[i for i in range(members) if i % 2 == core] for core in range(2)]
+    swap = lambda x: lax.all_to_all(x, every, 0, 0, tiled=True, axis_index_groups=same_core)
+    mine = mine.reshape(members // 2, 1, share * lanes)
+    mine = jnp.broadcast_to(swap(mine).sum(axis=0, keepdims=True), mine.shape)
+    mine = swap(mine).reshape(half, lanes)
+    other = lax.ppermute(mine, "dom", twins)
+    in_hbm = pl.BlockSpec(memory_space=pltpu.HBM)
+    in_vmem = pl.BlockSpec(memory_space=pltpu.VMEM)
+    parts = hidden // lanes
+    grad, bias, out = pl.pallas_call(
+        finish_kernel,
+        out_shape=(shape(tall, lanes), shape(parts, lanes), shape(parts, lanes)),
+        in_specs=[in_vmem] * 2,
+        out_specs=[in_hbm] * 3,
+        scratch_shapes=[
+            pltpu.VMEM((2, half, lanes), f32),
+            pltpu.VMEM((parts, lanes), f32),
+            pltpu.VMEM((parts, lanes), f32),
+            pltpu.SemaphoreType.DMA((4,)),
+        ],
+        compiler_params=pltpu.CompilerParams(vmem_limit_bytes=VMEM_GRANT),
+    )(mine, other)
+    grad = grad.reshape(feat // 8, parts, 8, lanes).transpose(0, 2, 1, 3).reshape(feat, hidden)
+    return values, grad, bias.reshape(-1), out.reshape(-1)
 
 
 def solution(mesh):

time: 108 us -> 98.3 us (0.910)
  waiting for transfers between devices: 23.8 us -> 17.9 us
  blocking collectives: 28.1 us -> 23.1 us
  local copies, waits for them, and re-layouts: 1.53 us -> 0.22 us
  Pallas kernels: 25.6 us -> 26.7 us
    ppermute x24 -> x32, waiting for transfers between devices: 23.8 us -> 17.9 us  [the longest x24 15.9 us: exchange(): lax.ppermute(x, 'dom', [(i, i ^ bits) for i in devices])]
    all_to_all x2, blocking collectives: 28.1 us -> 23.1 us  [local(): lax.all_to_all(x, every, 0, 0, tiled=True, axis_index_groups=same_core)]
    ppermute x24 -> x32, starting transfers between devices: 27.9 us -> 28.8 us  [the longest x24 28 us: exchange(): lax.ppermute(x, 'dom', [(i, i ^ bits) for i in devices])]
    pallas_call x15 -> x16, Pallas kernels: 25.6 us -> 25.9 us  [call(): pl.pallas_call(kernel, out_shape=out_shape, in_specs=[space(pltpu.HBM)] *...]
  transfers between devices with their start and end apart: 24 -> 32, of which waited for: 16 -> 15; matrix products, arithmetic and copies ran while one was open for 0% -> 0% of each run, Pallas kernels for 13% -> 16%
where the time goes in v3:
time: 98.3 us; the launch traced here: 98.1 us
  starting transfers between devices  28.8 us (29%)
  Pallas kernels  26.7 us (27%)
  blocking collectives  23.1 us (23%)
  waiting for transfers between devices  17.9 us (18%)
  between operations  1.2 us (1%)
    ppermute x24, starting transfers between devices, exchange(): lax.ppermute(x, 'dom', [(i, i ^ bits) for i in devices])  28 us
    pallas_call x16, Pallas kernels, call(): pl.pallas_call(kernel, out_shape=out_shape, in_specs=[space(pltpu.HBM)] *...  25.9 us
    all_to_all x2, blocking collectives, local(): lax.all_to_all(x, every, 0, 0, tiled=True, axis_index_groups=same_core)  23.1 us
    ppermute x24, waiting for transfers between devices, exchange(): lax.ppermute(x, 'dom', [(i, i ^ bits) for i in devices])  15.9 us
  transfers between devices with their start and end apart: 32, of which 15 were waited for; matrix products, arithmetic and copies ran while one was open for 0% of the time, Pallas kernels for 16%

profile of v3, /device:TPU:0, one launch (start us, length us, event | category | flops | bytes accessed | tf_op | source)
XLA Modules:
  0.0 98.1 jit_solution(13577627427261339166)
XLA Ops:
  0.6 1.0 %shard_map.147 = (f32[32,16,128]{2,1,0:T(8,128)S(1)}, bf16[32,32,128]{2,1,0:T(8,128)(2,1)S(1)}, f32[3,2,32,128]{3,2,1,0:T(8,128)S(1)}, f32[2,32,128]{2,1,0:T(8,128)S(1)}) custom-call(s32[2,8]{1,0:T(2,128)} %bitcast.59, f32[16,4096]{1,0:T(8,128)} %term_hbm.1), custom_call_target="tpu_custom_call" | custom-call | flops 83886080 | bytes 2621440 | tf_op jit(solution)/shard_map/pallas_call | solution.py:73
  1.7 2.5 %collective-permute-start.2 = (f32[2,32,128]{2,1,0:T(8,128)S(1)}, f32[2,32,128]{2,1,0:T(8,128)S(1)}, u32[]{:S(2)}, u32[]{:S(2)}) collective-permute-start(f32[2,32,128]{2,1,0:T(8,128)S(1)} %get-tuple-element.154), channel_id=1, source_target_pairs={{0,6},{2,4},{4,2},{6,0},{8,14},{10,12},{12,10},{14,8},{16,22},{18,... | collective-permute-start | bytes 98312 | tf_op jit(solution)/shard_map/ppermute | solution.py:52
  4.9 2.8 %shard_map.148 = (s32[226]{0:T(256)S(1)}, bf16[80,128,128]{2,1,0:T(8,128)(2,1)S(1)}, bf16[4096,128]{1,0:T(8,128)(2,1)S(1)}, bf16[128,512]{1,0:T(8,128)(2,1)S(1)}...) custom-call(s32[80]{0:T(128)} %refs_0_.1, s32[80]{0:T(128)} %refs_1_.1, s32[2,8]{1,0:T(2,128)} %bitcast.60, s32[16]{0:T(128)} %refs_3_.1, ...), custom_call_target="tpu_custom_call" | custom-call | flops 83886080 | bytes 2621440 | tf_op jit(solution)/shard_map/pallas_call | solution.py:73
  8.3 3.1 %collective-permute-start.3 = (f32[4,32,128]{2,1,0:T(8,128)S(1)}, f32[4,32,128]{2,1,0:T(8,128)S(1)}, u32[]{:S(2)}, u32[]{:S(2)}) collective-permute-start(f32[4,32,128]{2,1,0:T(8,128)S(1)} %get-tuple-element.141), channel_id=1, source_target_pairs={{0,8},{2,10},{4,12},{6,14},{8,0},{10,2},{12,4},{14,6},{16,24},{18,... | collective-permute-start | bytes 196616 | tf_op jit(solution)/shard_map/ppermute | solution.py:52
  11.4 2.0 %shard_map.149.part_ref = f32[33,16,128]{2,1,0:T(8,128)S(1)} custom-call(s32[226]{0:T(256)S(1)} %get-tuple-element.76.plan_ref, bf16[80,128,128]{2,1,0:T(8,128)(2,1)S(1)} %get-tuple-element.77.w_ref, bf16[32,32,128]{2,1,0:T(8,128)(2,1)S(1)} %get-tuple-element.78.split_ref), custom_call_target="tpu_custom_call" | custom-call | flops 83886080 | bytes 2621440 | tf_op jit(solution)/shard_map/pallas_call | solution.py:73
  13.4 1.4 %shard_map.150 = (f32[512,4096]{1,0:T(8,128)S(1)}, f32[32,1,128]{2,1,0:T(1,128)S(1)}) custom-call(bf16[128,512]{1,0:T(8,128)(2,1)S(1)} %get-tuple-element.79.w_ref, f32[1,512]{1,0:T(1,128)S(1)} %get-tuple-element.80.b_ref, f32[1,512]{1,0:T(1,128)S(1)} %get-tuple-element.81.v_ref, bf16[4096,128]{1,0:T(8,128)(2,1)S(1)} %get-tuple-element.82.f_ref), custom_call_target="tpu_custom_call" | custom-call | flops 536870912 | bytes 8388608 | tf_op jit(solution)/shard_map/pallas_call | solution.py:73
  14.9 1.0 %shard_map.151 = (f32[32,16,128]{2,1,0:T(8,128)S(1)}, bf16[32,32,128]{2,1,0:T(8,128)(2,1)S(1)}, f32[3,2,32,128]{3,2,1,0:T(8,128)S(1)}, f32[2,32,128]{2,1,0:T(8,128)S(1)}) custom-call(s32[226]{0:T(256)S(1)} %get-tuple-element.76.plan_ref, bf16[80,128,128]{2,1,0:T(8,128)(2,1)S(1)} %get-tuple-element.77.w_ref, f32[33,16,128]{2,1,0:T(8,128)S(1)} %shard_map.149.part_ref, ...), custom_call_target="tpu_custom_call" | custom-call | flops 83886080 | bytes 2621440 | tf_op jit(solution)/shard_map/pallas_call | solution.py:73
  17.9 2.0 %shard_map.152.part_ref = f32[33,16,128]{2,1,0:T(8,128)S(1)} custom-call(s32[226]{0:T(256)S(1)} %get-tuple-element.76.plan_ref, bf16[80,128,128]{2,1,0:T(8,128)(2,1)S(1)} %get-tuple-element.77.w_ref, bf16[32,32,128]{2,1,0:T(8,128)(2,1)S(1)} %get-tuple-element.88.split_ref), custom_call_target="tpu_custom_call" | custom-call | flops 83886080 | bytes 2621440 | tf_op jit(solution)/shard_map/pallas_call | solution.py:73
  21.0 1.8 %collective-permute-start.8 = (f32[4,32,128]{2,1,0:T(8,128)S(1)}, f32[4,32,128]{2,1,0:T(8,128)S(1)}, u32[]{:S(2)}, u32[]{:S(2)}) collective-permute-start(f32[4,32,128]{2,1,0:T(8,128)S(1)} %get-tuple-element.139), channel_id=1, source_target_pairs={{0,8},{2,10},{4,12},{6,14},{8,0},{10,2},{12,4},{14,6},{16,24},{18,... | collective-permute-start | bytes 196616 | tf_op jit(solution)/shard_map/ppermute | solution.py:52
  22.8 2.6 %collective-permute-done.8.got4 = f32[4,32,128]{2,1,0:T(8,128)S(1)} collective-permute-done((f32[4,32,128]{2,1,0:T(8,128)S(1)}, f32[4,32,128]{2,1,0:T(8,128)S(1)}, u32[]{:S(2)}, u32[]{:S(2)}) %collective-permute-start.8) | collective-permute-done | bytes 65568 | tf_op jit(solution)/shard_map/ppermute | solution.py:52
  25.4 1.0 %shard_map.153 = (f32[32,16,128]{2,1,0:T(8,128)S(1)}, bf16[32,32,128]{2,1,0:T(8,128)(2,1)S(1)}, f32[3,2,32,128]{3,2,1,0:T(8,128)S(1)}, f32[2,32,128]{2,1,0:T(8,128)S(1)}) custom-call(s32[226]{0:T(256)S(1)} %get-tuple-element.76.plan_ref, bf16[80,128,128]{2,1,0:T(8,128)(2,1)S(1)} %get-tuple-element.77.w_ref, f32[33,16,128]{2,1,0:T(8,128)S(1)} %shard_map.152.part_ref, ...), custom_call_target="tpu_custom_call" | custom-call | flops 83886080 | bytes 2621440 | tf_op jit(solution)/shard_map/pallas_call | solution.py:73
  26.5 1.2 %collective-permute-start.11 = (f32[2,32,128]{2,1,0:T(8,128)S(1)}, f32[2,32,128]{2,1,0:T(8,128)S(1)}, u32[]{:S(2)}, u32[]{:S(2)}) collective-permute-start(f32[2,32,128]{2,1,0:T(8,128)S(1)} %get-tuple-element.149), channel_id=1, source_target_pairs={{0,4},{2,6},{4,0},{6,2},{8,12},{10,14},{12,8},{14,10},{16,20},{18,... | collective-permute-start | bytes 98312 | tf_op jit(solution)/shard_map/ppermute | solution.py:52
  28.4 2.0 %shard_map.154.part_ref = f32[33,16,128]{2,1,0:T(8,128)S(1)} custom-call(s32[226]{0:T(256)S(1)} %get-tuple-element.76.plan_ref, bf16[80,128,128]{2,1,0:T(8,128)(2,1)S(1)} %get-tuple-element.77.w_ref, bf16[32,32,128]{2,1,0:T(8,128)(2,1)S(1)} %get-tuple-element.95.split_ref), custom_call_target="tpu_custom_call" | custom-call | flops 83886080 | bytes 2621440 | tf_op jit(solution)/shard_map/pallas_call | solution.py:73
  30.8 1.8 %collective-permute-start.13 = (f32[4,32,128]{2,1,0:T(8,128)S(1)}, f32[4,32,128]{2,1,0:T(8,128)S(1)}, u32[]{:S(2)}, u32[]{:S(2)}) collective-permute-start(f32[4,32,128]{2,1,0:T(8,128)S(1)} %get-tuple-element.137), channel_id=1, source_target_pairs={{0,8},{2,10},{4,12},{6,14},{8,0},{10,2},{12,4},{14,6},{16,24},{18,... | collective-permute-start | bytes 196616 | tf_op jit(solution)/shard_map/ppermute | solution.py:52
  32.5 2.7 %collective-permute-done.13.got4 = f32[4,32,128]{2,1,0:T(8,128)S(1)} collective-permute-done((f32[4,32,128]{2,1,0:T(8,128)S(1)}, f32[4,32,128]{2,1,0:T(8,128)S(1)}, u32[]{:S(2)}, u32[]{:S(2)}) %collective-permute-start.13) | collective-permute-done | bytes 65568 | tf_op jit(solution)/shard_map/ppermute | solution.py:52
  35.3 1.3 %shard_map.155 = (f32[32,16,128]{2,1,0:T(8,128)S(1)}, bf16[32,32,128]{2,1,0:T(8,128)(2,1)S(1)}, f32[3,2,32,128]{3,2,1,0:T(8,128)S(1)}, f32[2,32,128]{2,1,0:T(8,128)S(1)}) custom-call(s32[226]{0:T(256)S(1)} %get-tuple-element.76.plan_ref, bf16[80,128,128]{2,1,0:T(8,128)(2,1)S(1)} %get-tuple-element.77.w_ref, f32[33,16,128]{2,1,0:T(8,128)S(1)} %shard_map.154.part_ref, ...), custom_call_target="tpu_custom_call" | custom-call | flops 167772160 | bytes 2621440 | tf_op jit(solution)/shard_map/pallas_call | solution.py:73
  38.5 1.4 %shard_map.157.sum_ref = f32[33,16,128]{2,1,0:T(8,128)S(1)} custom-call(s32[226]{0:T(256)S(1)} %get-tuple-element.76.plan_ref, bf16[80,128,128]{2,1,0:T(8,128)(2,1)S(1)} %get-tuple-element.77.w_ref, bf16[32,32,128]{2,1,0:T(8,128)(2,1)S(1)} %get-tuple-element.104.split_ref), custom_call_target="tpu_custom_call" | custom-call | flops 83886080 | bytes 2621440 | tf_op jit(solution)/shard_map/pallas_call | solution.py:73
  40.2 1.2 %collective-permute-done.16.got2 = f32[2,32,128]{2,1,0:T(8,128)S(1)} collective-permute-done((f32[2,32,128]{2,1,0:T(8,128)S(1)}, f32[2,32,128]{2,1,0:T(8,128)S(1)}, u32[]{:S(2)}, u32[]{:S(2)}) %collective-permute-start.16) | collective-permute-done | bytes 32800 | tf_op jit(solution)/shard_map/ppermute | solution.py:52
  41.6 2.7 %collective-permute-start.18 = (f32[4,32,128]{2,1,0:T(8,128)S(1)}, f32[4,32,128]{2,1,0:T(8,128)S(1)}, u32[]{:S(2)}, u32[]{:S(2)}) collective-permute-start(f32[4,32,128]{2,1,0:T(8,128)S(1)} %get-tuple-element.135), channel_id=1, source_target_pairs={{0,8},{2,10},{4,12},{6,14},{8,0},{10,2},{12,4},{14,6},{16,24},{18,... | collective-permute-start | bytes 196616 | tf_op jit(solution)/shard_map/ppermute | solution.py:52
  44.3 2.2 %collective-permute-done.18.got4 = f32[4,32,128]{2,1,0:T(8,128)S(1)} collective-permute-done((f32[4,32,128]{2,1,0:T(8,128)S(1)}, f32[4,32,128]{2,1,0:T(8,128)S(1)}, u32[]{:S(2)}, u32[]{:S(2)}) %collective-permute-start.18) | collective-permute-done | bytes 65568 | tf_op jit(solution)/shard_map/ppermute | solution.py:52
  48.3 1.2 %collective-permute-start.20 = (f32[2,32,128]{2,1,0:T(8,128)S(1)}, f32[2,32,128]{2,1,0:T(8,128)S(1)}, u32[]{:S(2)}, u32[]{:S(2)}) collective-permute-start(f32[2,32,128]{2,1,0:T(8,128)S(1)} %get-tuple-element.144), channel_id=1, source_target_pairs={{0,2},{2,0},{4,6},{6,4},{8,10},{10,8},{12,14},{14,12},{16,18},{18,... | collective-permute-start | bytes 98312 | tf_op jit(solution)/shard_map/ppermute | solution.py:52
  49.5 1.3 %shard_map.159.sum_ref = f32[33,16,128]{2,1,0:T(8,128)S(1)} custom-call(s32[226]{0:T(256)S(1)} %get-tuple-element.76.plan_ref, bf16[80,128,128]{2,1,0:T(8,128)(2,1)S(1)} %get-tuple-element.77.w_ref, bf16[32,32,128]{2,1,0:T(8,128)(2,1)S(1)} %get-tuple-element.111.split_ref), custom_call_target="tpu_custom_call" | custom-call | flops 83886080 | bytes 2621440 | tf_op jit(solution)/shard_map/pallas_call | solution.py:73
  51.8 2.1 %collective-permute-start.23 = (f32[4,32,128]{2,1,0:T(8,128)S(1)}, f32[4,32,128]{2,1,0:T(8,128)S(1)}, u32[]{:S(2)}, u32[]{:S(2)}) collective-permute-start(f32[4,32,128]{2,1,0:T(8,128)S(1)} %get-tuple-element.133), channel_id=1, source_target_pairs={{0,8},{2,10},{4,12},{6,14},{8,0},{10,2},{12,4},{14,6},{16,24},{18,... | collective-permute-start | bytes 196616 | tf_op jit(solution)/shard_map/ppermute | solution.py:52
  53.8 2.4 %collective-permute-done.23.got4 = f32[4,32,128]{2,1,0:T(8,128)S(1)} collective-permute-done((f32[4,32,128]{2,1,0:T(8,128)S(1)}, f32[4,32,128]{2,1,0:T(8,128)S(1)}, u32[]{:S(2)}, u32[]{:S(2)}) %collective-permute-start.23) | collective-permute-done | bytes 65568 | tf_op jit(solution)/shard_map/ppermute | solution.py:52
  57.3 1.3 %collective-permute-start.26 = (f32[2,8,128]{2,1,0:T(8,128)S(1)}, f32[2,8,128]{2,1,0:T(8,128)S(1)}, u32[]{:S(2)}, u32[]{:S(2)}) collective-permute-start(f32[2,8,128]{2,1,0:T(8,128)S(1)} %get-tuple-element.200), channel_id=1, source_target_pairs={{0,4},{2,6},{4,0},{6,2},{8,12},{10,14},{12,8},{14,10},{16,20},{18,... | collective-permute-start | bytes 24584 | tf_op jit(solution)/shard_map/ppermute | solution.py:52
  59.2 1.5 %shard_map.161.node_ref = f32[32,1,128]{2,1,0:T(1,128)S(1)} custom-call(s32[226]{0:T(256)S(1)} %get-tuple-element.76.plan_ref, bf16[80,128,128]{2,1,0:T(8,128)(2,1)S(1)} %get-tuple-element.77.w_ref, bf16[32,32,128]{2,1,0:T(8,128)(2,1)S(1)} %get-tuple-element.118.split_ref, f32[32,16,128]{2,1,0:T(8,128)S(1)} %get-tuple-element.119.z0_ref, ...), custom_call_target="tpu_custom_call" | custom-call | flops 83886080 | bytes 2621440 | tf_op jit(solution)/shard_map/pallas_call | solution.py:73
  61.3 3.7 %collective-permute-start.28 = (f32[4,8,128]{2,1,0:T(8,128)S(1)}, f32[4,8,128]{2,1,0:T(8,128)S(1)}, u32[]{:S(2)}, u32[]{:S(2)}) collective-permute-start(f32[4,8,128]{2,1,0:T(8,128)S(1)} %get-tuple-element.158), channel_id=1, source_target_pairs={{0,8},{2,10},{4,12},{6,14},{8,0},{10,2},{12,4},{14,6},{16,24},{18,... | collective-permute-start | bytes 49160 | tf_op jit(solution)/shard_map/ppermute | solution.py:52
  65.0 1.7 %collective-permute-done.28.got4 = f32[4,8,128]{2,1,0:T(8,128)S(1)} collective-permute-done((f32[4,8,128]{2,1,0:T(8,128)S(1)}, f32[4,8,128]{2,1,0:T(8,128)S(1)}, u32[]{:S(2)}, u32[]{:S(2)}) %collective-permute-start.28) | collective-permute-done | bytes 16416 | tf_op jit(solution)/shard_map/ppermute | solution.py:52
  66.7 4.4 %shard_map.162 = f32[2,272,128]{2,1,0:T(8,128)S(1)} custom-call(s32[226]{0:T(256)S(1)} %get-tuple-element.76.plan_ref, f32[1,512]{1,0:T(1,128)S(1)} %get-tuple-element.81.v_ref, bf16[4096,128]{1,0:T(8,128)(2,1)S(1)} %get-tuple-element.82.f_ref, f32[512,4096]{1,0:T(8,128)S(1)} %get-tuple-element.102.act_ref, f32[32,1,128]{2,1,0:T(1,128)S(1)} %shard_map.161.node_ref, ...), custom_call_target="tpu_custom_call" | custom-call | flops 1073741824 | bytes 8388608 | tf_op jit(solution)/shard_map/pallas_call | solution.py:73
  71.1 1.3 %collective-permute-done.30 = f32[272,128]{1,0:T(8,128)S(1)} collective-permute-done((f32[272,128]{1,0:T(8,128)S(1)}, f32[272,128]{1,0:T(8,128)S(1)}, u32[]{:S(2)}, u32[]{:S(2)}) %collective-permute-start.30) | collective-permute-done | bytes 139296 | tf_op jit(solution)/shard_map/ppermute | solution.py:690
  72.5 12.3 %all_to_all.10 = f32[16,1,2176]{2,1,0:T(1,128)S(1)} all-to-all(f32[16,1,2176]{2,1,0:T(1,128)S(1)} %bitcast.56), channel_id=1, replica_groups={{0,4,8,12,16,20,24,28,1,5,9,13,17,21,25,29},{2,6,10,14,18,22,26,30,3,7,..., dimensions={0} | all-to-all | bytes 278528 | tf_op jit(solution)/shard_map/all_to_all | solution.py:692
  85.0 10.8 %all_to_all.11 = f32[16,1,2176]{2,1,0:T(1,128)S(1)} all-to-all(f32[16,1,2176]{2,1,0:T(1,128)S(1)} %broadcast_in_dim.14), channel_id=1, replica_groups={{0,4,8,12,16,20,24,28,1,5,9,13,17,21,25,29},{2,6,10,14,18,22,26,30,3,7,..., dimensions={0} | all-to-all | bytes 278528 | tf_op jit(solution)/shard_map/all_to_all | solution.py:692
  (94 shorter events, 15.0 us)
Async XLA Ops:
  1.7 6.0 %collective-permute-start.2 = (f32[2,32,128]{2,1,0:T(8,128)S(1)}, f32[2,32,128]{2,1,0:T(8,128)S(1)}, u32[]{:S(2)}, u32[]{:S(2)}) collective-permute-start(f32[2,32,128]{2,1,0:T(8,128)S(1)} %get-tuple-element.154), channel_id=1, source_target_pairs={{0,6},{2,4},{4,2},{6,0},{8,14},{10,12},{12,10},{14,8},{16,22},{18,... | collective-permute-start | bytes 98312 | tf_op jit(solution)/shard_map/ppermute | solution.py:52
  4.2 4.0 %collective-permute-start.1 = (f32[2,32,128]{2,1,0:T(8,128)S(1)}, f32[2,32,128]{2,1,0:T(8,128)S(1)}, u32[]{:S(2)}, u32[]{:S(2)}) collective-permute-start(f32[2,32,128]{2,1,0:T(8,128)S(1)} %get-tuple-element.155), channel_id=1, source_target_pairs={{0,4},{2,6},{4,0},{6,2},{8,12},{10,14},{12,8},{14,10},{16,20},{18,... | collective-permute-start | bytes 98312 | tf_op jit(solution)/shard_map/ppermute | solution.py:52
  4.8 3.3 %collective-permute-start = (f32[2,32,128]{2,1,0:T(8,128)S(1)}, f32[2,32,128]{2,1,0:T(8,128)S(1)}, u32[]{:S(2)}, u32[]{:S(2)}) collective-permute-start(f32[2,32,128]{2,1,0:T(8,128)S(1)} %get-tuple-element.156), channel_id=1, source_target_pairs={{0,2},{2,0},{4,6},{6,4},{8,10},{10,8},{12,14},{14,12},{16,18},{18,... | collective-permute-start | bytes 98312 | tf_op jit(solution)/shard_map/ppermute | solution.py:52
  8.2 6.7 %collective-permute-start.4 = (f32[4,32,128]{2,1,0:T(8,128)S(1)}, f32[4,32,128]{2,1,0:T(8,128)S(1)}, u32[]{:S(2)}, u32[]{:S(2)}) collective-permute-start(f32[4,32,128]{2,1,0:T(8,128)S(1)} %get-tuple-element.140), channel_id=1, source_target_pairs={{0,2},{2,0},{4,6},{6,4},{8,16},{10,18},{12,20},{14,22},{16,8},{18,... | collective-permute-start | bytes 196616 | tf_op jit(solution)/shard_map/ppermute | solution.py:58
  8.3 6.6 %collective-permute-start.3 = (f32[4,32,128]{2,1,0:T(8,128)S(1)}, f32[4,32,128]{2,1,0:T(8,128)S(1)}, u32[]{:S(2)}, u32[]{:S(2)}) collective-permute-start(f32[4,32,128]{2,1,0:T(8,128)S(1)} %get-tuple-element.141), channel_id=1, source_target_pairs={{0,8},{2,10},{4,12},{6,14},{8,0},{10,2},{12,4},{14,6},{16,24},{18,... | collective-permute-start | bytes 196616 | tf_op jit(solution)/shard_map/ppermute | solution.py:52
  15.9 4.0 %collective-permute-start.7 = (f32[2,32,128]{2,1,0:T(8,128)S(1)}, f32[2,32,128]{2,1,0:T(8,128)S(1)}, u32[]{:S(2)}, u32[]{:S(2)}) collective-permute-start(f32[2,32,128]{2,1,0:T(8,128)S(1)} %get-tuple-element.151), channel_id=1, source_target_pairs={{0,6},{2,4},{4,2},{6,0},{8,14},{10,12},{12,10},{14,8},{16,22},{18,... | collective-permute-start | bytes 98312 | tf_op jit(solution)/shard_map/ppermute | solution.py:52
  16.5 4.2 %collective-permute-start.6 = (f32[2,32,128]{2,1,0:T(8,128)S(1)}, f32[2,32,128]{2,1,0:T(8,128)S(1)}, u32[]{:S(2)}, u32[]{:S(2)}) collective-permute-start(f32[2,32,128]{2,1,0:T(8,128)S(1)} %get-tuple-element.152), channel_id=1, source_target_pairs={{0,4},{2,6},{4,0},{6,2},{8,12},{10,14},{12,8},{14,10},{16,20},{18,... | collective-permute-start | bytes 98312 | tf_op jit(solution)/shard_map/ppermute | solution.py:52
  17.4 3.3 %collective-permute-start.5 = (f32[2,32,128]{2,1,0:T(8,128)S(1)}, f32[2,32,128]{2,1,0:T(8,128)S(1)}, u32[]{:S(2)}, u32[]{:S(2)}) collective-permute-start(f32[2,32,128]{2,1,0:T(8,128)S(1)} %get-tuple-element.153), channel_id=1, source_target_pairs={{0,2},{2,0},{4,6},{6,4},{8,10},{10,8},{12,14},{14,12},{16,18},{18,... | collective-permute-start | bytes 98312 | tf_op jit(solution)/shard_map/ppermute | solution.py:52
  20.8 2.0 %collective-permute-start.9 = (f32[4,32,128]{2,1,0:T(8,128)S(1)}, f32[4,32,128]{2,1,0:T(8,128)S(1)}, u32[]{:S(2)}, u32[]{:S(2)}) collective-permute-start(f32[4,32,128]{2,1,0:T(8,128)S(1)} %get-tuple-element.138), channel_id=1, source_target_pairs={{0,2},{2,0},{4,6},{6,4},{8,16},{10,18},{12,20},{14,22},{16,8},{18,... | collective-permute-start | bytes 196616 | tf_op jit(solution)/shard_map/ppermute | solution.py:58
  21.0 4.4 %collective-permute-start.8 = (f32[4,32,128]{2,1,0:T(8,128)S(1)}, f32[4,32,128]{2,1,0:T(8,128)S(1)}, u32[]{:S(2)}, u32[]{:S(2)}) collective-permute-start(f32[4,32,128]{2,1,0:T(8,128)S(1)} %get-tuple-element.139), channel_id=1, source_target_pairs={{0,8},{2,10},{4,12},{6,14},{8,0},{10,2},{12,4},{14,6},{16,24},{18,... | collective-permute-start | bytes 196616 | tf_op jit(solution)/shard_map/ppermute | solution.py:52
  26.4 4.0 %collective-permute-start.12 = (f32[2,32,128]{2,1,0:T(8,128)S(1)}, f32[2,32,128]{2,1,0:T(8,128)S(1)}, u32[]{:S(2)}, u32[]{:S(2)}) collective-permute-start(f32[2,32,128]{2,1,0:T(8,128)S(1)} %get-tuple-element.148), channel_id=1, source_target_pairs={{0,6},{2,4},{4,2},{6,0},{8,14},{10,12},{12,10},{14,8},{16,22},{18,... | collective-permute-start | bytes 98312 | tf_op jit(solution)/shard_map/ppermute | solution.py:52
  26.5 4.1 %collective-permute-start.11 = (f32[2,32,128]{2,1,0:T(8,128)S(1)}, f32[2,32,128]{2,1,0:T(8,128)S(1)}, u32[]{:S(2)}, u32[]{:S(2)}) collective-permute-start(f32[2,32,128]{2,1,0:T(8,128)S(1)} %get-tuple-element.149), channel_id=1, source_target_pairs={{0,4},{2,6},{4,0},{6,2},{8,12},{10,14},{12,8},{14,10},{16,20},{18,... | collective-permute-start | bytes 98312 | tf_op jit(solution)/shard_map/ppermute | solution.py:52
  27.7 2.9 %collective-permute-start.10 = (f32[2,32,128]{2,1,0:T(8,128)S(1)}, f32[2,32,128]{2,1,0:T(8,128)S(1)}, u32[]{:S(2)}, u32[]{:S(2)}) collective-permute-start(f32[2,32,128]{2,1,0:T(8,128)S(1)} %get-tuple-element.150), channel_id=1, source_target_pairs={{0,2},{2,0},{4,6},{6,4},{8,10},{10,8},{12,14},{14,12},{16,18},{18,... | collective-permute-start | bytes 98312 | tf_op jit(solution)/shard_map/ppermute | solution.py:52
  30.7 1.9 %collective-permute-start.14 = (f32[4,32,128]{2,1,0:T(8,128)S(1)}, f32[4,32,128]{2,1,0:T(8,128)S(1)}, u32[]{:S(2)}, u32[]{:S(2)}) collective-permute-start(f32[4,32,128]{2,1,0:T(8,128)S(1)} %get-tuple-element.136), channel_id=1, source_target_pairs={{0,2},{2,0},{4,6},{6,4},{8,16},{10,18},{12,20},{14,22},{16,8},{18,... | collective-permute-start | bytes 196616 | tf_op jit(solution)/shard_map/ppermute | solution.py:58
  30.8 4.5 %collective-permute-start.13 = (f32[4,32,128]{2,1,0:T(8,128)S(1)}, f32[4,32,128]{2,1,0:T(8,128)S(1)}, u32[]{:S(2)}, u32[]{:S(2)}) collective-permute-start(f32[4,32,128]{2,1,0:T(8,128)S(1)} %get-tuple-element.137), channel_id=1, source_target_pairs={{0,8},{2,10},{4,12},{6,14},{8,0},{10,2},{12,4},{14,6},{16,24},{18,... | collective-permute-start | bytes 196616 | tf_op jit(solution)/shard_map/ppermute | solution.py:52
  36.6 3.6 %collective-permute-start.17 = (f32[2,32,128]{2,1,0:T(8,128)S(1)}, f32[2,32,128]{2,1,0:T(8,128)S(1)}, u32[]{:S(2)}, u32[]{:S(2)}) collective-permute-start(f32[2,32,128]{2,1,0:T(8,128)S(1)} %get-tuple-element.145), channel_id=1, source_target_pairs={{0,6},{2,4},{4,2},{6,0},{8,14},{10,12},{12,10},{14,8},{16,22},{18,... | collective-permute-start | bytes 98312 | tf_op jit(solution)/shard_map/ppermute | solution.py:52
  37.1 4.2 %collective-permute-start.16 = (f32[2,32,128]{2,1,0:T(8,128)S(1)}, f32[2,32,128]{2,1,0:T(8,128)S(1)}, u32[]{:S(2)}, u32[]{:S(2)}) collective-permute-start(f32[2,32,128]{2,1,0:T(8,128)S(1)} %get-tuple-element.146), channel_id=1, source_target_pairs={{0,4},{2,6},{4,0},{6,2},{8,12},{10,14},{12,8},{14,10},{16,20},{18,... | collective-permute-start | bytes 98312 | tf_op jit(solution)/shard_map/ppermute | solution.py:52
  38.0 3.3 %collective-permute-start.15 = (f32[2,32,128]{2,1,0:T(8,128)S(1)}, f32[2,32,128]{2,1,0:T(8,128)S(1)}, u32[]{:S(2)}, u32[]{:S(2)}) collective-permute-start(f32[2,32,128]{2,1,0:T(8,128)S(1)} %get-tuple-element.147), channel_id=1, source_target_pairs={{0,2},{2,0},{4,6},{6,4},{8,10},{10,8},{12,14},{14,12},{16,18},{18,... | collective-permute-start | bytes 98312 | tf_op jit(solution)/shard_map/ppermute | solution.py:52
  41.4 2.9 %collective-permute-start.19 = (f32[4,32,128]{2,1,0:T(8,128)S(1)}, f32[4,32,128]{2,1,0:T(8,128)S(1)}, u32[]{:S(2)}, u32[]{:S(2)}) collective-permute-start(f32[4,32,128]{2,1,0:T(8,128)S(1)} %get-tuple-element.134), channel_id=1, source_target_pairs={{0,2},{2,0},{4,6},{6,4},{8,16},{10,18},{12,20},{14,22},{16,8},{18,... | collective-permute-start | bytes 196616 | tf_op jit(solution)/shard_map/ppermute | solution.py:58
  41.6 5.0 %collective-permute-start.18 = (f32[4,32,128]{2,1,0:T(8,128)S(1)}, f32[4,32,128]{2,1,0:T(8,128)S(1)}, u32[]{:S(2)}, u32[]{:S(2)}) collective-permute-start(f32[4,32,128]{2,1,0:T(8,128)S(1)} %get-tuple-element.135), channel_id=1, source_target_pairs={{0,8},{2,10},{4,12},{6,14},{8,0},{10,2},{12,4},{14,6},{16,24},{18,... | collective-permute-start | bytes 196616 | tf_op jit(solution)/shard_map/ppermute | solution.py:52
  47.5 3.4 %collective-permute-start.22 = (f32[2,32,128]{2,1,0:T(8,128)S(1)}, f32[2,32,128]{2,1,0:T(8,128)S(1)}, u32[]{:S(2)}, u32[]{:S(2)}) collective-permute-start(f32[2,32,128]{2,1,0:T(8,128)S(1)} %get-tuple-element.142), channel_id=1, source_target_pairs={{0,6},{2,4},{4,2},{6,0},{8,14},{10,12},{12,10},{14,8},{16,22},{18,... | collective-permute-start | bytes 98312 | tf_op jit(solution)/shard_map/ppermute | solution.py:52
  47.6 4.0 %collective-permute-start.21 = (f32[2,32,128]{2,1,0:T(8,128)S(1)}, f32[2,32,128]{2,1,0:T(8,128)S(1)}, u32[]{:S(2)}, u32[]{:S(2)}) collective-permute-start(f32[2,32,128]{2,1,0:T(8,128)S(1)} %get-tuple-element.143), channel_id=1, source_target_pairs={{0,4},{2,6},{4,0},{6,2},{8,12},{10,14},{12,8},{14,10},{16,20},{18,... | collective-permute-start | bytes 98312 | tf_op jit(solution)/shard_map/ppermute | solution.py:52
  48.3 3.4 %collective-permute-start.20 = (f32[2,32,128]{2,1,0:T(8,128)S(1)}, f32[2,32,128]{2,1,0:T(8,128)S(1)}, u32[]{:S(2)}, u32[]{:S(2)}) collective-permute-start(f32[2,32,128]{2,1,0:T(8,128)S(1)} %get-tuple-element.144), channel_id=1, source_target_pairs={{0,2},{2,0},{4,6},{6,4},{8,10},{10,8},{12,14},{14,12},{16,18},{18,... | collective-permute-start | bytes 98312 | tf_op jit(solution)/shard_map/ppermute | solution.py:52
  51.7 2.2 %collective-permute-start.24 = (f32[4,32,128]{2,1,0:T(8,128)S(1)}, f32[4,32,128]{2,1,0:T(8,128)S(1)}, u32[]{:S(2)}, u32[]{:S(2)}) collective-permute-start(f32[4,32,128]{2,1,0:T(8,128)S(1)} %get-tuple-element.132), channel_id=1, source_target_pairs={{0,2},{2,0},{4,6},{6,4},{8,16},{10,18},{12,20},{14,22},{16,8},{18,... | collective-permute-start | bytes 196616 | tf_op jit(solution)/shard_map/ppermute | solution.py:58
  51.8 4.5 %collective-permute-start.23 = (f32[4,32,128]{2,1,0:T(8,128)S(1)}, f32[4,32,128]{2,1,0:T(8,128)S(1)}, u32[]{:S(2)}, u32[]{:S(2)}) collective-permute-start(f32[4,32,128]{2,1,0:T(8,128)S(1)} %get-tuple-element.133), channel_id=1, source_target_pairs={{0,8},{2,10},{4,12},{6,14},{8,0},{10,2},{12,4},{14,6},{16,24},{18,... | collective-permute-start | bytes 196616 | tf_op jit(solution)/shard_map/ppermute | solution.py:52
  57.3 3.4 %collective-permute-start.27 = (f32[2,8,128]{2,1,0:T(8,128)S(1)}, f32[2,8,128]{2,1,0:T(8,128)S(1)}, u32[]{:S(2)}, u32[]{:S(2)}) collective-permute-start(f32[2,8,128]{2,1,0:T(8,128)S(1)} %get-tuple-element.199), channel_id=1, source_target_pairs={{0,6},{2,4},{4,2},{6,0},{8,14},{10,12},{12,10},{14,8},{16,22},{18,... | collective-permute-start | bytes 24584 | tf_op jit(solution)/shard_map/ppermute | solution.py:52
  57.3 3.7 %collective-permute-start.26 = (f32[2,8,128]{2,1,0:T(8,128)S(1)}, f32[2,8,128]{2,1,0:T(8,128)S(1)}, u32[]{:S(2)}, u32[]{:S(2)}) collective-permute-start(f32[2,8,128]{2,1,0:T(8,128)S(1)} %get-tuple-element.200), channel_id=1, source_target_pairs={{0,4},{2,6},{4,0},{6,2},{8,12},{10,14},{12,8},{14,10},{16,20},{18,... | collective-permute-start | bytes 24584 | tf_op jit(solution)/shard_map/ppermute | solution.py:52
  58.6 2.4 %collective-permute-start.25 = (f32[2,8,128]{2,1,0:T(8,128)S(1)}, f32[2,8,128]{2,1,0:T(8,128)S(1)}, u32[]{:S(2)}, u32[]{:S(2)}) collective-permute-start(f32[2,8,128]{2,1,0:T(8,128)S(1)} %get-tuple-element.201), channel_id=1, source_target_pairs={{0,2},{2,0},{4,6},{6,4},{8,10},{10,8},{12,14},{14,12},{16,18},{18,... | collective-permute-start | bytes 24584 | tf_op jit(solution)/shard_map/ppermute | solution.py:52
  61.1 3.9 %collective-permute-start.29 = (f32[4,8,128]{2,1,0:T(8,128)S(1)}, f32[4,8,128]{2,1,0:T(8,128)S(1)}, u32[]{:S(2)}, u32[]{:S(2)}) collective-permute-start(f32[4,8,128]{2,1,0:T(8,128)S(1)} %get-tuple-element.157), channel_id=1, source_target_pairs={{0,2},{2,0},{4,6},{6,4},{8,16},{10,18},{12,20},{14,22},{16,8},{18,... | collective-permute-start | bytes 49160 | tf_op jit(solution)/shard_map/ppermute | solution.py:58
  61.3 5.4 %collective-permute-start.28 = (f32[4,8,128]{2,1,0:T(8,128)S(1)}, f32[4,8,128]{2,1,0:T(8,128)S(1)}, u32[]{:S(2)}, u32[]{:S(2)}) collective-permute-start(f32[4,8,128]{2,1,0:T(8,128)S(1)} %get-tuple-element.158), channel_id=1, source_target_pairs={{0,8},{2,10},{4,12},{6,14},{8,0},{10,2},{12,4},{14,6},{16,24},{18,... | collective-permute-start | bytes 49160 | tf_op jit(solution)/shard_map/ppermute | solution.py:52
  71.1 1.4 %collective-permute-start.30 = (f32[272,128]{1,0:T(8,128)S(1)}, f32[272,128]{1,0:T(8,128)S(1)}, u32[]{:S(2)}, u32[]{:S(2)}) collective-permute-start(f32[272,128]{1,0:T(8,128)S(1)} %slice_bitcast_fusion), channel_id=1, source_target_pairs={{0,2},{2,0},{4,6},{6,4},{8,10},{10,8},{12,14},{14,12},{16,18},{18,... | collective-permute-start | bytes 417800 | tf_op jit(solution)/shard_map/ppermute | solution.py:690
  95.8 1.4 %collective-permute-start.31 = (f32[272,128]{1,0:T(8,128)S(1)}, f32[272,128]{1,0:T(8,128)S(1)}, u32[]{:S(2)}, u32[]{:S(2)}) collective-permute-start(f32[272,128]{1,0:T(8,128)S(1)} %bitcast.54), channel_id=1, source_target_pairs={{0,2},{2,0},{4,6},{6,4},{8,10},{10,8},{12,14},{14,12},{16,18},{18,... | collective-permute-start | bytes 417800 | tf_op jit(solution)/shard_map/ppermute | solution.py:696
  (2 other events, 17.2 us)

commit v4 on v3

--- a/solution.py
+++ b/solution.py
@@ -61,27 +61,36 @@
     return (*near, first, second), done
 
 
-def call(kernel, out_shape, scratch, smem, vmem, flops, moved, hbm=(), smem_out=False, after=()):
+class Column:
+    def __init__(self, ref):
+        self.ref = ref
+
+    def __getitem__(self, k):
+        return self.ref[k, 0]
+
+
+def call(kernel, out_shape, scratch, plans, vmem, flops, moved, hbm=(), after=()):
     space = lambda kind: pl.BlockSpec(memory_space=kind)
     out_specs = jax.tree.map(lambda _: space(pltpu.VMEM), out_shape)
-    if smem_out:
-        out_specs = (space(pltpu.SMEM), *out_specs[1:])
-    if after:
-        inner, lead, span = kernel, len(hbm) + len(smem) + len(vmem), len(after)
-        kernel = lambda *refs: inner(*refs[:lead], *refs[lead + span :])
+    inner, at, lead = kernel, len(hbm), len(hbm) + len(plans)
+    stop, span = lead + len(vmem), len(after)
+
+    def kernel(*refs):
+        columns = [Column(ref) for ref in refs[at:lead]]
+        inner(*refs[:at], *columns, *refs[lead:stop], *refs[stop + span :])
+
     hbm = [HOLD(x) for x in hbm]
     return pl.pallas_call(
         kernel,
         out_shape=out_shape,
         in_specs=[space(pltpu.HBM)] * len(hbm)
-        + [space(pltpu.SMEM)] * len(smem)
-        + [space(pltpu.VMEM)] * len(vmem)
+        + [space(pltpu.VMEM)] * (len(plans) + len(vmem))
         + [space(pl.ANY)] * len(after),
         out_specs=out_specs,
         scratch_shapes=scratch,
         compiler_params=pltpu.CompilerParams(vmem_limit_bytes=VMEM_GRANT),
         cost_estimate=pl.CostEstimate(flops=flops, bytes_accessed=moved, transcendentals=0),
-    )(*hbm, *smem, *vmem, *after)
+    )(*hbm, *plans, *vmem, *after)
 
 
 def store_split(ref, k, x):
@@ -150,7 +159,8 @@
 
 def load_kernel(
     plan, rows_hbm, cols_hbm, send_hbm, dest_hbm, tile_hbm, f_hbm, w_hbm, b_hbm, v_hbm,
-    plan_ref, tile_ref, f_ref, w_ref, b_ref, v_ref, rows_ref, cols_ref, send_ref, dest_ref, sem, small,
+    table_ref, tile_ref, f_ref, w_ref, b_ref, v_ref,
+    plan_ref, rows_ref, cols_ref, send_ref, dest_ref, sem, small,
 ):
     smalls = [
         pltpu.make_async_copy(src, dst, small.at[k])
@@ -193,6 +203,8 @@
     near, far = lax.fori_loop(0, plan.extra, sort_tile, (jnp.int32(0), jnp.int32(0)))
     plan_ref[plan.near] = near
     plan_ref[plan.far] = far
+    for k in range(plan.size):
+        table_ref[k : k + 1] = jnp.full((1, table_ref.shape[1]), plan_ref[k], jnp.int32)
     for copy in larges:
         copy.wait()
 
@@ -574,10 +586,11 @@
         return call(
             functools.partial(load_kernel, plan),
             (
-                jax.ShapeDtypeStruct((plan.size,), jnp.int32),
+                jax.ShapeDtypeStruct((plan.size, lanes), jnp.int32),
                 *map(like, (tile_weight, features, w_input, row_b, row_v)),
             ),
             [
+                pltpu.SMEM((plan.size,), jnp.int32),
                 pltpu.SMEM(tile_rows.shape, jnp.int32),
                 pltpu.SMEM(tile_cols.shape, jnp.int32),
                 pltpu.SMEM(send_t.shape, jnp.int32),
@@ -590,7 +603,6 @@
             flops,
             moved,
             hbm=(tile_rows, tile_cols, send_t, dest_nodes, tile_weight, features, w_input, row_b, row_v),
-            smem_out=True,
             after=(ends,),
         )
 

time: 98.3 us -> 95.4 us (0.970)
  Pallas kernels: 26.7 us -> 20.1 us
  waiting for transfers between devices: 17.9 us -> 19.7 us
  starting transfers between devices: 28.8 us -> 30.1 us
    pallas_call x16, Pallas kernels: 25.9 us -> 19.4 us  [call(): pl.pallas_call(kernel, out_shape=out_shape, in_specs=[space(pltpu.HBM)] *...]
    ppermute x24, waiting for transfers between devices: 15.9 us -> 17.7 us  [exchange(): lax.ppermute(x, 'dom', [(i, i ^ bits) for i in devices])]
    ppermute x24, starting transfers between devices: 28 us -> 29.4 us  [exchange(): lax.ppermute(x, 'dom', [(i, i ^ bits) for i in devices])]
  transfers between devices with their start and end apart: 32 -> 32, of which waited for: 15 -> 16; matrix products, arithmetic and copies ran while one was open for 0% -> 0% of each run, Pallas kernels for 16% -> 12%
where the time goes in v4:
time: 95.4 us; the launch traced here: 95.1 us
  starting transfers between devices  30.1 us (32%)
  blocking collectives  23.5 us (25%)
  Pallas kernels  20.1 us (21%)
  waiting for transfers between devices  19.7 us (21%)
  between operations  1.19 us (1%)
    ppermute x24, starting transfers between devices, exchange(): lax.ppermute(x, 'dom', [(i, i ^ bits) for i in devices])  29.4 us
    all_to_all x2, blocking collectives, local(): lax.all_to_all(x, every, 0, 0, tiled=True, axis_index_groups=same_core)  23.5 us
    pallas_call x16, Pallas kernels, call(): pl.pallas_call(kernel, out_shape=out_shape, in_specs=[space(pltpu.HBM)] *...  19.4 us
    ppermute x24, waiting for transfers between devices, exchange(): lax.ppermute(x, 'dom', [(i, i ^ bits) for i in devices])  17.7 us
  transfers between devices with their start and end apart: 32, of which 16 were waited for; matrix products, arithmetic and copies ran while one was open for 0% of the time, Pallas kernels for 12%

profile of v4, /device:TPU:0, one launch (start us, length us, event | category | flops | bytes accessed | tf_op | source)
XLA Modules:
  0.0 95.1 jit_solution(14849231409745962024)
XLA Ops:
  0.6 1.0 %shard_map.147 = (f32[32,16,128]{2,1,0:T(8,128)S(1)}, bf16[32,32,128]{2,1,0:T(8,128)(2,1)S(1)}, f32[3,2,32,128]{3,2,1,0:T(8,128)S(1)}, f32[2,32,128]{2,1,0:T(8,128)S(1)}) custom-call(s32[2,8]{1,0:T(2,128)} %bitcast.59, f32[16,4096]{1,0:T(8,128)} %refs_1_.2), custom_call_target="tpu_custom_call" | custom-call | flops 83886080 | bytes 2621440 | tf_op jit(solution)/shard_map/pallas_call | solution.py:83
  1.7 2.5 %collective-permute-start.2 = (f32[2,32,128]{2,1,0:T(8,128)S(1)}, f32[2,32,128]{2,1,0:T(8,128)S(1)}, u32[]{:S(2)}, u32[]{:S(2)}) collective-permute-start(f32[2,32,128]{2,1,0:T(8,128)S(1)} %get-tuple-element.154), channel_id=1, source_target_pairs={{0,6},{2,4},{4,2},{6,0},{8,14},{10,12},{12,10},{14,8},{16,22},{18,... | collective-permute-start | bytes 98312 | tf_op jit(solution)/shard_map/ppermute | solution.py:52
  4.9 2.2 %shard_map.148 = (s32[226,128]{1,0:T(8,128)S(1)}, bf16[80,128,128]{2,1,0:T(8,128)(2,1)S(1)}, bf16[4096,128]{1,0:T(8,128)(2,1)S(1)}, bf16[128,512]{1,0:T(8,128)(2...) custom-call(s32[80]{0:T(128)} %refs_0_.1, s32[80]{0:T(128)} %refs_1_.3, s32[2,8]{1,0:T(2,128)} %bitcast.60, ...), custom_call_target="tpu_custom_call" | custom-call | flops 83886080 | bytes 2621440 | tf_op jit(solution)/shard_map/pallas_call | solution.py:83
  7.1 1.1 %collective-permute-done.1.refs_5_.refs_10_ = f32[2,32,128]{2,1,0:T(8,128)S(1)} collective-permute-done((f32[2,32,128]{2,1,0:T(8,128)S(1)}, f32[2,32,128]{2,1,0:T(8,128)S(1)}, u32[]{:S(2)}, u32[]{:S(2)}) %collective-permute-start.1) | collective-permute-done | bytes 32800 | tf_op jit(solution)/shard_map/ppermute | solution.py:52
  8.3 3.1 %collective-permute-start.3 = (f32[4,32,128]{2,1,0:T(8,128)S(1)}, f32[4,32,128]{2,1,0:T(8,128)S(1)}, u32[]{:S(2)}, u32[]{:S(2)}) collective-permute-start(f32[4,32,128]{2,1,0:T(8,128)S(1)} %get-tuple-element.141), channel_id=1, source_target_pairs={{0,8},{2,10},{4,12},{6,14},{8,0},{10,2},{12,4},{14,6},{16,24},{18,... | collective-permute-start | bytes 196616 | tf_op jit(solution)/shard_map/ppermute | solution.py:52
  11.4 1.5 %shard_map.149.refs_2_ = f32[33,16,128]{2,1,0:T(8,128)S(1)} custom-call(s32[226,128]{1,0:T(8,128)S(1)} %get-tuple-element.76.refs_0_, bf16[80,128,128]{2,1,0:T(8,128)(2,1)S(1)} %get-tuple-element.77.refs_1_, bf16[32,32,128]{2,1,0:T(8,128)(2,1)S(1)} %get-tuple-element.78.refs_2_), custom_call_target="tpu_custom_call" | custom-call | flops 83886080 | bytes 2621440 | tf_op jit(solution)/shard_map/pallas_call | solution.py:83
  12.9 1.4 %shard_map.150 = (f32[512,4096]{1,0:T(8,128)S(1)}, f32[32,1,128]{2,1,0:T(1,128)S(1)}) custom-call(bf16[128,512]{1,0:T(8,128)(2,1)S(1)} %get-tuple-element.79.refs_0_, f32[1,512]{1,0:T(1,128)S(1)} %get-tuple-element.80.refs_1_, f32[1,512]{1,0:T(1,128)S(1)} %get-tuple-element.81.refs_2_.refs_1_, bf16[4096,128]{1,0:T(8,128)(2,1)S(1)} %get-tuple-element.82.refs_3_.refs_2_), custom_call_target="tpu_custom_call" | custom-call | flops 536870912 | bytes 8388608 | tf_op jit(solution)/shard_map/pallas_call | solution.py:83
  15.2 0.9 collective-permute-start.6
  16.9 1.5 %shard_map.152.refs_2_ = f32[33,16,128]{2,1,0:T(8,128)S(1)} custom-call(s32[226,128]{1,0:T(8,128)S(1)} %get-tuple-element.76.refs_0_, bf16[80,128,128]{2,1,0:T(8,128)(2,1)S(1)} %get-tuple-element.77.refs_1_, bf16[32,32,128]{2,1,0:T(8,128)(2,1)S(1)} %get-tuple-element.88.refs_2_), custom_call_target="tpu_custom_call" | custom-call | flops 83886080 | bytes 2621440 | tf_op jit(solution)/shard_map/pallas_call | solution.py:83
  18.4 1.0 %collective-permute-done.6.refs_5_ = f32[2,32,128]{2,1,0:T(8,128)S(1)} collective-permute-done((f32[2,32,128]{2,1,0:T(8,128)S(1)}, f32[2,32,128]{2,1,0:T(8,128)S(1)}, u32[]{:S(2)}, u32[]{:S(2)}) %collective-permute-start.6) | collective-permute-done | bytes 32800 | tf_op jit(solution)/shard_map/ppermute | solution.py:52
  19.6 1.8 %collective-permute-start.8 = (f32[4,32,128]{2,1,0:T(8,128)S(1)}, f32[4,32,128]{2,1,0:T(8,128)S(1)}, u32[]{:S(2)}, u32[]{:S(2)}) collective-permute-start(f32[4,32,128]{2,1,0:T(8,128)S(1)} %get-tuple-element.139), channel_id=1, source_target_pairs={{0,8},{2,10},{4,12},{6,14},{8,0},{10,2},{12,4},{14,6},{16,24},{18,... | collective-permute-start | bytes 196616 | tf_op jit(solution)/shard_map/ppermute | solution.py:52
  21.5 2.6 %collective-permute-done.8.refs_7_ = f32[4,32,128]{2,1,0:T(8,128)S(1)} collective-permute-done((f32[4,32,128]{2,1,0:T(8,128)S(1)}, f32[4,32,128]{2,1,0:T(8,128)S(1)}, u32[]{:S(2)}, u32[]{:S(2)}) %collective-permute-start.8) | collective-permute-done | bytes 65568 | tf_op jit(solution)/shard_map/ppermute | solution.py:52
  24.7 1.2 %collective-permute-start.11 = (f32[2,32,128]{2,1,0:T(8,128)S(1)}, f32[2,32,128]{2,1,0:T(8,128)S(1)}, u32[]{:S(2)}, u32[]{:S(2)}) collective-permute-start(f32[2,32,128]{2,1,0:T(8,128)S(1)} %get-tuple-element.149), channel_id=1, source_target_pairs={{0,4},{2,6},{4,0},{6,2},{8,12},{10,14},{12,8},{14,10},{16,20},{18,... | collective-permute-start | bytes 98312 | tf_op jit(solution)/shard_map/ppermute | solution.py:52
  26.6 1.5 %shard_map.154.refs_2_ = f32[33,16,128]{2,1,0:T(8,128)S(1)} custom-call(s32[226,128]{1,0:T(8,128)S(1)} %get-tuple-element.76.refs_0_, bf16[80,128,128]{2,1,0:T(8,128)(2,1)S(1)} %get-tuple-element.77.refs_1_, bf16[32,32,128]{2,1,0:T(8,128)(2,1)S(1)} %get-tuple-element.95.refs_2_), custom_call_target="tpu_custom_call" | custom-call | flops 83886080 | bytes 2621440 | tf_op jit(solution)/shard_map/pallas_call | solution.py:83
  29.1 3.1 %collective-permute-start.13 = (f32[4,32,128]{2,1,0:T(8,128)S(1)}, f32[4,32,128]{2,1,0:T(8,128)S(1)}, u32[]{:S(2)}, u32[]{:S(2)}) collective-permute-start(f32[4,32,128]{2,1,0:T(8,128)S(1)} %get-tuple-element.137), channel_id=1, source_target_pairs={{0,8},{2,10},{4,12},{6,14},{8,0},{10,2},{12,4},{14,6},{16,24},{18,... | collective-permute-start | bytes 196616 | tf_op jit(solution)/shard_map/ppermute | solution.py:52
  32.1 2.2 %collective-permute-done.13.refs_7_ = f32[4,32,128]{2,1,0:T(8,128)S(1)} collective-permute-done((f32[4,32,128]{2,1,0:T(8,128)S(1)}, f32[4,32,128]{2,1,0:T(8,128)S(1)}, u32[]{:S(2)}, u32[]{:S(2)}) %collective-permute-start.13) | collective-permute-done | bytes 65568 | tf_op jit(solution)/shard_map/ppermute | solution.py:52
  34.4 0.8 shard_map.155
  36.1 1.0 %collective-permute-start.15 = (f32[2,32,128]{2,1,0:T(8,128)S(1)}, f32[2,32,128]{2,1,0:T(8,128)S(1)}, u32[]{:S(2)}, u32[]{:S(2)}) collective-permute-start(f32[2,32,128]{2,1,0:T(8,128)S(1)} %get-tuple-element.147), channel_id=1, source_target_pairs={{0,2},{2,0},{4,6},{6,4},{8,10},{10,8},{12,14},{14,12},{16,18},{18,... | collective-permute-start | bytes 98312 | tf_op jit(solution)/shard_map/ppermute | solution.py:52
  37.2 0.8 shard_map.157.refs_3_
  39.6 2.7 %collective-permute-start.18 = (f32[4,32,128]{2,1,0:T(8,128)S(1)}, f32[4,32,128]{2,1,0:T(8,128)S(1)}, u32[]{:S(2)}, u32[]{:S(2)}) collective-permute-start(f32[4,32,128]{2,1,0:T(8,128)S(1)} %get-tuple-element.135), channel_id=1, source_target_pairs={{0,8},{2,10},{4,12},{6,14},{8,0},{10,2},{12,4},{14,6},{16,24},{18,... | collective-permute-start | bytes 196616 | tf_op jit(solution)/shard_map/ppermute | solution.py:52
  42.3 2.2 %collective-permute-done.18.refs_7_ = f32[4,32,128]{2,1,0:T(8,128)S(1)} collective-permute-done((f32[4,32,128]{2,1,0:T(8,128)S(1)}, f32[4,32,128]{2,1,0:T(8,128)S(1)}, u32[]{:S(2)}, u32[]{:S(2)}) %collective-permute-start.18) | collective-permute-done | bytes 65568 | tf_op jit(solution)/shard_map/ppermute | solution.py:52
  45.1 1.3 %collective-permute-start.21 = (f32[2,32,128]{2,1,0:T(8,128)S(1)}, f32[2,32,128]{2,1,0:T(8,128)S(1)}, u32[]{:S(2)}, u32[]{:S(2)}) collective-permute-start(f32[2,32,128]{2,1,0:T(8,128)S(1)} %get-tuple-element.143), channel_id=1, source_target_pairs={{0,4},{2,6},{4,0},{6,2},{8,12},{10,14},{12,8},{14,10},{16,20},{18,... | collective-permute-start | bytes 98312 | tf_op jit(solution)/shard_map/ppermute | solution.py:52
  49.3 3.2 %collective-permute-start.23 = (f32[4,32,128]{2,1,0:T(8,128)S(1)}, f32[4,32,128]{2,1,0:T(8,128)S(1)}, u32[]{:S(2)}, u32[]{:S(2)}) collective-permute-start(f32[4,32,128]{2,1,0:T(8,128)S(1)} %get-tuple-element.133), channel_id=1, source_target_pairs={{0,8},{2,10},{4,12},{6,14},{8,0},{10,2},{12,4},{14,6},{16,24},{18,... | collective-permute-start | bytes 196616 | tf_op jit(solution)/shard_map/ppermute | solution.py:52
  52.6 2.2 %collective-permute-done.23.refs_7_ = f32[4,32,128]{2,1,0:T(8,128)S(1)} collective-permute-done((f32[4,32,128]{2,1,0:T(8,128)S(1)}, f32[4,32,128]{2,1,0:T(8,128)S(1)}, u32[]{:S(2)}, u32[]{:S(2)}) %collective-permute-start.23) | collective-permute-done | bytes 65568 | tf_op jit(solution)/shard_map/ppermute | solution.py:52
  56.1 1.2 %collective-permute-start.25 = (f32[2,8,128]{2,1,0:T(8,128)S(1)}, f32[2,8,128]{2,1,0:T(8,128)S(1)}, u32[]{:S(2)}, u32[]{:S(2)}) collective-permute-start(f32[2,8,128]{2,1,0:T(8,128)S(1)} %get-tuple-element.201), channel_id=1, source_target_pairs={{0,2},{2,0},{4,6},{6,4},{8,10},{10,8},{12,14},{14,12},{16,18},{18,... | collective-permute-start | bytes 24584 | tf_op jit(solution)/shard_map/ppermute | solution.py:52
  57.3 0.9 shard_map.161.refs_4_
  59.2 2.7 %collective-permute-start.28 = (f32[4,8,128]{2,1,0:T(8,128)S(1)}, f32[4,8,128]{2,1,0:T(8,128)S(1)}, u32[]{:S(2)}, u32[]{:S(2)}) collective-permute-start(f32[4,8,128]{2,1,0:T(8,128)S(1)} %get-tuple-element.158), channel_id=1, source_target_pairs={{0,8},{2,10},{4,12},{6,14},{8,0},{10,2},{12,4},{14,6},{16,24},{18,... | collective-permute-start | bytes 49160 | tf_op jit(solution)/shard_map/ppermute | solution.py:52
  61.9 1.7 %collective-permute-done.28.refs_8_ = f32[4,8,128]{2,1,0:T(8,128)S(1)} collective-permute-done((f32[4,8,128]{2,1,0:T(8,128)S(1)}, f32[4,8,128]{2,1,0:T(8,128)S(1)}, u32[]{:S(2)}, u32[]{:S(2)}) %collective-permute-start.28) | collective-permute-done | bytes 16416 | tf_op jit(solution)/shard_map/ppermute | solution.py:52
  63.7 4.0 %shard_map.162 = f32[2,272,128]{2,1,0:T(8,128)S(1)} custom-call(s32[226,128]{1,0:T(8,128)S(1)} %get-tuple-element.76.refs_0_, f32[1,512]{1,0:T(1,128)S(1)} %get-tuple-element.81.refs_2_.refs_1_, bf16[4096,128]{1,0:T(8,128)(2,1)S(1)} %get-tuple-element.82.refs_3_.refs_2_, f32[512,4096]{1,0:T(8,128)S(1)} %get-tuple-element.102.refs_3_, ...), custom_call_target="tpu_custom_call" | custom-call | flops 1073741824 | bytes 8388608 | tf_op jit(solution)/shard_map/pallas_call | solution.py:83
  67.7 1.3 %collective-permute-done.30 = f32[272,128]{1,0:T(8,128)S(1)} collective-permute-done((f32[272,128]{1,0:T(8,128)S(1)}, f32[272,128]{1,0:T(8,128)S(1)}, u32[]{:S(2)}, u32[]{:S(2)}) %collective-permute-start.30) | collective-permute-done | bytes 139296 | tf_op jit(solution)/shard_map/ppermute | solution.py:702
  69.1 12.8 %all_to_all.10 = f32[16,1,2176]{2,1,0:T(1,128)S(1)} all-to-all(f32[16,1,2176]{2,1,0:T(1,128)S(1)} %bitcast.56), channel_id=1, replica_groups={{0,4,8,12,16,20,24,28,1,5,9,13,17,21,25,29},{2,6,10,14,18,22,26,30,3,7,..., dimensions={0} | all-to-all | bytes 278528 | tf_op jit(solution)/shard_map/all_to_all | solution.py:704
  82.0 10.8 %all_to_all.11 = f32[16,1,2176]{2,1,0:T(1,128)S(1)} all-to-all(f32[16,1,2176]{2,1,0:T(1,128)S(1)} %broadcast_in_dim.14), channel_id=1, replica_groups={{0,4,8,12,16,20,24,28,1,5,9,13,17,21,25,29},{2,6,10,14,18,22,26,30,3,7,..., dimensions={0} | all-to-all | bytes 278528 | tf_op jit(solution)/shard_map/all_to_all | solution.py:704
  (94 shorter events, 15.5 us)
Async XLA Ops:
  1.7 5.4 %collective-permute-start.2 = (f32[2,32,128]{2,1,0:T(8,128)S(1)}, f32[2,32,128]{2,1,0:T(8,128)S(1)}, u32[]{:S(2)}, u32[]{:S(2)}) collective-permute-start(f32[2,32,128]{2,1,0:T(8,128)S(1)} %get-tuple-element.154), channel_id=1, source_target_pairs={{0,6},{2,4},{4,2},{6,0},{8,14},{10,12},{12,10},{14,8},{16,22},{18,... | collective-permute-start | bytes 98312 | tf_op jit(solution)/shard_map/ppermute | solution.py:52
  4.2 4.0 %collective-permute-start.1 = (f32[2,32,128]{2,1,0:T(8,128)S(1)}, f32[2,32,128]{2,1,0:T(8,128)S(1)}, u32[]{:S(2)}, u32[]{:S(2)}) collective-permute-start(f32[2,32,128]{2,1,0:T(8,128)S(1)} %get-tuple-element.155), channel_id=1, source_target_pairs={{0,4},{2,6},{4,0},{6,2},{8,12},{10,14},{12,8},{14,10},{16,20},{18,... | collective-permute-start | bytes 98312 | tf_op jit(solution)/shard_map/ppermute | solution.py:52
  4.8 3.3 %collective-permute-start = (f32[2,32,128]{2,1,0:T(8,128)S(1)}, f32[2,32,128]{2,1,0:T(8,128)S(1)}, u32[]{:S(2)}, u32[]{:S(2)}) collective-permute-start(f32[2,32,128]{2,1,0:T(8,128)S(1)} %get-tuple-element.156), channel_id=1, source_target_pairs={{0,2},{2,0},{4,6},{6,4},{8,10},{10,8},{12,14},{14,12},{16,18},{18,... | collective-permute-start | bytes 98312 | tf_op jit(solution)/shard_map/ppermute | solution.py:52
  8.2 6.2 %collective-permute-start.4 = (f32[4,32,128]{2,1,0:T(8,128)S(1)}, f32[4,32,128]{2,1,0:T(8,128)S(1)}, u32[]{:S(2)}, u32[]{:S(2)}) collective-permute-start(f32[4,32,128]{2,1,0:T(8,128)S(1)} %get-tuple-element.140), channel_id=1, source_target_pairs={{0,2},{2,0},{4,6},{6,4},{8,16},{10,18},{12,20},{14,22},{16,8},{18,... | collective-permute-start | bytes 196616 | tf_op jit(solution)/shard_map/ppermute | solution.py:58
  8.3 6.1 %collective-permute-start.3 = (f32[4,32,128]{2,1,0:T(8,128)S(1)}, f32[4,32,128]{2,1,0:T(8,128)S(1)}, u32[]{:S(2)}, u32[]{:S(2)}) collective-permute-start(f32[4,32,128]{2,1,0:T(8,128)S(1)} %get-tuple-element.141), channel_id=1, source_target_pairs={{0,8},{2,10},{4,12},{6,14},{8,0},{10,2},{12,4},{14,6},{16,24},{18,... | collective-permute-start | bytes 196616 | tf_op jit(solution)/shard_map/ppermute | solution.py:52
  15.0 3.4 %collective-permute-start.7 = (f32[2,32,128]{2,1,0:T(8,128)S(1)}, f32[2,32,128]{2,1,0:T(8,128)S(1)}, u32[]{:S(2)}, u32[]{:S(2)}) collective-permute-start(f32[2,32,128]{2,1,0:T(8,128)S(1)} %get-tuple-element.151), channel_id=1, source_target_pairs={{0,6},{2,4},{4,2},{6,0},{8,14},{10,12},{12,10},{14,8},{16,22},{18,... | collective-permute-start | bytes 98312 | tf_op jit(solution)/shard_map/ppermute | solution.py:52
  15.2 4.3 %collective-permute-start.6 = (f32[2,32,128]{2,1,0:T(8,128)S(1)}, f32[2,32,128]{2,1,0:T(8,128)S(1)}, u32[]{:S(2)}, u32[]{:S(2)}) collective-permute-start(f32[2,32,128]{2,1,0:T(8,128)S(1)} %get-tuple-element.152), channel_id=1, source_target_pairs={{0,4},{2,6},{4,0},{6,2},{8,12},{10,14},{12,8},{14,10},{16,20},{18,... | collective-permute-start | bytes 98312 | tf_op jit(solution)/shard_map/ppermute | solution.py:52
  16.1 3.3 %collective-permute-start.5 = (f32[2,32,128]{2,1,0:T(8,128)S(1)}, f32[2,32,128]{2,1,0:T(8,128)S(1)}, u32[]{:S(2)}, u32[]{:S(2)}) collective-permute-start(f32[2,32,128]{2,1,0:T(8,128)S(1)} %get-tuple-element.153), channel_id=1, source_target_pairs={{0,2},{2,0},{4,6},{6,4},{8,10},{10,8},{12,14},{14,12},{16,18},{18,... | collective-permute-start | bytes 98312 | tf_op jit(solution)/shard_map/ppermute | solution.py:52
  19.5 2.0 %collective-permute-start.9 = (f32[4,32,128]{2,1,0:T(8,128)S(1)}, f32[4,32,128]{2,1,0:T(8,128)S(1)}, u32[]{:S(2)}, u32[]{:S(2)}) collective-permute-start(f32[4,32,128]{2,1,0:T(8,128)S(1)} %get-tuple-element.138), channel_id=1, source_target_pairs={{0,2},{2,0},{4,6},{6,4},{8,16},{10,18},{12,20},{14,22},{16,8},{18,... | collective-permute-start | bytes 196616 | tf_op jit(solution)/shard_map/ppermute | solution.py:58
  19.6 4.4 %collective-permute-start.8 = (f32[4,32,128]{2,1,0:T(8,128)S(1)}, f32[4,32,128]{2,1,0:T(8,128)S(1)}, u32[]{:S(2)}, u32[]{:S(2)}) collective-permute-start(f32[4,32,128]{2,1,0:T(8,128)S(1)} %get-tuple-element.139), channel_id=1, source_target_pairs={{0,8},{2,10},{4,12},{6,14},{8,0},{10,2},{12,4},{14,6},{16,24},{18,... | collective-permute-start | bytes 196616 | tf_op jit(solution)/shard_map/ppermute | solution.py:52
  24.6 3.5 %collective-permute-start.12 = (f32[2,32,128]{2,1,0:T(8,128)S(1)}, f32[2,32,128]{2,1,0:T(8,128)S(1)}, u32[]{:S(2)}, u32[]{:S(2)}) collective-permute-start(f32[2,32,128]{2,1,0:T(8,128)S(1)} %get-tuple-element.148), channel_id=1, source_target_pairs={{0,6},{2,4},{4,2},{6,0},{8,14},{10,12},{12,10},{14,8},{16,22},{18,... | collective-permute-start | bytes 98312 | tf_op jit(solution)/shard_map/ppermute | solution.py:52
  24.7 4.2 %collective-permute-start.11 = (f32[2,32,128]{2,1,0:T(8,128)S(1)}, f32[2,32,128]{2,1,0:T(8,128)S(1)}, u32[]{:S(2)}, u32[]{:S(2)}) collective-permute-start(f32[2,32,128]{2,1,0:T(8,128)S(1)} %get-tuple-element.149), channel_id=1, source_target_pairs={{0,4},{2,6},{4,0},{6,2},{8,12},{10,14},{12,8},{14,10},{16,20},{18,... | collective-permute-start | bytes 98312 | tf_op jit(solution)/shard_map/ppermute | solution.py:52
  25.9 3.1 %collective-permute-start.10 = (f32[2,32,128]{2,1,0:T(8,128)S(1)}, f32[2,32,128]{2,1,0:T(8,128)S(1)}, u32[]{:S(2)}, u32[]{:S(2)}) collective-permute-start(f32[2,32,128]{2,1,0:T(8,128)S(1)} %get-tuple-element.150), channel_id=1, source_target_pairs={{0,2},{2,0},{4,6},{6,4},{8,10},{10,8},{12,14},{14,12},{16,18},{18,... | collective-permute-start | bytes 98312 | tf_op jit(solution)/shard_map/ppermute | solution.py:52
  29.0 3.1 %collective-permute-start.14 = (f32[4,32,128]{2,1,0:T(8,128)S(1)}, f32[4,32,128]{2,1,0:T(8,128)S(1)}, u32[]{:S(2)}, u32[]{:S(2)}) collective-permute-start(f32[4,32,128]{2,1,0:T(8,128)S(1)} %get-tuple-element.136), channel_id=1, source_target_pairs={{0,2},{2,0},{4,6},{6,4},{8,16},{10,18},{12,20},{14,22},{16,8},{18,... | collective-permute-start | bytes 196616 | tf_op jit(solution)/shard_map/ppermute | solution.py:58
  29.1 5.3 %collective-permute-start.13 = (f32[4,32,128]{2,1,0:T(8,128)S(1)}, f32[4,32,128]{2,1,0:T(8,128)S(1)}, u32[]{:S(2)}, u32[]{:S(2)}) collective-permute-start(f32[4,32,128]{2,1,0:T(8,128)S(1)} %get-tuple-element.137), channel_id=1, source_target_pairs={{0,8},{2,10},{4,12},{6,14},{8,0},{10,2},{12,4},{14,6},{16,24},{18,... | collective-permute-start | bytes 196616 | tf_op jit(solution)/shard_map/ppermute | solution.py:52
  35.2 3.4 %collective-permute-start.17 = (f32[2,32,128]{2,1,0:T(8,128)S(1)}, f32[2,32,128]{2,1,0:T(8,128)S(1)}, u32[]{:S(2)}, u32[]{:S(2)}) collective-permute-start(f32[2,32,128]{2,1,0:T(8,128)S(1)} %get-tuple-element.145), channel_id=1, source_target_pairs={{0,6},{2,4},{4,2},{6,0},{8,14},{10,12},{12,10},{14,8},{16,22},{18,... | collective-permute-start | bytes 98312 | tf_op jit(solution)/shard_map/ppermute | solution.py:52
  35.3 4.1 %collective-permute-start.16 = (f32[2,32,128]{2,1,0:T(8,128)S(1)}, f32[2,32,128]{2,1,0:T(8,128)S(1)}, u32[]{:S(2)}, u32[]{:S(2)}) collective-permute-start(f32[2,32,128]{2,1,0:T(8,128)S(1)} %get-tuple-element.146), channel_id=1, source_target_pairs={{0,4},{2,6},{4,0},{6,2},{8,12},{10,14},{12,8},{14,10},{16,20},{18,... | collective-permute-start | bytes 98312 | tf_op jit(solution)/shard_map/ppermute | solution.py:52
  36.1 3.3 %collective-permute-start.15 = (f32[2,32,128]{2,1,0:T(8,128)S(1)}, f32[2,32,128]{2,1,0:T(8,128)S(1)}, u32[]{:S(2)}, u32[]{:S(2)}) collective-permute-start(f32[2,32,128]{2,1,0:T(8,128)S(1)} %get-tuple-element.147), channel_id=1, source_target_pairs={{0,2},{2,0},{4,6},{6,4},{8,10},{10,8},{12,14},{14,12},{16,18},{18,... | collective-permute-start | bytes 98312 | tf_op jit(solution)/shard_map/ppermute | solution.py:52
  39.5 2.8 %collective-permute-start.19 = (f32[4,32,128]{2,1,0:T(8,128)S(1)}, f32[4,32,128]{2,1,0:T(8,128)S(1)}, u32[]{:S(2)}, u32[]{:S(2)}) collective-permute-start(f32[4,32,128]{2,1,0:T(8,128)S(1)} %get-tuple-element.134), channel_id=1, source_target_pairs={{0,2},{2,0},{4,6},{6,4},{8,16},{10,18},{12,20},{14,22},{16,8},{18,... | collective-permute-start | bytes 196616 | tf_op jit(solution)/shard_map/ppermute | solution.py:58
  39.6 4.9 %collective-permute-start.18 = (f32[4,32,128]{2,1,0:T(8,128)S(1)}, f32[4,32,128]{2,1,0:T(8,128)S(1)}, u32[]{:S(2)}, u32[]{:S(2)}) collective-permute-start(f32[4,32,128]{2,1,0:T(8,128)S(1)} %get-tuple-element.135), channel_id=1, source_target_pairs={{0,8},{2,10},{4,12},{6,14},{8,0},{10,2},{12,4},{14,6},{16,24},{18,... | collective-permute-start | bytes 196616 | tf_op jit(solution)/shard_map/ppermute | solution.py:52
  45.0 3.5 %collective-permute-start.22 = (f32[2,32,128]{2,1,0:T(8,128)S(1)}, f32[2,32,128]{2,1,0:T(8,128)S(1)}, u32[]{:S(2)}, u32[]{:S(2)}) collective-permute-start(f32[2,32,128]{2,1,0:T(8,128)S(1)} %get-tuple-element.142), channel_id=1, source_target_pairs={{0,6},{2,4},{4,2},{6,0},{8,14},{10,12},{12,10},{14,8},{16,22},{18,... | collective-permute-start | bytes 98312 | tf_op jit(solution)/shard_map/ppermute | solution.py:52
  45.1 4.0 %collective-permute-start.21 = (f32[2,32,128]{2,1,0:T(8,128)S(1)}, f32[2,32,128]{2,1,0:T(8,128)S(1)}, u32[]{:S(2)}, u32[]{:S(2)}) collective-permute-start(f32[2,32,128]{2,1,0:T(8,128)S(1)} %get-tuple-element.143), channel_id=1, source_target_pairs={{0,4},{2,6},{4,0},{6,2},{8,12},{10,14},{12,8},{14,10},{16,20},{18,... | collective-permute-start | bytes 98312 | tf_op jit(solution)/shard_map/ppermute | solution.py:52
  46.3 2.8 %collective-permute-start.20 = (f32[2,32,128]{2,1,0:T(8,128)S(1)}, f32[2,32,128]{2,1,0:T(8,128)S(1)}, u32[]{:S(2)}, u32[]{:S(2)}) collective-permute-start(f32[2,32,128]{2,1,0:T(8,128)S(1)} %get-tuple-element.144), channel_id=1, source_target_pairs={{0,2},{2,0},{4,6},{6,4},{8,10},{10,8},{12,14},{14,12},{16,18},{18,... | collective-permute-start | bytes 98312 | tf_op jit(solution)/shard_map/ppermute | solution.py:52
  49.2 3.4 %collective-permute-start.24 = (f32[4,32,128]{2,1,0:T(8,128)S(1)}, f32[4,32,128]{2,1,0:T(8,128)S(1)}, u32[]{:S(2)}, u32[]{:S(2)}) collective-permute-start(f32[4,32,128]{2,1,0:T(8,128)S(1)} %get-tuple-element.132), channel_id=1, source_target_pairs={{0,2},{2,0},{4,6},{6,4},{8,16},{10,18},{12,20},{14,22},{16,8},{18,... | collective-permute-start | bytes 196616 | tf_op jit(solution)/shard_map/ppermute | solution.py:58
  49.3 5.5 %collective-permute-start.23 = (f32[4,32,128]{2,1,0:T(8,128)S(1)}, f32[4,32,128]{2,1,0:T(8,128)S(1)}, u32[]{:S(2)}, u32[]{:S(2)}) collective-permute-start(f32[4,32,128]{2,1,0:T(8,128)S(1)} %get-tuple-element.133), channel_id=1, source_target_pairs={{0,8},{2,10},{4,12},{6,14},{8,0},{10,2},{12,4},{14,6},{16,24},{18,... | collective-permute-start | bytes 196616 | tf_op jit(solution)/shard_map/ppermute | solution.py:52
  55.3 3.1 %collective-permute-start.27 = (f32[2,8,128]{2,1,0:T(8,128)S(1)}, f32[2,8,128]{2,1,0:T(8,128)S(1)}, u32[]{:S(2)}, u32[]{:S(2)}) collective-permute-start(f32[2,8,128]{2,1,0:T(8,128)S(1)} %get-tuple-element.199), channel_id=1, source_target_pairs={{0,6},{2,4},{4,2},{6,0},{8,14},{10,12},{12,10},{14,8},{16,22},{18,... | collective-permute-start | bytes 24584 | tf_op jit(solution)/shard_map/ppermute | solution.py:52
  55.4 3.7 %collective-permute-start.26 = (f32[2,8,128]{2,1,0:T(8,128)S(1)}, f32[2,8,128]{2,1,0:T(8,128)S(1)}, u32[]{:S(2)}, u32[]{:S(2)}) collective-permute-start(f32[2,8,128]{2,1,0:T(8,128)S(1)} %get-tuple-element.200), channel_id=1, source_target_pairs={{0,4},{2,6},{4,0},{6,2},{8,12},{10,14},{12,8},{14,10},{16,20},{18,... | collective-permute-start | bytes 24584 | tf_op jit(solution)/shard_map/ppermute | solution.py:52
  56.1 3.1 %collective-permute-start.25 = (f32[2,8,128]{2,1,0:T(8,128)S(1)}, f32[2,8,128]{2,1,0:T(8,128)S(1)}, u32[]{:S(2)}, u32[]{:S(2)}) collective-permute-start(f32[2,8,128]{2,1,0:T(8,128)S(1)} %get-tuple-element.201), channel_id=1, source_target_pairs={{0,2},{2,0},{4,6},{6,4},{8,10},{10,8},{12,14},{14,12},{16,18},{18,... | collective-permute-start | bytes 24584 | tf_op jit(solution)/shard_map/ppermute | solution.py:52
  59.2 2.8 %collective-permute-start.29 = (f32[4,8,128]{2,1,0:T(8,128)S(1)}, f32[4,8,128]{2,1,0:T(8,128)S(1)}, u32[]{:S(2)}, u32[]{:S(2)}) collective-permute-start(f32[4,8,128]{2,1,0:T(8,128)S(1)} %get-tuple-element.157), channel_id=1, source_target_pairs={{0,2},{2,0},{4,6},{6,4},{8,16},{10,18},{12,20},{14,22},{16,8},{18,... | collective-permute-start | bytes 49160 | tf_op jit(solution)/shard_map/ppermute | solution.py:58
  59.2 4.4 %collective-permute-start.28 = (f32[4,8,128]{2,1,0:T(8,128)S(1)}, f32[4,8,128]{2,1,0:T(8,128)S(1)}, u32[]{:S(2)}, u32[]{:S(2)}) collective-permute-start(f32[4,8,128]{2,1,0:T(8,128)S(1)} %get-tuple-element.158), channel_id=1, source_target_pairs={{0,8},{2,10},{4,12},{6,14},{8,0},{10,2},{12,4},{14,6},{16,24},{18,... | collective-permute-start | bytes 49160 | tf_op jit(solution)/shard_map/ppermute | solution.py:52
  67.7 1.4 %collective-permute-start.30 = (f32[272,128]{1,0:T(8,128)S(1)}, f32[272,128]{1,0:T(8,128)S(1)}, u32[]{:S(2)}, u32[]{:S(2)}) collective-permute-start(f32[272,128]{1,0:T(8,128)S(1)} %slice_bitcast_fusion), channel_id=1, source_target_pairs={{0,2},{2,0},{4,6},{6,4},{8,10},{10,8},{12,14},{14,12},{16,18},{18,... | collective-permute-start | bytes 417800 | tf_op jit(solution)/shard_map/ppermute | solution.py:702
  92.8 1.4 %collective-permute-start.31 = (f32[272,128]{1,0:T(8,128)S(1)}, f32[272,128]{1,0:T(8,128)S(1)}, u32[]{:S(2)}, u32[]{:S(2)}) collective-permute-start(f32[272,128]{1,0:T(8,128)S(1)} %bitcast.54), channel_id=1, source_target_pairs={{0,2},{2,0},{4,6},{6,4},{8,10},{10,8},{12,14},{14,12},{16,18},{18,... | collective-permute-start | bytes 417800 | tf_op jit(solution)/shard_map/ppermute | solution.py:708
  (2 other events, 19.3 us)

commit v5 on v4

--- a/solution.py
+++ b/solution.py
@@ -439,32 +439,13 @@
         node_ref[k] = jnp.sum(left, axis=0, keepdims=True)
 
 
-def gradient_kernel(
-    plan, count, reach, width, scale, plan_ref, v_ref, f_ref, act_ref, node_ref,
-    got1, got2, got3, got4, got5, packed_ref, total_ref, all_ref,
-):
-    blocks, _, lanes = node_ref.shape
-    me = lax.axis_index("dom")
-    collect(all_ref, (got1, got2, got3, got4, got5))
-    for k in range(blocks):
-        total_ref[k] = node_ref[k]
-    for o, f in enumerate(offsets(reach)):
-        there = present(me, count, f)
-        at = place(me, -f)
-        for m in range(width):
-            b = plan_ref[plan.send + o * width + m]
-            total_ref[b] = total_ref[b] - jnp.where(there, all_ref[at, m : m + 1], 0.0)
-    hidden = act_ref.shape[0]
-    out_sum = jnp.zeros((hidden, lanes), jnp.float32)
-    bias_sum = jnp.zeros((hidden, lanes), jnp.float32)
-    grad = jnp.zeros((hidden, f_ref.shape[1]), jnp.float32)
+def add_gradients(items, act_ref, f_ref, grad, out_sum, bias_sum):
     group = 4
-    for c in range(blocks // group):
+    for c in range(0, len(items), group):
         highs = []
         lows = []
-        for k in range(c * group, (c + 1) * group):
-            act = act_ref[:, k * lanes : (k + 1) * lanes]
-            node = total_ref[k] * scale
+        for at, node in items[c : c + group]:
+            act = act_ref[:, at]
             weighted = act * node
             pre = node - weighted * act
             out_sum = out_sum + weighted
@@ -472,13 +453,43 @@
             high = pre.astype(jnp.bfloat16)
             highs.append(high)
             lows.append((pre - high.astype(jnp.float32)).astype(jnp.bfloat16))
-        f = f_ref[c * group * lanes : (c + 1) * group * lanes]
+        f = jnp.concatenate([f_ref[at] for at, _ in items[c : c + group]], axis=0)
         grad = grad + lax.dot_general(
             jnp.concatenate(highs, axis=1), f, NN, preferred_element_type=jnp.float32
         )
         grad = grad + lax.dot_general(
             jnp.concatenate(lows, axis=1), f, NN, preferred_element_type=jnp.float32
         )
+    return grad, out_sum, bias_sum
+
+
+def own_gradient_kernel(scale, f_ref, act_ref, node_ref, grad_ref, out_ref, bias_ref):
+    blocks, _, lanes = node_ref.shape
+    items = [
+        (slice(k * lanes, (k + 1) * lanes), node_ref[k] * scale) for k in range(blocks)
+    ]
+    zeros = [jnp.zeros(ref.shape, jnp.float32) for ref in (grad_ref, out_ref, bias_ref)]
+    grad_ref[...], out_ref[...], bias_ref[...] = add_gradients(items, act_ref, f_ref, *zeros)
+
+
+def gradient_kernel(
+    plan, count, reach, width, scale, plan_ref, v_ref, f_ref, act_ref, grad_ref, out_ref, bias_ref,
+    got1, got2, got3, got4, got5, packed_ref, all_ref,
+):
+    hidden, lanes = out_ref.shape
+    me = lax.axis_index("dom")
+    collect(all_ref, (got1, got2, got3, got4, got5))
+    items = []
+    for o, f in enumerate(offsets(reach)):
+        there = present(me, count, f)
+        at = place(me, -f)
+        for m in range(width):
+            block = plan_ref[plan.send + o * width + m]
+            row = jnp.where(there, -scale * all_ref[at, m : m + 1], 0.0)
+            items.append((pl.ds(pl.multiple_of(block * lanes, lanes), lanes), row))
+    grad, out_sum, bias_sum = add_gradients(
+        items, act_ref, f_ref, grad_ref[...], out_ref[...], bias_ref[...]
+    )
     v = v_ref[...]
     core = me & 1
     half = packed_ref.shape[1]
@@ -686,17 +697,23 @@
     share = -(-(tall + 2 * hidden // lanes) // members)
     half = share * members // 2
     scale = 1.0 / math.sqrt(nodes * count * rows * lax.axis_size("dest"))
+    own = call(
+        functools.partial(own_gradient_kernel, scale),
+        (shape(hidden, feat), shape(hidden, lanes), shape(hidden, lanes)),
+        [],
+        (),
+        (feature, act, node),
+        4 * nodes * hidden * feat,
+        nodes * hidden * 4,
+    )
     packed = call(
         functools.partial(gradient_kernel, plan, count, reach, width, scale),
         shape(2, half, lanes),
-        [
-            pltpu.VMEM((blocks, 1, lanes), f32),
-            pltpu.VMEM((PLACES, 8, lanes), f32),
-        ],
+        [pltpu.VMEM((PLACES, 8, lanes), f32)],
         (plans,),
-        (v_out, feature, act, node, *got),
-        4 * nodes * hidden * feat,
-        nodes * hidden * 4,
+        (v_out, feature, act, *own, *got),
+        4 * slots * lanes * hidden * feat,
+        slots * lanes * hidden * 4,
     )
     twins = [(i, i ^ 1) for i in range(count)]
     mine = packed[0] + lax.ppermute(packed[1], "dom", twins)

time: 95.4 us -> 94.8 us (level)
  waiting for transfers between devices: 19.7 us -> 17.9 us
  Pallas kernels: 20.1 us -> 21.9 us
    ppermute x24, waiting for transfers between devices: 17.7 us -> 16 us  [exchange(): lax.ppermute(x, 'dom', [(i, i ^ bits) for i in devices])]
    pallas_call x16 -> x17, Pallas kernels: 19.4 us -> 21.1 us  [call(): pl.pallas_call(kernel, out_shape=out_shape, in_specs=[space(pltpu.HBM)] *...]
  transfers between devices with their start and end apart: 32 -> 32, of which waited for: 16 -> 15; matrix products, arithmetic and copies ran while one was open for 0% -> 0% of each run, Pallas kernels for 12% -> 16%
where the time goes in v5:
time: 94.8 us; the launch traced here: 94.6 us
  starting transfers between devices  30.1 us (32%)
  blocking collectives  23.1 us (24%)
  Pallas kernels  21.9 us (23%)
  waiting for transfers between devices  17.9 us (19%)
  between operations  1.22 us (1%)
    ppermute x24, starting transfers between devices, exchange(): lax.ppermute(x, 'dom', [(i, i ^ bits) for i in devices])  29.3 us
    all_to_all x2, blocking collectives, local(): lax.all_to_all(x, every, 0, 0, tiled=True, axis_index_groups=same_core)  23.1 us
    pallas_call x17, Pallas kernels, call(): pl.pallas_call(kernel, out_shape=out_shape, in_specs=[space(pltpu.HBM)] *...  21.1 us
    ppermute x24, waiting for transfers between devices, exchange(): lax.ppermute(x, 'dom', [(i, i ^ bits) for i in devices])  16 us
  transfers between devices with their start and end apart: 32, of which 15 were waited for; matrix products, arithmetic and copies ran while one was open for 0% of the time, Pallas kernels for 16%

profile of v5, /device:TPU:0, one launch (start us, length us, event | category | flops | bytes accessed | tf_op | source)
XLA Modules:
  0.0 94.6 jit_solution(2580375952377368222)
XLA Ops:
  0.6 1.0 %shard_map.147 = (f32[32,16,128]{2,1,0:T(8,128)S(1)}, bf16[32,32,128]{2,1,0:T(8,128)(2,1)S(1)}, f32[3,2,32,128]{3,2,1,0:T(8,128)S(1)}, f32[2,32,128]{2,1,0:T(8,128)S(1)}) custom-call(s32[2,8]{1,0:T(2,128)} %bitcast.59, f32[16,4096]{1,0:T(8,128)} %refs_1_.2), custom_call_target="tpu_custom_call" | custom-call | flops 83886080 | bytes 2621440 | tf_op jit(solution)/shard_map/pallas_call | solution.py:83
  1.7 2.5 %collective-permute-start.2 = (f32[2,32,128]{2,1,0:T(8,128)S(1)}, f32[2,32,128]{2,1,0:T(8,128)S(1)}, u32[]{:S(2)}, u32[]{:S(2)}) collective-permute-start(f32[2,32,128]{2,1,0:T(8,128)S(1)} %get-tuple-element.160), channel_id=1, source_target_pairs={{0,6},{2,4},{4,2},{6,0},{8,14},{10,12},{12,10},{14,8},{16,22},{18,... | collective-permute-start | bytes 98312 | tf_op jit(solution)/shard_map/ppermute | solution.py:52
  4.9 2.2 %shard_map.148 = (s32[226,128]{1,0:T(8,128)S(1)}, bf16[80,128,128]{2,1,0:T(8,128)(2,1)S(1)}, bf16[4096,128]{1,0:T(8,128)(2,1)S(1)}, bf16[128,512]{1,0:T(8,128)(2...) custom-call(s32[80]{0:T(128)} %refs_0_.1, s32[80]{0:T(128)} %refs_1_.3, s32[2,8]{1,0:T(2,128)} %bitcast.60, ...), custom_call_target="tpu_custom_call" | custom-call | flops 83886080 | bytes 2621440 | tf_op jit(solution)/shard_map/pallas_call | solution.py:83
  7.1 1.1 %collective-permute-done.1.refs_5_.refs_10_ = f32[2,32,128]{2,1,0:T(8,128)S(1)} collective-permute-done((f32[2,32,128]{2,1,0:T(8,128)S(1)}, f32[2,32,128]{2,1,0:T(8,128)S(1)}, u32[]{:S(2)}, u32[]{:S(2)}) %collective-permute-start.1) | collective-permute-done | bytes 32800 | tf_op jit(solution)/shard_map/ppermute | solution.py:52
  8.3 3.1 %collective-permute-start.3 = (f32[4,32,128]{2,1,0:T(8,128)S(1)}, f32[4,32,128]{2,1,0:T(8,128)S(1)}, u32[]{:S(2)}, u32[]{:S(2)}) collective-permute-start(f32[4,32,128]{2,1,0:T(8,128)S(1)} %get-tuple-element.147), channel_id=1, source_target_pairs={{0,8},{2,10},{4,12},{6,14},{8,0},{10,2},{12,4},{14,6},{16,24},{18,... | collective-permute-start | bytes 196616 | tf_op jit(solution)/shard_map/ppermute | solution.py:52
  11.4 1.5 %shard_map.149.refs_2_ = f32[33,16,128]{2,1,0:T(8,128)S(1)} custom-call(s32[226,128]{1,0:T(8,128)S(1)} %get-tuple-element.79.refs_0_, bf16[80,128,128]{2,1,0:T(8,128)(2,1)S(1)} %get-tuple-element.80.refs_1_, bf16[32,32,128]{2,1,0:T(8,128)(2,1)S(1)} %get-tuple-element.81.refs_2_), custom_call_target="tpu_custom_call" | custom-call | flops 83886080 | bytes 2621440 | tf_op jit(solution)/shard_map/pallas_call | solution.py:83
  12.9 1.4 %shard_map.150 = (f32[512,4096]{1,0:T(8,128)S(1)}, f32[32,1,128]{2,1,0:T(1,128)S(1)}) custom-call(bf16[128,512]{1,0:T(8,128)(2,1)S(1)} %get-tuple-element.82.refs_0_, f32[1,512]{1,0:T(1,128)S(1)} %get-tuple-element.83.refs_1_, f32[1,512]{1,0:T(1,128)S(1)} %get-tuple-element.84.refs_2_.refs_1_, bf16[4096,128]{1,0:T(8,128)(2,1)S(1)} %get-tuple-element.85.refs_3_.refs_0_.refs_2_), custom_call_target="tpu_custom_call" | custom-call | flops 536870912 | bytes 8388608 | tf_op jit(solution)/shard_map/pallas_call | solution.py:83
  15.2 0.9 collective-permute-start.6
  16.9 1.5 %shard_map.152.refs_2_ = f32[33,16,128]{2,1,0:T(8,128)S(1)} custom-call(s32[226,128]{1,0:T(8,128)S(1)} %get-tuple-element.79.refs_0_, bf16[80,128,128]{2,1,0:T(8,128)(2,1)S(1)} %get-tuple-element.80.refs_1_, bf16[32,32,128]{2,1,0:T(8,128)(2,1)S(1)} %get-tuple-element.91.refs_2_), custom_call_target="tpu_custom_call" | custom-call | flops 83886080 | bytes 2621440 | tf_op jit(solution)/shard_map/pallas_call | solution.py:83
  18.4 1.0 %collective-permute-done.6.refs_5_ = f32[2,32,128]{2,1,0:T(8,128)S(1)} collective-permute-done((f32[2,32,128]{2,1,0:T(8,128)S(1)}, f32[2,32,128]{2,1,0:T(8,128)S(1)}, u32[]{:S(2)}, u32[]{:S(2)}) %collective-permute-start.6) | collective-permute-done | bytes 32800 | tf_op jit(solution)/shard_map/ppermute | solution.py:52
  19.7 1.8 %collective-permute-start.8 = (f32[4,32,128]{2,1,0:T(8,128)S(1)}, f32[4,32,128]{2,1,0:T(8,128)S(1)}, u32[]{:S(2)}, u32[]{:S(2)}) collective-permute-start(f32[4,32,128]{2,1,0:T(8,128)S(1)} %get-tuple-element.145), channel_id=1, source_target_pairs={{0,8},{2,10},{4,12},{6,14},{8,0},{10,2},{12,4},{14,6},{16,24},{18,... | collective-permute-start | bytes 196616 | tf_op jit(solution)/shard_map/ppermute | solution.py:52
  21.5 2.6 %collective-permute-done.8.refs_7_ = f32[4,32,128]{2,1,0:T(8,128)S(1)} collective-permute-done((f32[4,32,128]{2,1,0:T(8,128)S(1)}, f32[4,32,128]{2,1,0:T(8,128)S(1)}, u32[]{:S(2)}, u32[]{:S(2)}) %collective-permute-start.8) | collective-permute-done | bytes 65568 | tf_op jit(solution)/shard_map/ppermute | solution.py:52
  24.7 1.2 %collective-permute-start.11 = (f32[2,32,128]{2,1,0:T(8,128)S(1)}, f32[2,32,128]{2,1,0:T(8,128)S(1)}, u32[]{:S(2)}, u32[]{:S(2)}) collective-permute-start(f32[2,32,128]{2,1,0:T(8,128)S(1)} %get-tuple-element.155), channel_id=1, source_target_pairs={{0,4},{2,6},{4,0},{6,2},{8,12},{10,14},{12,8},{14,10},{16,20},{18,... | collective-permute-start | bytes 98312 | tf_op jit(solution)/shard_map/ppermute | solution.py:52
  26.6 1.5 %shard_map.154.refs_2_ = f32[33,16,128]{2,1,0:T(8,128)S(1)} custom-call(s32[226,128]{1,0:T(8,128)S(1)} %get-tuple-element.79.refs_0_, bf16[80,128,128]{2,1,0:T(8,128)(2,1)S(1)} %get-tuple-element.80.refs_1_, bf16[32,32,128]{2,1,0:T(8,128)(2,1)S(1)} %get-tuple-element.98.refs_2_), custom_call_target="tpu_custom_call" | custom-call | flops 83886080 | bytes 2621440 | tf_op jit(solution)/shard_map/pallas_call | solution.py:83
  29.1 3.0 %collective-permute-start.13 = (f32[4,32,128]{2,1,0:T(8,128)S(1)}, f32[4,32,128]{2,1,0:T(8,128)S(1)}, u32[]{:S(2)}, u32[]{:S(2)}) collective-permute-start(f32[4,32,128]{2,1,0:T(8,128)S(1)} %get-tuple-element.143), channel_id=1, source_target_pairs={{0,8},{2,10},{4,12},{6,14},{8,0},{10,2},{12,4},{14,6},{16,24},{18,... | collective-permute-start | bytes 196616 | tf_op jit(solution)/shard_map/ppermute | solution.py:52
  32.1 2.2 %collective-permute-done.13.refs_7_ = f32[4,32,128]{2,1,0:T(8,128)S(1)} collective-permute-done((f32[4,32,128]{2,1,0:T(8,128)S(1)}, f32[4,32,128]{2,1,0:T(8,128)S(1)}, u32[]{:S(2)}, u32[]{:S(2)}) %collective-permute-start.13) | collective-permute-done | bytes 65568 | tf_op jit(solution)/shard_map/ppermute | solution.py:52
  34.4 0.8 shard_map.155
  36.1 1.0 %collective-permute-start.15 = (f32[2,32,128]{2,1,0:T(8,128)S(1)}, f32[2,32,128]{2,1,0:T(8,128)S(1)}, u32[]{:S(2)}, u32[]{:S(2)}) collective-permute-start(f32[2,32,128]{2,1,0:T(8,128)S(1)} %get-tuple-element.153), channel_id=1, source_target_pairs={{0,2},{2,0},{4,6},{6,4},{8,10},{10,8},{12,14},{14,12},{16,18},{18,... | collective-permute-start | bytes 98312 | tf_op jit(solution)/shard_map/ppermute | solution.py:52
  39.6 2.6 %collective-permute-start.18 = (f32[4,32,128]{2,1,0:T(8,128)S(1)}, f32[4,32,128]{2,1,0:T(8,128)S(1)}, u32[]{:S(2)}, u32[]{:S(2)}) collective-permute-start(f32[4,32,128]{2,1,0:T(8,128)S(1)} %get-tuple-element.141), channel_id=1, source_target_pairs={{0,8},{2,10},{4,12},{6,14},{8,0},{10,2},{12,4},{14,6},{16,24},{18,... | collective-permute-start | bytes 196616 | tf_op jit(solution)/shard_map/ppermute | solution.py:52
  42.2 2.2 %collective-permute-done.18.refs_7_ = f32[4,32,128]{2,1,0:T(8,128)S(1)} collective-permute-done((f32[4,32,128]{2,1,0:T(8,128)S(1)}, f32[4,32,128]{2,1,0:T(8,128)S(1)}, u32[]{:S(2)}, u32[]{:S(2)}) %collective-permute-start.18) | collective-permute-done | bytes 65568 | tf_op jit(solution)/shard_map/ppermute | solution.py:52
  45.0 1.3 %collective-permute-start.21 = (f32[2,32,128]{2,1,0:T(8,128)S(1)}, f32[2,32,128]{2,1,0:T(8,128)S(1)}, u32[]{:S(2)}, u32[]{:S(2)}) collective-permute-start(f32[2,32,128]{2,1,0:T(8,128)S(1)} %get-tuple-element.149), channel_id=1, source_target_pairs={{0,4},{2,6},{4,0},{6,2},{8,12},{10,14},{12,8},{14,10},{16,20},{18,... | collective-permute-start | bytes 98312 | tf_op jit(solution)/shard_map/ppermute | solution.py:52
  46.9 0.8 shard_map.159.refs_3_
  49.3 3.3 %collective-permute-start.23 = (f32[4,32,128]{2,1,0:T(8,128)S(1)}, f32[4,32,128]{2,1,0:T(8,128)S(1)}, u32[]{:S(2)}, u32[]{:S(2)}) collective-permute-start(f32[4,32,128]{2,1,0:T(8,128)S(1)} %get-tuple-element.139), channel_id=1, source_target_pairs={{0,8},{2,10},{4,12},{6,14},{8,0},{10,2},{12,4},{14,6},{16,24},{18,... | collective-permute-start | bytes 196616 | tf_op jit(solution)/shard_map/ppermute | solution.py:52
  52.6 2.2 %collective-permute-done.23.refs_7_ = f32[4,32,128]{2,1,0:T(8,128)S(1)} collective-permute-done((f32[4,32,128]{2,1,0:T(8,128)S(1)}, f32[4,32,128]{2,1,0:T(8,128)S(1)}, u32[]{:S(2)}, u32[]{:S(2)}) %collective-permute-start.23) | collective-permute-done | bytes 65568 | tf_op jit(solution)/shard_map/ppermute | solution.py:52
  56.1 1.2 %collective-permute-start.25 = (f32[2,8,128]{2,1,0:T(8,128)S(1)}, f32[2,8,128]{2,1,0:T(8,128)S(1)}, u32[]{:S(2)}, u32[]{:S(2)}) collective-permute-start(f32[2,8,128]{2,1,0:T(8,128)S(1)} %get-tuple-element.207), channel_id=1, source_target_pairs={{0,2},{2,0},{4,6},{6,4},{8,10},{10,8},{12,14},{14,12},{16,18},{18,... | collective-permute-start | bytes 24584 | tf_op jit(solution)/shard_map/ppermute | solution.py:52
  57.3 0.9 shard_map.161.refs_2_
  59.2 2.6 %collective-permute-start.28 = (f32[4,8,128]{2,1,0:T(8,128)S(1)}, f32[4,8,128]{2,1,0:T(8,128)S(1)}, u32[]{:S(2)}, u32[]{:S(2)}) collective-permute-start(f32[4,8,128]{2,1,0:T(8,128)S(1)} %get-tuple-element.164), channel_id=1, source_target_pairs={{0,8},{2,10},{4,12},{6,14},{8,0},{10,2},{12,4},{14,6},{16,24},{18,... | collective-permute-start | bytes 49160 | tf_op jit(solution)/shard_map/ppermute | solution.py:52
  61.8 3.5 %shard_map.162 = (f32[512,128]{1,0:T(8,128)S(1)}, f32[512,128]{1,0:T(8,128)S(1)}, f32[512,128]{1,0:T(8,128)S(1)}) custom-call(bf16[4096,128]{1,0:T(8,128)(2,1)S(1)} %get-tuple-element.85.refs_3_.refs_0_.refs_2_, f32[512,4096]{1,0:T(8,128)S(1)} %get-tuple-element.105.refs_1_.refs_3_, f32[32,1,128]{2,1,0:T(1,128)S(1)} %shard_map.161.refs_2_), custom_call_target="tpu_custom_call" | custom-call | flops 1073741824 | bytes 8388608 | tf_op jit(solution)/shard_map/pallas_call | solution.py:83
  65.3 2.2 %shard_map.163 = f32[2,272,128]{2,1,0:T(8,128)S(1)} custom-call(s32[226,128]{1,0:T(8,128)S(1)} %get-tuple-element.79.refs_0_, f32[1,512]{1,0:T(1,128)S(1)} %get-tuple-element.84.refs_2_.refs_1_, bf16[4096,128]{1,0:T(8,128)(2,1)S(1)} %get-tuple-element.85.refs_3_.refs_0_.refs_2_, f32[512,4096]{1,0:T(8,128)S(1)} %get-tuple-element.105.refs_1_.refs_3_, ...), custom_call_target="tpu_custom_call" | custom-call | flops 536870912 | bytes 4194304 | tf_op jit(solution)/shard_map/pallas_call | solution.py:83
  67.7 1.3 %collective-permute-done.30 = f32[272,128]{1,0:T(8,128)S(1)} collective-permute-done((f32[272,128]{1,0:T(8,128)S(1)}, f32[272,128]{1,0:T(8,128)S(1)}, u32[]{:S(2)}, u32[]{:S(2)}) %collective-permute-start.30) | collective-permute-done | bytes 139296 | tf_op jit(solution)/shard_map/ppermute | solution.py:719
  69.0 12.3 %all_to_all.10 = f32[16,1,2176]{2,1,0:T(1,128)S(1)} all-to-all(f32[16,1,2176]{2,1,0:T(1,128)S(1)} %bitcast.56), channel_id=1, replica_groups={{0,4,8,12,16,20,24,28,1,5,9,13,17,21,25,29},{2,6,10,14,18,22,26,30,3,7,..., dimensions={0} | all-to-all | bytes 278528 | tf_op jit(solution)/shard_map/all_to_all | solution.py:721
  81.5 10.8 %all_to_all.11 = f32[16,1,2176]{2,1,0:T(1,128)S(1)} all-to-all(f32[16,1,2176]{2,1,0:T(1,128)S(1)} %broadcast_in_dim.14), channel_id=1, replica_groups={{0,4,8,12,16,20,24,28,1,5,9,13,17,21,25,29},{2,6,10,14,18,22,26,30,3,7,..., dimensions={0} | all-to-all | bytes 278528 | tf_op jit(solution)/shard_map/all_to_all | solution.py:721
  (95 shorter events, 15.4 us)
Async XLA Ops:
  1.7 5.4 %collective-permute-start.2 = (f32[2,32,128]{2,1,0:T(8,128)S(1)}, f32[2,32,128]{2,1,0:T(8,128)S(1)}, u32[]{:S(2)}, u32[]{:S(2)}) collective-permute-start(f32[2,32,128]{2,1,0:T(8,128)S(1)} %get-tuple-element.160), channel_id=1, source_target_pairs={{0,6},{2,4},{4,2},{6,0},{8,14},{10,12},{12,10},{14,8},{16,22},{18,... | collective-permute-start | bytes 98312 | tf_op jit(solution)/shard_map/ppermute | solution.py:52
  4.2 4.0 %collective-permute-start.1 = (f32[2,32,128]{2,1,0:T(8,128)S(1)}, f32[2,32,128]{2,1,0:T(8,128)S(1)}, u32[]{:S(2)}, u32[]{:S(2)}) collective-permute-start(f32[2,32,128]{2,1,0:T(8,128)S(1)} %get-tuple-element.161), channel_id=1, source_target_pairs={{0,4},{2,6},{4,0},{6,2},{8,12},{10,14},{12,8},{14,10},{16,20},{18,... | collective-permute-start | bytes 98312 | tf_op jit(solution)/shard_map/ppermute | solution.py:52
  4.8 3.3 %collective-permute-start = (f32[2,32,128]{2,1,0:T(8,128)S(1)}, f32[2,32,128]{2,1,0:T(8,128)S(1)}, u32[]{:S(2)}, u32[]{:S(2)}) collective-permute-start(f32[2,32,128]{2,1,0:T(8,128)S(1)} %get-tuple-element.162), channel_id=1, source_target_pairs={{0,2},{2,0},{4,6},{6,4},{8,10},{10,8},{12,14},{14,12},{16,18},{18,... | collective-permute-start | bytes 98312 | tf_op jit(solution)/shard_map/ppermute | solution.py:52
  8.2 6.2 %collective-permute-start.4 = (f32[4,32,128]{2,1,0:T(8,128)S(1)}, f32[4,32,128]{2,1,0:T(8,128)S(1)}, u32[]{:S(2)}, u32[]{:S(2)}) collective-permute-start(f32[4,32,128]{2,1,0:T(8,128)S(1)} %get-tuple-element.146), channel_id=1, source_target_pairs={{0,2},{2,0},{4,6},{6,4},{8,16},{10,18},{12,20},{14,22},{16,8},{18,... | collective-permute-start | bytes 196616 | tf_op jit(solution)/shard_map/ppermute | solution.py:58
  8.3 6.1 %collective-permute-start.3 = (f32[4,32,128]{2,1,0:T(8,128)S(1)}, f32[4,32,128]{2,1,0:T(8,128)S(1)}, u32[]{:S(2)}, u32[]{:S(2)}) collective-permute-start(f32[4,32,128]{2,1,0:T(8,128)S(1)} %get-tuple-element.147), channel_id=1, source_target_pairs={{0,8},{2,10},{4,12},{6,14},{8,0},{10,2},{12,4},{14,6},{16,24},{18,... | collective-permute-start | bytes 196616 | tf_op jit(solution)/shard_map/ppermute | solution.py:52
  15.0 3.4 %collective-permute-start.7 = (f32[2,32,128]{2,1,0:T(8,128)S(1)}, f32[2,32,128]{2,1,0:T(8,128)S(1)}, u32[]{:S(2)}, u32[]{:S(2)}) collective-permute-start(f32[2,32,128]{2,1,0:T(8,128)S(1)} %get-tuple-element.157), channel_id=1, source_target_pairs={{0,6},{2,4},{4,2},{6,0},{8,14},{10,12},{12,10},{14,8},{16,22},{18,... | collective-permute-start | bytes 98312 | tf_op jit(solution)/shard_map/ppermute | solution.py:52
  15.2 4.3 %collective-permute-start.6 = (f32[2,32,128]{2,1,0:T(8,128)S(1)}, f32[2,32,128]{2,1,0:T(8,128)S(1)}, u32[]{:S(2)}, u32[]{:S(2)}) collective-permute-start(f32[2,32,128]{2,1,0:T(8,128)S(1)} %get-tuple-element.158), channel_id=1, source_target_pairs={{0,4},{2,6},{4,0},{6,2},{8,12},{10,14},{12,8},{14,10},{16,20},{18,... | collective-permute-start | bytes 98312 | tf_op jit(solution)/shard_map/ppermute | solution.py:52
  16.1 3.3 %collective-permute-start.5 = (f32[2,32,128]{2,1,0:T(8,128)S(1)}, f32[2,32,128]{2,1,0:T(8,128)S(1)}, u32[]{:S(2)}, u32[]{:S(2)}) collective-permute-start(f32[2,32,128]{2,1,0:T(8,128)S(1)} %get-tuple-element.159), channel_id=1, source_target_pairs={{0,2},{2,0},{4,6},{6,4},{8,10},{10,8},{12,14},{14,12},{16,18},{18,... | collective-permute-start | bytes 98312 | tf_op jit(solution)/shard_map/ppermute | solution.py:52
  19.5 2.0 %collective-permute-start.9 = (f32[4,32,128]{2,1,0:T(8,128)S(1)}, f32[4,32,128]{2,1,0:T(8,128)S(1)}, u32[]{:S(2)}, u32[]{:S(2)}) collective-permute-start(f32[4,32,128]{2,1,0:T(8,128)S(1)} %get-tuple-element.144), channel_id=1, source_target_pairs={{0,2},{2,0},{4,6},{6,4},{8,16},{10,18},{12,20},{14,22},{16,8},{18,... | collective-permute-start | bytes 196616 | tf_op jit(solution)/shard_map/ppermute | solution.py:58
  19.7 4.4 %collective-permute-start.8 = (f32[4,32,128]{2,1,0:T(8,128)S(1)}, f32[4,32,128]{2,1,0:T(8,128)S(1)}, u32[]{:S(2)}, u32[]{:S(2)}) collective-permute-start(f32[4,32,128]{2,1,0:T(8,128)S(1)} %get-tuple-element.145), channel_id=1, source_target_pairs={{0,8},{2,10},{4,12},{6,14},{8,0},{10,2},{12,4},{14,6},{16,24},{18,... | collective-permute-start | bytes 196616 | tf_op jit(solution)/shard_map/ppermute | solution.py:52
  24.6 3.5 %collective-permute-start.12 = (f32[2,32,128]{2,1,0:T(8,128)S(1)}, f32[2,32,128]{2,1,0:T(8,128)S(1)}, u32[]{:S(2)}, u32[]{:S(2)}) collective-permute-start(f32[2,32,128]{2,1,0:T(8,128)S(1)} %get-tuple-element.154), channel_id=1, source_target_pairs={{0,6},{2,4},{4,2},{6,0},{8,14},{10,12},{12,10},{14,8},{16,22},{18,... | collective-permute-start | bytes 98312 | tf_op jit(solution)/shard_map/ppermute | solution.py:52
  24.7 4.2 %collective-permute-start.11 = (f32[2,32,128]{2,1,0:T(8,128)S(1)}, f32[2,32,128]{2,1,0:T(8,128)S(1)}, u32[]{:S(2)}, u32[]{:S(2)}) collective-permute-start(f32[2,32,128]{2,1,0:T(8,128)S(1)} %get-tuple-element.155), channel_id=1, source_target_pairs={{0,4},{2,6},{4,0},{6,2},{8,12},{10,14},{12,8},{14,10},{16,20},{18,... | collective-permute-start | bytes 98312 | tf_op jit(solution)/shard_map/ppermute | solution.py:52
  25.9 3.1 %collective-permute-start.10 = (f32[2,32,128]{2,1,0:T(8,128)S(1)}, f32[2,32,128]{2,1,0:T(8,128)S(1)}, u32[]{:S(2)}, u32[]{:S(2)}) collective-permute-start(f32[2,32,128]{2,1,0:T(8,128)S(1)} %get-tuple-element.156), channel_id=1, source_target_pairs={{0,2},{2,0},{4,6},{6,4},{8,10},{10,8},{12,14},{14,12},{16,18},{18,... | collective-permute-start | bytes 98312 | tf_op jit(solution)/shard_map/ppermute | solution.py:52
  29.0 3.1 %collective-permute-start.14 = (f32[4,32,128]{2,1,0:T(8,128)S(1)}, f32[4,32,128]{2,1,0:T(8,128)S(1)}, u32[]{:S(2)}, u32[]{:S(2)}) collective-permute-start(f32[4,32,128]{2,1,0:T(8,128)S(1)} %get-tuple-element.142), channel_id=1, source_target_pairs={{0,2},{2,0},{4,6},{6,4},{8,16},{10,18},{12,20},{14,22},{16,8},{18,... | collective-permute-start | bytes 196616 | tf_op jit(solution)/shard_map/ppermute | solution.py:58
  29.1 5.3 %collective-permute-start.13 = (f32[4,32,128]{2,1,0:T(8,128)S(1)}, f32[4,32,128]{2,1,0:T(8,128)S(1)}, u32[]{:S(2)}, u32[]{:S(2)}) collective-permute-start(f32[4,32,128]{2,1,0:T(8,128)S(1)} %get-tuple-element.143), channel_id=1, source_target_pairs={{0,8},{2,10},{4,12},{6,14},{8,0},{10,2},{12,4},{14,6},{16,24},{18,... | collective-permute-start | bytes 196616 | tf_op jit(solution)/shard_map/ppermute | solution.py:52
  35.2 3.4 %collective-permute-start.17 = (f32[2,32,128]{2,1,0:T(8,128)S(1)}, f32[2,32,128]{2,1,0:T(8,128)S(1)}, u32[]{:S(2)}, u32[]{:S(2)}) collective-permute-start(f32[2,32,128]{2,1,0:T(8,128)S(1)} %get-tuple-element.151), channel_id=1, source_target_pairs={{0,6},{2,4},{4,2},{6,0},{8,14},{10,12},{12,10},{14,8},{16,22},{18,... | collective-permute-start | bytes 98312 | tf_op jit(solution)/shard_map/ppermute | solution.py:52
  35.3 4.2 %collective-permute-start.16 = (f32[2,32,128]{2,1,0:T(8,128)S(1)}, f32[2,32,128]{2,1,0:T(8,128)S(1)}, u32[]{:S(2)}, u32[]{:S(2)}) collective-permute-start(f32[2,32,128]{2,1,0:T(8,128)S(1)} %get-tuple-element.152), channel_id=1, source_target_pairs={{0,4},{2,6},{4,0},{6,2},{8,12},{10,14},{12,8},{14,10},{16,20},{18,... | collective-permute-start | bytes 98312 | tf_op jit(solution)/shard_map/ppermute | solution.py:52
  36.1 3.3 %collective-permute-start.15 = (f32[2,32,128]{2,1,0:T(8,128)S(1)}, f32[2,32,128]{2,1,0:T(8,128)S(1)}, u32[]{:S(2)}, u32[]{:S(2)}) collective-permute-start(f32[2,32,128]{2,1,0:T(8,128)S(1)} %get-tuple-element.153), channel_id=1, source_target_pairs={{0,2},{2,0},{4,6},{6,4},{8,10},{10,8},{12,14},{14,12},{16,18},{18,... | collective-permute-start | bytes 98312 | tf_op jit(solution)/shard_map/ppermute | solution.py:52
  39.5 2.7 %collective-permute-start.19 = (f32[4,32,128]{2,1,0:T(8,128)S(1)}, f32[4,32,128]{2,1,0:T(8,128)S(1)}, u32[]{:S(2)}, u32[]{:S(2)}) collective-permute-start(f32[4,32,128]{2,1,0:T(8,128)S(1)} %get-tuple-element.140), channel_id=1, source_target_pairs={{0,2},{2,0},{4,6},{6,4},{8,16},{10,18},{12,20},{14,22},{16,8},{18,... | collective-permute-start | bytes 196616 | tf_op jit(solution)/shard_map/ppermute | solution.py:58
  39.6 4.9 %collective-permute-start.18 = (f32[4,32,128]{2,1,0:T(8,128)S(1)}, f32[4,32,128]{2,1,0:T(8,128)S(1)}, u32[]{:S(2)}, u32[]{:S(2)}) collective-permute-start(f32[4,32,128]{2,1,0:T(8,128)S(1)} %get-tuple-element.141), channel_id=1, source_target_pairs={{0,8},{2,10},{4,12},{6,14},{8,0},{10,2},{12,4},{14,6},{16,24},{18,... | collective-permute-start | bytes 196616 | tf_op jit(solution)/shard_map/ppermute | solution.py:52
  44.9 3.6 %collective-permute-start.22 = (f32[2,32,128]{2,1,0:T(8,128)S(1)}, f32[2,32,128]{2,1,0:T(8,128)S(1)}, u32[]{:S(2)}, u32[]{:S(2)}) collective-permute-start(f32[2,32,128]{2,1,0:T(8,128)S(1)} %get-tuple-element.148), channel_id=1, source_target_pairs={{0,6},{2,4},{4,2},{6,0},{8,14},{10,12},{12,10},{14,8},{16,22},{18,... | collective-permute-start | bytes 98312 | tf_op jit(solution)/shard_map/ppermute | solution.py:52
  45.0 4.0 %collective-permute-start.21 = (f32[2,32,128]{2,1,0:T(8,128)S(1)}, f32[2,32,128]{2,1,0:T(8,128)S(1)}, u32[]{:S(2)}, u32[]{:S(2)}) collective-permute-start(f32[2,32,128]{2,1,0:T(8,128)S(1)} %get-tuple-element.149), channel_id=1, source_target_pairs={{0,4},{2,6},{4,0},{6,2},{8,12},{10,14},{12,8},{14,10},{16,20},{18,... | collective-permute-start | bytes 98312 | tf_op jit(solution)/shard_map/ppermute | solution.py:52
  46.4 2.6 %collective-permute-start.20 = (f32[2,32,128]{2,1,0:T(8,128)S(1)}, f32[2,32,128]{2,1,0:T(8,128)S(1)}, u32[]{:S(2)}, u32[]{:S(2)}) collective-permute-start(f32[2,32,128]{2,1,0:T(8,128)S(1)} %get-tuple-element.150), channel_id=1, source_target_pairs={{0,2},{2,0},{4,6},{6,4},{8,10},{10,8},{12,14},{14,12},{16,18},{18,... | collective-permute-start | bytes 98312 | tf_op jit(solution)/shard_map/ppermute | solution.py:52
  49.1 3.5 %collective-permute-start.24 = (f32[4,32,128]{2,1,0:T(8,128)S(1)}, f32[4,32,128]{2,1,0:T(8,128)S(1)}, u32[]{:S(2)}, u32[]{:S(2)}) collective-permute-start(f32[4,32,128]{2,1,0:T(8,128)S(1)} %get-tuple-element.138), channel_id=1, source_target_pairs={{0,2},{2,0},{4,6},{6,4},{8,16},{10,18},{12,20},{14,22},{16,8},{18,... | collective-permute-start | bytes 196616 | tf_op jit(solution)/shard_map/ppermute | solution.py:58
  49.3 5.5 %collective-permute-start.23 = (f32[4,32,128]{2,1,0:T(8,128)S(1)}, f32[4,32,128]{2,1,0:T(8,128)S(1)}, u32[]{:S(2)}, u32[]{:S(2)}) collective-permute-start(f32[4,32,128]{2,1,0:T(8,128)S(1)} %get-tuple-element.139), channel_id=1, source_target_pairs={{0,8},{2,10},{4,12},{6,14},{8,0},{10,2},{12,4},{14,6},{16,24},{18,... | collective-permute-start | bytes 196616 | tf_op jit(solution)/shard_map/ppermute | solution.py:52
  55.3 3.1 %collective-permute-start.27 = (f32[2,8,128]{2,1,0:T(8,128)S(1)}, f32[2,8,128]{2,1,0:T(8,128)S(1)}, u32[]{:S(2)}, u32[]{:S(2)}) collective-permute-start(f32[2,8,128]{2,1,0:T(8,128)S(1)} %get-tuple-element.205), channel_id=1, source_target_pairs={{0,6},{2,4},{4,2},{6,0},{8,14},{10,12},{12,10},{14,8},{16,22},{18,... | collective-permute-start | bytes 24584 | tf_op jit(solution)/shard_map/ppermute | solution.py:52
  55.4 3.7 %collective-permute-start.26 = (f32[2,8,128]{2,1,0:T(8,128)S(1)}, f32[2,8,128]{2,1,0:T(8,128)S(1)}, u32[]{:S(2)}, u32[]{:S(2)}) collective-permute-start(f32[2,8,128]{2,1,0:T(8,128)S(1)} %get-tuple-element.206), channel_id=1, source_target_pairs={{0,4},{2,6},{4,0},{6,2},{8,12},{10,14},{12,8},{14,10},{16,20},{18,... | collective-permute-start | bytes 24584 | tf_op jit(solution)/shard_map/ppermute | solution.py:52
  56.1 3.1 %collective-permute-start.25 = (f32[2,8,128]{2,1,0:T(8,128)S(1)}, f32[2,8,128]{2,1,0:T(8,128)S(1)}, u32[]{:S(2)}, u32[]{:S(2)}) collective-permute-start(f32[2,8,128]{2,1,0:T(8,128)S(1)} %get-tuple-element.207), channel_id=1, source_target_pairs={{0,2},{2,0},{4,6},{6,4},{8,10},{10,8},{12,14},{14,12},{16,18},{18,... | collective-permute-start | bytes 24584 | tf_op jit(solution)/shard_map/ppermute | solution.py:52
  59.2 6.2 %collective-permute-start.29 = (f32[4,8,128]{2,1,0:T(8,128)S(1)}, f32[4,8,128]{2,1,0:T(8,128)S(1)}, u32[]{:S(2)}, u32[]{:S(2)}) collective-permute-start(f32[4,8,128]{2,1,0:T(8,128)S(1)} %get-tuple-element.163), channel_id=1, source_target_pairs={{0,2},{2,0},{4,6},{6,4},{8,16},{10,18},{12,20},{14,22},{16,8},{18,... | collective-permute-start | bytes 49160 | tf_op jit(solution)/shard_map/ppermute | solution.py:58
  59.2 6.1 %collective-permute-start.28 = (f32[4,8,128]{2,1,0:T(8,128)S(1)}, f32[4,8,128]{2,1,0:T(8,128)S(1)}, u32[]{:S(2)}, u32[]{:S(2)}) collective-permute-start(f32[4,8,128]{2,1,0:T(8,128)S(1)} %get-tuple-element.164), channel_id=1, source_target_pairs={{0,8},{2,10},{4,12},{6,14},{8,0},{10,2},{12,4},{14,6},{16,24},{18,... | collective-permute-start | bytes 49160 | tf_op jit(solution)/shard_map/ppermute | solution.py:52
  67.6 1.4 %collective-permute-start.30 = (f32[272,128]{1,0:T(8,128)S(1)}, f32[272,128]{1,0:T(8,128)S(1)}, u32[]{:S(2)}, u32[]{:S(2)}) collective-permute-start(f32[272,128]{1,0:T(8,128)S(1)} %slice_bitcast_fusion), channel_id=1, source_target_pairs={{0,2},{2,0},{4,6},{6,4},{8,10},{10,8},{12,14},{14,12},{16,18},{18,... | collective-permute-start | bytes 417800 | tf_op jit(solution)/shard_map/ppermute | solution.py:719
  92.3 1.4 %collective-permute-start.31 = (f32[272,128]{1,0:T(8,128)S(1)}, f32[272,128]{1,0:T(8,128)S(1)}, u32[]{:S(2)}, u32[]{:S(2)}) collective-permute-start(f32[272,128]{1,0:T(8,128)S(1)} %bitcast.54), channel_id=1, source_target_pairs={{0,2},{2,0},{4,6},{6,4},{8,10},{10,8},{12,14},{14,12},{16,18},{18,... | collective-permute-start | bytes 417800 | tf_op jit(solution)/shard_map/ppermute | solution.py:725
  (2 other events, 19.3 us)

commit v6 on v5

--- a/solution.py
+++ b/solution.py
@@ -227,7 +227,7 @@
 
 
 def first_kernel(
-    reach, width, send_hbm, term_hbm, z_ref, split_ref, pairs_ref, ends_ref, send_ref, term_ref, sem, small
+    reach, width, send_hbm, term_hbm, z_ref, pairs_ref, ends_ref, send_ref, term_ref, sem, small
 ):
     blocks, _, lanes = z_ref.shape
     parts = sem.shape[0]
@@ -243,9 +243,7 @@
     for i, copy in enumerate(copies):
         copy.wait()
         for k in range(i * span, (i + 1) * span):
-            z = jnp.exp(term_ref[:, k * lanes : (k + 1) * lanes])
-            z_ref[k] = z
-            store_split(split_ref, k, z)
+            z_ref[k] = jnp.exp(term_ref[:, k * lanes : (k + 1) * lanes])
     asked.wait()
     send_items(
         pairs_ref, ends_ref, reach, 1, send_slots(width, lambda o, m: z_ref[send_ref[m, o]])
@@ -268,6 +266,12 @@
 
 def near_kernel(plan, forward, plan_ref, w_ref, split_ref, sum_ref):
     near_products(plan, plan_ref, w_ref, split_ref, sum_ref, forward)
+
+
+def near_values_kernel(plan, plan_ref, w_ref, z_ref, sum_ref, split_ref):
+    for k in range(plan.blocks):
+        store_split(split_ref, k, z_ref[k])
+    near_products(plan, plan_ref, w_ref, split_ref, sum_ref, True)
 
 
 def backed_up(
@@ -308,7 +312,7 @@
 def backup_kernel(
     plan, reach, width, plan_ref, w_ref, part_ref, growth_ref,
     got1, got2, got3, got4, got5,
-    z_ref, next_ref, pairs_ref, ends_ref, all_ref, ext_ref, sum_ref,
+    z_ref, pairs_ref, ends_ref, all_ref, ext_ref, sum_ref,
 ):
     blocks, rows, lanes = z_ref.shape
     me = lax.axis_index("dom")
@@ -318,9 +322,7 @@
     )
     dest = goal_of(plan, plan_ref, rows, lanes)
     for k in range(blocks):
-        z = with_goal(k, blocks, growth_ref, sum_ref, dest, me)
-        z_ref[k] = z
-        store_split(next_ref, k, z)
+        z_ref[k] = with_goal(k, blocks, growth_ref, sum_ref, dest, me)
     send_items(
         pairs_ref, ends_ref, reach, 1,
         send_slots(width, lambda o, m: z_ref[plan_ref[plan.send + o * width + m]]),
@@ -440,7 +442,7 @@
 
 
 def add_gradients(items, act_ref, f_ref, grad, out_sum, bias_sum):
-    group = 4
+    group = 8
     for c in range(0, len(items), group):
         highs = []
         lows = []
@@ -577,9 +579,9 @@
     send_t = send_blocks.T
     row_b = b_input[None, :]
 
-    z0, split, pairs, ends = call(
+    z0, pairs, ends = call(
         bind(first_kernel),
-        (field, halves, *parcels),
+        (field, *parcels),
         [
             pltpu.SMEM(send_t.shape, jnp.int32),
             pltpu.VMEM(terminal.shape, f32),
@@ -633,10 +635,15 @@
         nodes * hidden * 4,
     )
 
+    def near_values(z):
+        kernel = functools.partial(near_values_kernel, plan)
+        scratch = [pltpu.VMEM((blocks, 2 * rows, lanes), bf16)]
+        return call(kernel, padded, scratch, (plans,), (weight, z), flops, moved)
+
     def backup(part, got):
         return call(
             bind(backup_kernel, plan),
-            (field, halves, *parcels),
+            (field, *parcels),
             [all_s, ext_s, sum_s],
             (plans,),
             (weight, part, growth, *got),
@@ -644,10 +651,10 @@
             moved,
         )
 
-    z1, split, pairs, ends = backup(near(split, True), far)
-    got, part = exchange(pairs, ends, lambda: near(split, True))
-    z2, split2, pairs, ends = backup(part, got)
-    got, part = exchange(pairs, ends, lambda: near(split2, True))
+    z1, pairs, ends = backup(near_values(z0), far)
+    got, part = exchange(pairs, ends, lambda: near_values(z1))
+    z2, pairs, ends = backup(part, got)
+    got, part = exchange(pairs, ends, lambda: near_values(z2))
     z3, split3, pairs, ends = call(
         bind(turn_kernel, plan),
         (field, halves, *parcels),

time: 94.8 us -> 94.8 us (level)
  no operation moved by 1% of the time
where the time goes in v6:
time: 94.8 us; the launch traced here: 94.5 us
  starting transfers between devices  30.1 us (32%)
  blocking collectives  23.1 us (24%)
  Pallas kernels  21.8 us (23%)
  waiting for transfers between devices  17.9 us (19%)
  between operations  1.21 us (1%)
    ppermute x24, starting transfers between devices, exchange(): lax.ppermute(x, 'dom', [(i, i ^ bits) for i in devices])  29.3 us
    all_to_all x2, blocking collectives, local(): lax.all_to_all(x, every, 0, 0, tiled=True, axis_index_groups=same_core)  23.1 us
    pallas_call x17, Pallas kernels, call(): pl.pallas_call(kernel, out_shape=out_shape, in_specs=[space(pltpu.HBM)] *...  21 us
    ppermute x24, waiting for transfers between devices, exchange(): lax.ppermute(x, 'dom', [(i, i ^ bits) for i in devices])  16 us
  transfers between devices with their start and end apart: 32, of which 15 were waited for; matrix products, arithmetic and copies ran while one was open for 0% of the time, Pallas kernels for 16%

profile of v6, /device:TPU:0, one launch (start us, length us, event | category | flops | bytes accessed | tf_op | source)
XLA Modules:
  0.0 94.5 jit_solution(6827695689442976687)
XLA Ops:
  0.6 1.0 %shard_map.147 = (f32[32,16,128]{2,1,0:T(8,128)S(1)}, f32[3,2,32,128]{3,2,1,0:T(8,128)S(1)}, f32[2,32,128]{2,1,0:T(8,128)S(1)}) custom-call(s32[2,8]{1,0:T(2,128)} %bitcast.59, f32[16,4096]{1,0:T(8,128)} %refs_1_.2), custom_call_target="tpu_custom_call" | custom-call | flops 83886080 | bytes 2621440 | tf_op jit(solution)/shard_map/pallas_call | solution.py:83
  1.7 2.5 %collective-permute-start.2 = (f32[2,32,128]{2,1,0:T(8,128)S(1)}, f32[2,32,128]{2,1,0:T(8,128)S(1)}, u32[]{:S(2)}, u32[]{:S(2)}) collective-permute-start(f32[2,32,128]{2,1,0:T(8,128)S(1)} %get-tuple-element.154), channel_id=1, source_target_pairs={{0,6},{2,4},{4,2},{6,0},{8,14},{10,12},{12,10},{14,8},{16,22},{18,... | collective-permute-start | bytes 98312 | tf_op jit(solution)/shard_map/ppermute | solution.py:52
  4.9 2.2 %shard_map.148 = (s32[226,128]{1,0:T(8,128)S(1)}, bf16[80,128,128]{2,1,0:T(8,128)(2,1)S(1)}, bf16[4096,128]{1,0:T(8,128)(2,1)S(1)}, bf16[128,512]{1,0:T(8,128)(2...) custom-call(s32[80]{0:T(128)} %refs_0_.1, s32[80]{0:T(128)} %refs_1_.3, s32[2,8]{1,0:T(2,128)} %bitcast.60, ...), custom_call_target="tpu_custom_call" | custom-call | flops 83886080 | bytes 2621440 | tf_op jit(solution)/shard_map/pallas_call | solution.py:83
  7.1 1.1 %collective-permute-done.1.refs_5_.refs_10_ = f32[2,32,128]{2,1,0:T(8,128)S(1)} collective-permute-done((f32[2,32,128]{2,1,0:T(8,128)S(1)}, f32[2,32,128]{2,1,0:T(8,128)S(1)}, u32[]{:S(2)}, u32[]{:S(2)}) %collective-permute-start.1) | collective-permute-done | bytes 32800 | tf_op jit(solution)/shard_map/ppermute | solution.py:52
  8.3 3.1 %collective-permute-start.3 = (f32[4,32,128]{2,1,0:T(8,128)S(1)}, f32[4,32,128]{2,1,0:T(8,128)S(1)}, u32[]{:S(2)}, u32[]{:S(2)}) collective-permute-start(f32[4,32,128]{2,1,0:T(8,128)S(1)} %get-tuple-element.141), channel_id=1, source_target_pairs={{0,8},{2,10},{4,12},{6,14},{8,0},{10,2},{12,4},{14,6},{16,24},{18,... | collective-permute-start | bytes 196616 | tf_op jit(solution)/shard_map/ppermute | solution.py:52
  11.4 1.5 %shard_map.149.refs_2_ = f32[33,16,128]{2,1,0:T(8,128)S(1)} custom-call(s32[226,128]{1,0:T(8,128)S(1)} %get-tuple-element.76.refs_0_, bf16[80,128,128]{2,1,0:T(8,128)(2,1)S(1)} %get-tuple-element.77.refs_1_, f32[32,16,128]{2,1,0:T(8,128)S(1)} %get-tuple-element.78.refs_2_.refs_3_), custom_call_target="tpu_custom_call" | custom-call | flops 83886080 | bytes 2621440 | tf_op jit(solution)/shard_map/pallas_call | solution.py:83
  12.9 1.4 %shard_map.150 = (f32[512,4096]{1,0:T(8,128)S(1)}, f32[32,1,128]{2,1,0:T(1,128)S(1)}) custom-call(bf16[128,512]{1,0:T(8,128)(2,1)S(1)} %get-tuple-element.79.refs_0_, f32[1,512]{1,0:T(1,128)S(1)} %get-tuple-element.80.refs_1_, f32[1,512]{1,0:T(1,128)S(1)} %get-tuple-element.81.refs_2_.refs_1_, bf16[4096,128]{1,0:T(8,128)(2,1)S(1)} %get-tuple-element.82.refs_3_.refs_0_.refs_2_), custom_call_target="tpu_custom_call" | custom-call | flops 536870912 | bytes 8388608 | tf_op jit(solution)/shard_map/pallas_call | solution.py:83
  15.1 0.9 collective-permute-start.6
  16.9 1.5 %shard_map.152.refs_2_ = f32[33,16,128]{2,1,0:T(8,128)S(1)} custom-call(s32[226,128]{1,0:T(8,128)S(1)} %get-tuple-element.76.refs_0_, bf16[80,128,128]{2,1,0:T(8,128)(2,1)S(1)} %get-tuple-element.77.refs_1_, f32[32,16,128]{2,1,0:T(8,128)S(1)} %get-tuple-element.88.refs_2_.refs_4_), custom_call_target="tpu_custom_call" | custom-call | flops 83886080 | bytes 2621440 | tf_op jit(solution)/shard_map/pallas_call | solution.py:83
  18.4 1.0 %collective-permute-done.6.refs_5_ = f32[2,32,128]{2,1,0:T(8,128)S(1)} collective-permute-done((f32[2,32,128]{2,1,0:T(8,128)S(1)}, f32[2,32,128]{2,1,0:T(8,128)S(1)}, u32[]{:S(2)}, u32[]{:S(2)}) %collective-permute-start.6) | collective-permute-done | bytes 32800 | tf_op jit(solution)/shard_map/ppermute | solution.py:52
  19.6 1.8 %collective-permute-start.8 = (f32[4,32,128]{2,1,0:T(8,128)S(1)}, f32[4,32,128]{2,1,0:T(8,128)S(1)}, u32[]{:S(2)}, u32[]{:S(2)}) collective-permute-start(f32[4,32,128]{2,1,0:T(8,128)S(1)} %get-tuple-element.139), channel_id=1, source_target_pairs={{0,8},{2,10},{4,12},{6,14},{8,0},{10,2},{12,4},{14,6},{16,24},{18,... | collective-permute-start | bytes 196616 | tf_op jit(solution)/shard_map/ppermute | solution.py:52
  21.4 2.6 %collective-permute-done.8.refs_7_ = f32[4,32,128]{2,1,0:T(8,128)S(1)} collective-permute-done((f32[4,32,128]{2,1,0:T(8,128)S(1)}, f32[4,32,128]{2,1,0:T(8,128)S(1)}, u32[]{:S(2)}, u32[]{:S(2)}) %collective-permute-start.8) | collective-permute-done | bytes 65568 | tf_op jit(solution)/shard_map/ppermute | solution.py:52
  24.7 1.2 %collective-permute-start.11 = (f32[2,32,128]{2,1,0:T(8,128)S(1)}, f32[2,32,128]{2,1,0:T(8,128)S(1)}, u32[]{:S(2)}, u32[]{:S(2)}) collective-permute-start(f32[2,32,128]{2,1,0:T(8,128)S(1)} %get-tuple-element.149), channel_id=1, source_target_pairs={{0,4},{2,6},{4,0},{6,2},{8,12},{10,14},{12,8},{14,10},{16,20},{18,... | collective-permute-start | bytes 98312 | tf_op jit(solution)/shard_map/ppermute | solution.py:52
  26.5 1.5 %shard_map.154.refs_2_ = f32[33,16,128]{2,1,0:T(8,128)S(1)} custom-call(s32[226,128]{1,0:T(8,128)S(1)} %get-tuple-element.76.refs_0_, bf16[80,128,128]{2,1,0:T(8,128)(2,1)S(1)} %get-tuple-element.77.refs_1_, f32[32,16,128]{2,1,0:T(8,128)S(1)} %get-tuple-element.95.refs_2_.refs_5_), custom_call_target="tpu_custom_call" | custom-call | flops 83886080 | bytes 2621440 | tf_op jit(solution)/shard_map/pallas_call | solution.py:83
  29.0 3.0 %collective-permute-start.13 = (f32[4,32,128]{2,1,0:T(8,128)S(1)}, f32[4,32,128]{2,1,0:T(8,128)S(1)}, u32[]{:S(2)}, u32[]{:S(2)}) collective-permute-start(f32[4,32,128]{2,1,0:T(8,128)S(1)} %get-tuple-element.137), channel_id=1, source_target_pairs={{0,8},{2,10},{4,12},{6,14},{8,0},{10,2},{12,4},{14,6},{16,24},{18,... | collective-permute-start | bytes 196616 | tf_op jit(solution)/shard_map/ppermute | solution.py:52
  32.1 2.2 %collective-permute-done.13.refs_7_ = f32[4,32,128]{2,1,0:T(8,128)S(1)} collective-permute-done((f32[4,32,128]{2,1,0:T(8,128)S(1)}, f32[4,32,128]{2,1,0:T(8,128)S(1)}, u32[]{:S(2)}, u32[]{:S(2)}) %collective-permute-start.13) | collective-permute-done | bytes 65568 | tf_op jit(solution)/shard_map/ppermute | solution.py:52
  34.3 0.8 shard_map.155
  36.1 1.0 %collective-permute-start.15 = (f32[2,32,128]{2,1,0:T(8,128)S(1)}, f32[2,32,128]{2,1,0:T(8,128)S(1)}, u32[]{:S(2)}, u32[]{:S(2)}) collective-permute-start(f32[2,32,128]{2,1,0:T(8,128)S(1)} %get-tuple-element.147), channel_id=1, source_target_pairs={{0,2},{2,0},{4,6},{6,4},{8,10},{10,8},{12,14},{14,12},{16,18},{18,... | collective-permute-start | bytes 98312 | tf_op jit(solution)/shard_map/ppermute | solution.py:52
  37.1 0.8 shard_map.157.refs_3_
  39.5 2.6 %collective-permute-start.18 = (f32[4,32,128]{2,1,0:T(8,128)S(1)}, f32[4,32,128]{2,1,0:T(8,128)S(1)}, u32[]{:S(2)}, u32[]{:S(2)}) collective-permute-start(f32[4,32,128]{2,1,0:T(8,128)S(1)} %get-tuple-element.135), channel_id=1, source_target_pairs={{0,8},{2,10},{4,12},{6,14},{8,0},{10,2},{12,4},{14,6},{16,24},{18,... | collective-permute-start | bytes 196616 | tf_op jit(solution)/shard_map/ppermute | solution.py:52
  42.2 2.2 %collective-permute-done.18.refs_7_ = f32[4,32,128]{2,1,0:T(8,128)S(1)} collective-permute-done((f32[4,32,128]{2,1,0:T(8,128)S(1)}, f32[4,32,128]{2,1,0:T(8,128)S(1)}, u32[]{:S(2)}, u32[]{:S(2)}) %collective-permute-start.18) | collective-permute-done | bytes 65568 | tf_op jit(solution)/shard_map/ppermute | solution.py:52
  45.0 1.3 %collective-permute-start.21 = (f32[2,32,128]{2,1,0:T(8,128)S(1)}, f32[2,32,128]{2,1,0:T(8,128)S(1)}, u32[]{:S(2)}, u32[]{:S(2)}) collective-permute-start(f32[2,32,128]{2,1,0:T(8,128)S(1)} %get-tuple-element.143), channel_id=1, source_target_pairs={{0,4},{2,6},{4,0},{6,2},{8,12},{10,14},{12,8},{14,10},{16,20},{18,... | collective-permute-start | bytes 98312 | tf_op jit(solution)/shard_map/ppermute | solution.py:52
  49.2 3.3 %collective-permute-start.23 = (f32[4,32,128]{2,1,0:T(8,128)S(1)}, f32[4,32,128]{2,1,0:T(8,128)S(1)}, u32[]{:S(2)}, u32[]{:S(2)}) collective-permute-start(f32[4,32,128]{2,1,0:T(8,128)S(1)} %get-tuple-element.133), channel_id=1, source_target_pairs={{0,8},{2,10},{4,12},{6,14},{8,0},{10,2},{12,4},{14,6},{16,24},{18,... | collective-permute-start | bytes 196616 | tf_op jit(solution)/shard_map/ppermute | solution.py:52
  52.5 2.2 %collective-permute-done.23.refs_7_ = f32[4,32,128]{2,1,0:T(8,128)S(1)} collective-permute-done((f32[4,32,128]{2,1,0:T(8,128)S(1)}, f32[4,32,128]{2,1,0:T(8,128)S(1)}, u32[]{:S(2)}, u32[]{:S(2)}) %collective-permute-start.23) | collective-permute-done | bytes 65568 | tf_op jit(solution)/shard_map/ppermute | solution.py:52
  56.0 1.2 %collective-permute-start.25 = (f32[2,8,128]{2,1,0:T(8,128)S(1)}, f32[2,8,128]{2,1,0:T(8,128)S(1)}, u32[]{:S(2)}, u32[]{:S(2)}) collective-permute-start(f32[2,8,128]{2,1,0:T(8,128)S(1)} %get-tuple-element.201), channel_id=1, source_target_pairs={{0,2},{2,0},{4,6},{6,4},{8,10},{10,8},{12,14},{14,12},{16,18},{18,... | collective-permute-start | bytes 24584 | tf_op jit(solution)/shard_map/ppermute | solution.py:52
  57.2 0.9 shard_map.161.refs_2_
  59.2 2.6 %collective-permute-start.28 = (f32[4,8,128]{2,1,0:T(8,128)S(1)}, f32[4,8,128]{2,1,0:T(8,128)S(1)}, u32[]{:S(2)}, u32[]{:S(2)}) collective-permute-start(f32[4,8,128]{2,1,0:T(8,128)S(1)} %get-tuple-element.158), channel_id=1, source_target_pairs={{0,8},{2,10},{4,12},{6,14},{8,0},{10,2},{12,4},{14,6},{16,24},{18,... | collective-permute-start | bytes 49160 | tf_op jit(solution)/shard_map/ppermute | solution.py:52
  61.8 3.5 %shard_map.162 = (f32[512,128]{1,0:T(8,128)S(1)}, f32[512,128]{1,0:T(8,128)S(1)}, f32[512,128]{1,0:T(8,128)S(1)}) custom-call(bf16[4096,128]{1,0:T(8,128)(2,1)S(1)} %get-tuple-element.82.refs_3_.refs_0_.refs_2_, f32[512,4096]{1,0:T(8,128)S(1)} %get-tuple-element.102.refs_1_.refs_3_, f32[32,1,128]{2,1,0:T(1,128)S(1)} %shard_map.161.refs_2_), custom_call_target="tpu_custom_call" | custom-call | flops 1073741824 | bytes 8388608 | tf_op jit(solution)/shard_map/pallas_call | solution.py:83
  65.4 2.2 %shard_map.163 = f32[2,272,128]{2,1,0:T(8,128)S(1)} custom-call(s32[226,128]{1,0:T(8,128)S(1)} %get-tuple-element.76.refs_0_, f32[1,512]{1,0:T(1,128)S(1)} %get-tuple-element.81.refs_2_.refs_1_, bf16[4096,128]{1,0:T(8,128)(2,1)S(1)} %get-tuple-element.82.refs_3_.refs_0_.refs_2_, f32[512,4096]{1,0:T(8,128)S(1)} %get-tuple-element.102.refs_1_.refs_3_, ...), custom_call_target="tpu_custom_call" | custom-call | flops 536870912 | bytes 4194304 | tf_op jit(solution)/shard_map/pallas_call | solution.py:83
  67.6 1.3 %collective-permute-done.30 = f32[272,128]{1,0:T(8,128)S(1)} collective-permute-done((f32[272,128]{1,0:T(8,128)S(1)}, f32[272,128]{1,0:T(8,128)S(1)}, u32[]{:S(2)}, u32[]{:S(2)}) %collective-permute-start.30) | collective-permute-done | bytes 139296 | tf_op jit(solution)/shard_map/ppermute | solution.py:726
  69.0 12.3 %all_to_all.10 = f32[16,1,2176]{2,1,0:T(1,128)S(1)} all-to-all(f32[16,1,2176]{2,1,0:T(1,128)S(1)} %bitcast.56), channel_id=1, replica_groups={{0,4,8,12,16,20,24,28,1,5,9,13,17,21,25,29},{2,6,10,14,18,22,26,30,3,7,..., dimensions={0} | all-to-all | bytes 278528 | tf_op jit(solution)/shard_map/all_to_all | solution.py:728
  81.5 10.8 %all_to_all.11 = f32[16,1,2176]{2,1,0:T(1,128)S(1)} all-to-all(f32[16,1,2176]{2,1,0:T(1,128)S(1)} %broadcast_in_dim.14), channel_id=1, replica_groups={{0,4,8,12,16,20,24,28,1,5,9,13,17,21,25,29},{2,6,10,14,18,22,26,30,3,7,..., dimensions={0} | all-to-all | bytes 278528 | tf_op jit(solution)/shard_map/all_to_all | solution.py:728
  (95 shorter events, 15.4 us)
Async XLA Ops:
  1.7 5.4 %collective-permute-start.2 = (f32[2,32,128]{2,1,0:T(8,128)S(1)}, f32[2,32,128]{2,1,0:T(8,128)S(1)}, u32[]{:S(2)}, u32[]{:S(2)}) collective-permute-start(f32[2,32,128]{2,1,0:T(8,128)S(1)} %get-tuple-element.154), channel_id=1, source_target_pairs={{0,6},{2,4},{4,2},{6,0},{8,14},{10,12},{12,10},{14,8},{16,22},{18,... | collective-permute-start | bytes 98312 | tf_op jit(solution)/shard_map/ppermute | solution.py:52
  4.2 4.0 %collective-permute-start.1 = (f32[2,32,128]{2,1,0:T(8,128)S(1)}, f32[2,32,128]{2,1,0:T(8,128)S(1)}, u32[]{:S(2)}, u32[]{:S(2)}) collective-permute-start(f32[2,32,128]{2,1,0:T(8,128)S(1)} %get-tuple-element.155), channel_id=1, source_target_pairs={{0,4},{2,6},{4,0},{6,2},{8,12},{10,14},{12,8},{14,10},{16,20},{18,... | collective-permute-start | bytes 98312 | tf_op jit(solution)/shard_map/ppermute | solution.py:52
  4.8 3.3 %collective-permute-start = (f32[2,32,128]{2,1,0:T(8,128)S(1)}, f32[2,32,128]{2,1,0:T(8,128)S(1)}, u32[]{:S(2)}, u32[]{:S(2)}) collective-permute-start(f32[2,32,128]{2,1,0:T(8,128)S(1)} %get-tuple-element.156), channel_id=1, source_target_pairs={{0,2},{2,0},{4,6},{6,4},{8,10},{10,8},{12,14},{14,12},{16,18},{18,... | collective-permute-start | bytes 98312 | tf_op jit(solution)/shard_map/ppermute | solution.py:52
  8.2 6.2 %collective-permute-start.4 = (f32[4,32,128]{2,1,0:T(8,128)S(1)}, f32[4,32,128]{2,1,0:T(8,128)S(1)}, u32[]{:S(2)}, u32[]{:S(2)}) collective-permute-start(f32[4,32,128]{2,1,0:T(8,128)S(1)} %get-tuple-element.140), channel_id=1, source_target_pairs={{0,2},{2,0},{4,6},{6,4},{8,16},{10,18},{12,20},{14,22},{16,8},{18,... | collective-permute-start | bytes 196616 | tf_op jit(solution)/shard_map/ppermute | solution.py:58
  8.3 6.1 %collective-permute-start.3 = (f32[4,32,128]{2,1,0:T(8,128)S(1)}, f32[4,32,128]{2,1,0:T(8,128)S(1)}, u32[]{:S(2)}, u32[]{:S(2)}) collective-permute-start(f32[4,32,128]{2,1,0:T(8,128)S(1)} %get-tuple-element.141), channel_id=1, source_target_pairs={{0,8},{2,10},{4,12},{6,14},{8,0},{10,2},{12,4},{14,6},{16,24},{18,... | collective-permute-start | bytes 196616 | tf_op jit(solution)/shard_map/ppermute | solution.py:52
  14.9 3.4 %collective-permute-start.7 = (f32[2,32,128]{2,1,0:T(8,128)S(1)}, f32[2,32,128]{2,1,0:T(8,128)S(1)}, u32[]{:S(2)}, u32[]{:S(2)}) collective-permute-start(f32[2,32,128]{2,1,0:T(8,128)S(1)} %get-tuple-element.151), channel_id=1, source_target_pairs={{0,6},{2,4},{4,2},{6,0},{8,14},{10,12},{12,10},{14,8},{16,22},{18,... | collective-permute-start | bytes 98312 | tf_op jit(solution)/shard_map/ppermute | solution.py:52
  15.1 4.3 %collective-permute-start.6 = (f32[2,32,128]{2,1,0:T(8,128)S(1)}, f32[2,32,128]{2,1,0:T(8,128)S(1)}, u32[]{:S(2)}, u32[]{:S(2)}) collective-permute-start(f32[2,32,128]{2,1,0:T(8,128)S(1)} %get-tuple-element.152), channel_id=1, source_target_pairs={{0,4},{2,6},{4,0},{6,2},{8,12},{10,14},{12,8},{14,10},{16,20},{18,... | collective-permute-start | bytes 98312 | tf_op jit(solution)/shard_map/ppermute | solution.py:52
  16.1 3.3 %collective-permute-start.5 = (f32[2,32,128]{2,1,0:T(8,128)S(1)}, f32[2,32,128]{2,1,0:T(8,128)S(1)}, u32[]{:S(2)}, u32[]{:S(2)}) collective-permute-start(f32[2,32,128]{2,1,0:T(8,128)S(1)} %get-tuple-element.153), channel_id=1, source_target_pairs={{0,2},{2,0},{4,6},{6,4},{8,10},{10,8},{12,14},{14,12},{16,18},{18,... | collective-permute-start | bytes 98312 | tf_op jit(solution)/shard_map/ppermute | solution.py:52
  19.5 2.0 %collective-permute-start.9 = (f32[4,32,128]{2,1,0:T(8,128)S(1)}, f32[4,32,128]{2,1,0:T(8,128)S(1)}, u32[]{:S(2)}, u32[]{:S(2)}) collective-permute-start(f32[4,32,128]{2,1,0:T(8,128)S(1)} %get-tuple-element.138), channel_id=1, source_target_pairs={{0,2},{2,0},{4,6},{6,4},{8,16},{10,18},{12,20},{14,22},{16,8},{18,... | collective-permute-start | bytes 196616 | tf_op jit(solution)/shard_map/ppermute | solution.py:58
  19.6 4.4 %collective-permute-start.8 = (f32[4,32,128]{2,1,0:T(8,128)S(1)}, f32[4,32,128]{2,1,0:T(8,128)S(1)}, u32[]{:S(2)}, u32[]{:S(2)}) collective-permute-start(f32[4,32,128]{2,1,0:T(8,128)S(1)} %get-tuple-element.139), channel_id=1, source_target_pairs={{0,8},{2,10},{4,12},{6,14},{8,0},{10,2},{12,4},{14,6},{16,24},{18,... | collective-permute-start | bytes 196616 | tf_op jit(solution)/shard_map/ppermute | solution.py:52
  24.6 3.5 %collective-permute-start.12 = (f32[2,32,128]{2,1,0:T(8,128)S(1)}, f32[2,32,128]{2,1,0:T(8,128)S(1)}, u32[]{:S(2)}, u32[]{:S(2)}) collective-permute-start(f32[2,32,128]{2,1,0:T(8,128)S(1)} %get-tuple-element.148), channel_id=1, source_target_pairs={{0,6},{2,4},{4,2},{6,0},{8,14},{10,12},{12,10},{14,8},{16,22},{18,... | collective-permute-start | bytes 98312 | tf_op jit(solution)/shard_map/ppermute | solution.py:52
  24.7 4.2 %collective-permute-start.11 = (f32[2,32,128]{2,1,0:T(8,128)S(1)}, f32[2,32,128]{2,1,0:T(8,128)S(1)}, u32[]{:S(2)}, u32[]{:S(2)}) collective-permute-start(f32[2,32,128]{2,1,0:T(8,128)S(1)} %get-tuple-element.149), channel_id=1, source_target_pairs={{0,4},{2,6},{4,0},{6,2},{8,12},{10,14},{12,8},{14,10},{16,20},{18,... | collective-permute-start | bytes 98312 | tf_op jit(solution)/shard_map/ppermute | solution.py:52
  25.8 3.1 %collective-permute-start.10 = (f32[2,32,128]{2,1,0:T(8,128)S(1)}, f32[2,32,128]{2,1,0:T(8,128)S(1)}, u32[]{:S(2)}, u32[]{:S(2)}) collective-permute-start(f32[2,32,128]{2,1,0:T(8,128)S(1)} %get-tuple-element.150), channel_id=1, source_target_pairs={{0,2},{2,0},{4,6},{6,4},{8,10},{10,8},{12,14},{14,12},{16,18},{18,... | collective-permute-start | bytes 98312 | tf_op jit(solution)/shard_map/ppermute | solution.py:52
  28.9 3.1 %collective-permute-start.14 = (f32[4,32,128]{2,1,0:T(8,128)S(1)}, f32[4,32,128]{2,1,0:T(8,128)S(1)}, u32[]{:S(2)}, u32[]{:S(2)}) collective-permute-start(f32[4,32,128]{2,1,0:T(8,128)S(1)} %get-tuple-element.136), channel_id=1, source_target_pairs={{0,2},{2,0},{4,6},{6,4},{8,16},{10,18},{12,20},{14,22},{16,8},{18,... | collective-permute-start | bytes 196616 | tf_op jit(solution)/shard_map/ppermute | solution.py:58
  29.0 5.3 %collective-permute-start.13 = (f32[4,32,128]{2,1,0:T(8,128)S(1)}, f32[4,32,128]{2,1,0:T(8,128)S(1)}, u32[]{:S(2)}, u32[]{:S(2)}) collective-permute-start(f32[4,32,128]{2,1,0:T(8,128)S(1)} %get-tuple-element.137), channel_id=1, source_target_pairs={{0,8},{2,10},{4,12},{6,14},{8,0},{10,2},{12,4},{14,6},{16,24},{18,... | collective-permute-start | bytes 196616 | tf_op jit(solution)/shard_map/ppermute | solution.py:52
  35.2 3.4 %collective-permute-start.17 = (f32[2,32,128]{2,1,0:T(8,128)S(1)}, f32[2,32,128]{2,1,0:T(8,128)S(1)}, u32[]{:S(2)}, u32[]{:S(2)}) collective-permute-start(f32[2,32,128]{2,1,0:T(8,128)S(1)} %get-tuple-element.145), channel_id=1, source_target_pairs={{0,6},{2,4},{4,2},{6,0},{8,14},{10,12},{12,10},{14,8},{16,22},{18,... | collective-permute-start | bytes 98312 | tf_op jit(solution)/shard_map/ppermute | solution.py:52
  35.3 4.1 %collective-permute-start.16 = (f32[2,32,128]{2,1,0:T(8,128)S(1)}, f32[2,32,128]{2,1,0:T(8,128)S(1)}, u32[]{:S(2)}, u32[]{:S(2)}) collective-permute-start(f32[2,32,128]{2,1,0:T(8,128)S(1)} %get-tuple-element.146), channel_id=1, source_target_pairs={{0,4},{2,6},{4,0},{6,2},{8,12},{10,14},{12,8},{14,10},{16,20},{18,... | collective-permute-start | bytes 98312 | tf_op jit(solution)/shard_map/ppermute | solution.py:52
  36.1 3.3 %collective-permute-start.15 = (f32[2,32,128]{2,1,0:T(8,128)S(1)}, f32[2,32,128]{2,1,0:T(8,128)S(1)}, u32[]{:S(2)}, u32[]{:S(2)}) collective-permute-start(f32[2,32,128]{2,1,0:T(8,128)S(1)} %get-tuple-element.147), channel_id=1, source_target_pairs={{0,2},{2,0},{4,6},{6,4},{8,10},{10,8},{12,14},{14,12},{16,18},{18,... | collective-permute-start | bytes 98312 | tf_op jit(solution)/shard_map/ppermute | solution.py:52
  39.5 2.7 %collective-permute-start.19 = (f32[4,32,128]{2,1,0:T(8,128)S(1)}, f32[4,32,128]{2,1,0:T(8,128)S(1)}, u32[]{:S(2)}, u32[]{:S(2)}) collective-permute-start(f32[4,32,128]{2,1,0:T(8,128)S(1)} %get-tuple-element.134), channel_id=1, source_target_pairs={{0,2},{2,0},{4,6},{6,4},{8,16},{10,18},{12,20},{14,22},{16,8},{18,... | collective-permute-start | bytes 196616 | tf_op jit(solution)/shard_map/ppermute | solution.py:58
  39.5 4.9 %collective-permute-start.18 = (f32[4,32,128]{2,1,0:T(8,128)S(1)}, f32[4,32,128]{2,1,0:T(8,128)S(1)}, u32[]{:S(2)}, u32[]{:S(2)}) collective-permute-start(f32[4,32,128]{2,1,0:T(8,128)S(1)} %get-tuple-element.135), channel_id=1, source_target_pairs={{0,8},{2,10},{4,12},{6,14},{8,0},{10,2},{12,4},{14,6},{16,24},{18,... | collective-permute-start | bytes 196616 | tf_op jit(solution)/shard_map/ppermute | solution.py:52
  44.9 3.6 %collective-permute-start.22 = (f32[2,32,128]{2,1,0:T(8,128)S(1)}, f32[2,32,128]{2,1,0:T(8,128)S(1)}, u32[]{:S(2)}, u32[]{:S(2)}) collective-permute-start(f32[2,32,128]{2,1,0:T(8,128)S(1)} %get-tuple-element.142), channel_id=1, source_target_pairs={{0,6},{2,4},{4,2},{6,0},{8,14},{10,12},{12,10},{14,8},{16,22},{18,... | collective-permute-start | bytes 98312 | tf_op jit(solution)/shard_map/ppermute | solution.py:52
  45.0 4.0 %collective-permute-start.21 = (f32[2,32,128]{2,1,0:T(8,128)S(1)}, f32[2,32,128]{2,1,0:T(8,128)S(1)}, u32[]{:S(2)}, u32[]{:S(2)}) collective-permute-start(f32[2,32,128]{2,1,0:T(8,128)S(1)} %get-tuple-element.143), channel_id=1, source_target_pairs={{0,4},{2,6},{4,0},{6,2},{8,12},{10,14},{12,8},{14,10},{16,20},{18,... | collective-permute-start | bytes 98312 | tf_op jit(solution)/shard_map/ppermute | solution.py:52
  46.3 2.7 %collective-permute-start.20 = (f32[2,32,128]{2,1,0:T(8,128)S(1)}, f32[2,32,128]{2,1,0:T(8,128)S(1)}, u32[]{:S(2)}, u32[]{:S(2)}) collective-permute-start(f32[2,32,128]{2,1,0:T(8,128)S(1)} %get-tuple-element.144), channel_id=1, source_target_pairs={{0,2},{2,0},{4,6},{6,4},{8,10},{10,8},{12,14},{14,12},{16,18},{18,... | collective-permute-start | bytes 98312 | tf_op jit(solution)/shard_map/ppermute | solution.py:52
  49.0 3.5 %collective-permute-start.24 = (f32[4,32,128]{2,1,0:T(8,128)S(1)}, f32[4,32,128]{2,1,0:T(8,128)S(1)}, u32[]{:S(2)}, u32[]{:S(2)}) collective-permute-start(f32[4,32,128]{2,1,0:T(8,128)S(1)} %get-tuple-element.132), channel_id=1, source_target_pairs={{0,2},{2,0},{4,6},{6,4},{8,16},{10,18},{12,20},{14,22},{16,8},{18,... | collective-permute-start | bytes 196616 | tf_op jit(solution)/shard_map/ppermute | solution.py:58
  49.2 5.5 %collective-permute-start.23 = (f32[4,32,128]{2,1,0:T(8,128)S(1)}, f32[4,32,128]{2,1,0:T(8,128)S(1)}, u32[]{:S(2)}, u32[]{:S(2)}) collective-permute-start(f32[4,32,128]{2,1,0:T(8,128)S(1)} %get-tuple-element.133), channel_id=1, source_target_pairs={{0,8},{2,10},{4,12},{6,14},{8,0},{10,2},{12,4},{14,6},{16,24},{18,... | collective-permute-start | bytes 196616 | tf_op jit(solution)/shard_map/ppermute | solution.py:52
  55.3 3.1 %collective-permute-start.27 = (f32[2,8,128]{2,1,0:T(8,128)S(1)}, f32[2,8,128]{2,1,0:T(8,128)S(1)}, u32[]{:S(2)}, u32[]{:S(2)}) collective-permute-start(f32[2,8,128]{2,1,0:T(8,128)S(1)} %get-tuple-element.199), channel_id=1, source_target_pairs={{0,6},{2,4},{4,2},{6,0},{8,14},{10,12},{12,10},{14,8},{16,22},{18,... | collective-permute-start | bytes 24584 | tf_op jit(solution)/shard_map/ppermute | solution.py:52
  55.4 3.7 %collective-permute-start.26 = (f32[2,8,128]{2,1,0:T(8,128)S(1)}, f32[2,8,128]{2,1,0:T(8,128)S(1)}, u32[]{:S(2)}, u32[]{:S(2)}) collective-permute-start(f32[2,8,128]{2,1,0:T(8,128)S(1)} %get-tuple-element.200), channel_id=1, source_target_pairs={{0,4},{2,6},{4,0},{6,2},{8,12},{10,14},{12,8},{14,10},{16,20},{18,... | collective-permute-start | bytes 24584 | tf_op jit(solution)/shard_map/ppermute | solution.py:52
  56.0 3.1 %collective-permute-start.25 = (f32[2,8,128]{2,1,0:T(8,128)S(1)}, f32[2,8,128]{2,1,0:T(8,128)S(1)}, u32[]{:S(2)}, u32[]{:S(2)}) collective-permute-start(f32[2,8,128]{2,1,0:T(8,128)S(1)} %get-tuple-element.201), channel_id=1, source_target_pairs={{0,2},{2,0},{4,6},{6,4},{8,10},{10,8},{12,14},{14,12},{16,18},{18,... | collective-permute-start | bytes 24584 | tf_op jit(solution)/shard_map/ppermute | solution.py:52
  59.1 6.2 %collective-permute-start.29 = (f32[4,8,128]{2,1,0:T(8,128)S(1)}, f32[4,8,128]{2,1,0:T(8,128)S(1)}, u32[]{:S(2)}, u32[]{:S(2)}) collective-permute-start(f32[4,8,128]{2,1,0:T(8,128)S(1)} %get-tuple-element.157), channel_id=1, source_target_pairs={{0,2},{2,0},{4,6},{6,4},{8,16},{10,18},{12,20},{14,22},{16,8},{18,... | collective-permute-start | bytes 49160 | tf_op jit(solution)/shard_map/ppermute | solution.py:58
  59.2 6.2 %collective-permute-start.28 = (f32[4,8,128]{2,1,0:T(8,128)S(1)}, f32[4,8,128]{2,1,0:T(8,128)S(1)}, u32[]{:S(2)}, u32[]{:S(2)}) collective-permute-start(f32[4,8,128]{2,1,0:T(8,128)S(1)} %get-tuple-element.158), channel_id=1, source_target_pairs={{0,8},{2,10},{4,12},{6,14},{8,0},{10,2},{12,4},{14,6},{16,24},{18,... | collective-permute-start | bytes 49160 | tf_op jit(solution)/shard_map/ppermute | solution.py:52
  67.5 1.4 %collective-permute-start.30 = (f32[272,128]{1,0:T(8,128)S(1)}, f32[272,128]{1,0:T(8,128)S(1)}, u32[]{:S(2)}, u32[]{:S(2)}) collective-permute-start(f32[272,128]{1,0:T(8,128)S(1)} %slice_bitcast_fusion), channel_id=1, source_target_pairs={{0,2},{2,0},{4,6},{6,4},{8,10},{10,8},{12,14},{14,12},{16,18},{18,... | collective-permute-start | bytes 417800 | tf_op jit(solution)/shard_map/ppermute | solution.py:726
  92.3 1.4 %collective-permute-start.31 = (f32[272,128]{1,0:T(8,128)S(1)}, f32[272,128]{1,0:T(8,128)S(1)}, u32[]{:S(2)}, u32[]{:S(2)}) collective-permute-start(f32[272,128]{1,0:T(8,128)S(1)} %bitcast.54), channel_id=1, source_target_pairs={{0,2},{2,0},{4,6},{6,4},{8,10},{10,8},{12,14},{14,12},{16,18},{18,... | collective-permute-start | bytes 417800 | tf_op jit(solution)/shard_map/ppermute | solution.py:732
  (2 other events, 19.3 us)
